TPU v7x, 128 devices: a whole 4x4x4 slice. The times are simulated.
128 devices in a mesh: row: 8 (over x_lo, z), col: 16 (over x_hi, y, core).
Axes of the slice: x: 4 (x_hi: 2, x_lo: 2; x = x_hi * 2 + x_lo), y: 4, z: 4, core: 2. Of those that a mesh axis runs over, the one named last changes fastest.
Arguments:
- ancestor: float32 [24576, 24576], P('row', 'col'), may hold values from -6 to 6
- lhat_one: float32 [24576, 512], P('col', 'row'), may hold values from -0.15625 to 0.15625
- lhat_two: float32 [24576, 512], P('col', 'row'), may hold values from -0.15625 to 0.15625
- link_two: float32 [512, 512], replicated, may hold values from -0.25 to 0.25
- diag_one: float32 [512, 512], replicated, may hold values from -6 to 6
- diag_two: float32 [512, 512], replicated, may hold values from -6 to 6
- mask_one: int32 [192], replicated, may hold values from 0 to 1, as said below
- mask_two: int32 [192], replicated, may hold values from 0 to 1, as said below
Outputs:
- x_one: float32 [24576, 512], P('row', 'col')
- d_one: float32 [512, 512], replicated
- x_two: float32 [24576, 512], P('row', 'col')
- link_inverse: float32 [512, 512], replicated
- d_two: float32 [512, 512], replicated
Inputs may be any that keep to these rules, and one draw needn't show every extreme that they name: `mask_one`: 1 where a block of 128 factor rows is nonzero, else 0; the last block is always nonzero. `mask_two`: 1 where a block of 128 factor rows is nonzero, else 0; the last block is always nonzero.
All inputs are finite; a program needn't handle non-finite values.
Results may differ from a plain program's by a relative error of at most 0.00011.
Values sent between devices are 32-bit elements; how exact they have to be, the bound alone decides.
No kernel may reach another device: no remote copies, remote signals or barrier semaphores. Data moves between devices by JAX's collectives and lax.ppermute only.
A program may use at most 128 MiB of HBM per device.

v0:
```python
import jax
import jax.numpy as jnp
from jax import lax
from jax.sharding import PartitionSpec as P

BLOCK = 128


def spread(value, axis, source):
    kept = jnp.where(lax.axis_index(axis) == source, value, 0).astype(value.dtype)
    return lax.psum(kept, axis)


def product(left, right):
    return jnp.dot(left, right, precision=lax.Precision.HIGHEST, preferred_element_type=jnp.float32)


def per_device(ancestor, lhat_one, lhat_two, link_two, diag_one, diag_two, mask_one, mask_two):
    column_index = lax.axis_index("col")
    row_index = lax.axis_index("row")
    row_count = lax.axis_size("row")
    column_count = lax.axis_size("col")
    column_rows = lhat_one.shape[0]
    sub_rows = column_rows // row_count
    full_width = link_two.shape[0]
    column_width = full_width // column_count
    blocks = column_rows // BLOCK

    def factor(factor_part, block_mask):
        complete = lax.all_gather(factor_part, "row", axis=1, tiled=True)
        mask_part = lax.dynamic_slice_in_dim(block_mask, column_index * blocks, blocks)
        expanded = jnp.repeat(mask_part.astype(jnp.float32), BLOCK, total_repeat_length=column_rows)
        return complete * expanded[:, None]

    def row_sum(partial_value):
        own_part = -lax.psum_scatter(partial_value, "col", scatter_dimension=1, tiled=True)
        complete = lax.all_gather(own_part, "col", axis=1, tiled=True)
        return (own_part, complete)

    def mirror(complete):
        parity = column_index % 2
        section = lax.dynamic_slice_in_dim(complete, parity * column_rows, column_rows, 0)
        received = spread(section, "row", column_index // 2)
        return lax.dynamic_slice_in_dim(received, row_index * sub_rows, sub_rows, 0)

    def rows_of(matrix):
        return lax.dynamic_slice_in_dim(matrix, row_index * sub_rows, sub_rows, 0)

    factor_one = factor(lhat_one, mask_one)
    x_one, complete_one = row_sum(product(ancestor, factor_one))
    factor_two = factor(lhat_two, mask_two)
    link_rows = lax.dynamic_slice_in_dim(link_two, column_index * column_width, column_width, 0)
    mirrored_one = mirror(complete_one)
    ancestor_two = product(ancestor, factor_two)
    ancestor_two = ancestor_two + product(x_one, link_rows)
    factor_sub_one = rows_of(factor_one)
    factor_sub_two = rows_of(factor_two)
    column_diag, column_link = lax.psum(
        (product(factor_sub_one.T, mirrored_one), product(mirrored_one.T, factor_sub_two)), "row"
    )
    diag_part, link_part = lax.psum((column_diag, column_link), "col")
    d_one = diag_one - diag_part
    link_inverse = -(link_part + product(d_one, link_two))
    x_two, complete_two = row_sum(ancestor_two)
    mirrored_two = mirror(complete_two)
    column_last = lax.psum(product(factor_sub_two.T, mirrored_two), "row")
    last_part = lax.psum(column_last, "col")
    d_two = diag_two - last_part - product(link_two.T, link_inverse)
    return (x_one, d_one, x_two, link_inverse, d_two)


def solution(mesh):
    in_specs = (P("row", "col"), P("col", "row"), P("col", "row"), P(), P(), P(), P(), P())
    out_specs = (P("row", "col"), P(), P("row", "col"), P(), P())
    return jax.shard_map(
        per_device, mesh=mesh, in_specs=in_specs, out_specs=out_specs, check_vma=False
    )
```

profile of v0, /device:TPU:1, one launch (start us, length us, event | category | flops | bytes accessed | tf_op | source)
XLA Modules:
  0.0 834.8 jit_solution(3131778317618149508)
XLA Ops:
  10.2 7.6 select_select_fusion.1
  17.8 36.9 %all-gather.5.cloned.1.call-done = f32[1536,512]{0,1:T(8,128)} async-done(((f32[1536,64]{0,1:T(8,128)}), f32[1536,512]{0,1:T(8,128)}) %all-gather.5.cloned.1.call-update) | async-done | bytes 3145744 | tf_op jit(solution)/shard_map/all_gather | solution.py:30
  54.7 2.2 broadcast_multiply_fusion.1
  58.5 35.0 %convolution_bitcast_fusion = f32[3072,512]{0,1:T(8,128)} fusion(f32[1536,512]{0,1:T(8,128)S(1)} %broadcast_multiply_fusion.1, f32[3072,1536]{1,0:T(8,128)} %param.14), kind=kOutput, calls=%fused_computation.1 | convolution fusion | flops 28991029248 | bytes 28311552 | tf_op jit(solution)/shard_map/dot_general | solution.py:15
  94.5 7.5 select_select_fusion
  102.0 2.2 broadcast_multiply_fusion
  104.2 1.6 copy-done.1
  105.9 35.0 %fusion.32 = f32[512,3072]{1,0:T(8,128)} fusion(f32[1536,512]{0,1:T(8,128)S(1)} %broadcast_multiply_fusion, f32[3072,1536]{1,0:T(8,128)} %param.14), kind=kOutput, calls=%fused_computation.45 | convolution fusion | flops 28991029248 | bytes 28311552 | tf_op jit(solution)/shard_map/dot_general | solution.py:15
  140.8 53.9 %reduce-scatter.3.cloned.1.call-done = f32[3072,32]{0,1:T(8,128)} async-done(((f32[3072,512]{0,1:T(8,128)}), f32[3072,32]{0,1:T(8,128)}) %reduce-scatter.3.cloned.1.call-update) | async-done | bytes 393232 | tf_op jit(solution)/shard_map/reduce_scatter | solution.py:36
  195.7 9.0 %bitcast_add_fusion = f32[3072,512]{0,1:T(8,128)} fusion(f32[512,3072]{1,0:T(8,128)} %fusion.32, f32[3072,32]{0,1:T(8,128)S(1)} %neg.9, f32[512,512]{1,0:T(8,128)S(1)} %copy-done, s32[]{:T(128)S(6)} %select_n.60), kind=kOutput, calls=%fused_computation | convolution fusion | flops 605552640 | bytes 13041668 | tf_op jit(solution)/shard_map/dot_general | solution.py:15
  205.5 88.1 %reduce-scatter.5.cloned.1.call-done = f32[3072,32]{0,1:T(8,128)} async-done(((f32[3072,512]{0,1:T(8,128)}), f32[3072,32]{0,1:T(8,128)}) %reduce-scatter.5.cloned.1.call-update) | async-done | bytes 393232 | tf_op jit(solution)/shard_map/reduce_scatter | solution.py:36
  293.5 1.8 neg.10
  295.4 65.3 %all-gather.7.cloned.1.call-done = f32[3072,512]{0,1:T(8,128)} async-done(((f32[3072,32]{0,1:T(8,128)}), f32[3072,512]{0,1:T(8,128)}) %all-gather.7.cloned.1.call-update) | async-done | bytes 6291472 | tf_op jit(solution)/shard_map/all_gather | solution.py:37
  360.7 3.8 dynamic-slice_select_fusion.1
  364.5 60.5 %all-gather.11.cloned.1.call-done = f32[3072,512]{0,1:T(8,128)} async-done(((f32[3072,32]{0,1:T(8,128)}), f32[3072,512]{0,1:T(8,128)}) %all-gather.11.cloned.1.call-update) | async-done | bytes 6291472 | tf_op jit(solution)/shard_map/all_gather | solution.py:37
  425.1 3.8 dynamic-slice_select_fusion
  429.2 142.2 %all-reduce.11.cloned.1.call-done = (f32[1536,512]{0,1:T(8,128)}, f32[1536,512]{0,1:T(8,128)}) async-done(((f32[1536,512]{0,1:T(8,128)}, f32[1536,512]{0,1:T(8,128)}), (f32[1536,512]{0,1:T(8,128)}, f32[1536,512]{0,1:T(8,128)})) %all-reduce.11.cloned.1.call-update) | async-done | bytes 6291472 | tf_op jit(solution)/shard_map/psum | solution.py:11
  571.4 3.5 fusion.4
  574.9 3.5 fusion.7
  578.4 3.5 fusion.2
  582.0 87.9 %all-reduce.9.cloned.1.call-done = (f32[512,512]{1,0:T(8,128)}, f32[512,512]{1,0:T(8,128)}, f32[512,512]{1,0:T(8,128)}) async-done(((f32[512,512]{1,0:T(8,128)}, f32[512,512]{1,0:T(8,128)}, f32[512,512]{1,0:T(8,128)}), (f32[512,512]{1,0:T(8,128)}, f32[512,512]{1,0:T(8,128)}, f32[512,512]{1,0:T(8,128)})) %all-reduce.9.cloned.1.call-update) | async-done | bytes 3145744 | tf_op jit(solution)/shard_map/psum | solution.py:58
  670.0 151.8 %all-reduce.7.cloned.1.call-done = (f32[512,512]{1,0:T(8,128)}, f32[512,512]{1,0:T(8,128)}, f32[512,512]{1,0:T(8,128)}) async-done(((f32[512,512]{1,0:T(8,128)}, f32[512,512]{1,0:T(8,128)}, f32[512,512]{1,0:T(8,128)}), (f32[512,512]{1,0:T(8,128)}, f32[512,512]{1,0:T(8,128)}, f32[512,512]{1,0:T(8,128)})) %all-reduce.7.cloned.1.call-update) | async-done | bytes 3145744 | tf_op jit(solution)/shard_map/psum | solution.py:61
  823.4 1.9 fusion.1
  825.3 2.9 fusion
  (43 shorter events, 9.3 us)
Async XLA Ops:
  7.2 188.6 %copy-start = (f32[512,512]{1,0:T(8,128)S(1)}, f32[512,512]{1,0:T(8,128)}, u32[]{:S(2)}) copy-start(f32[512,512]{1,0:T(8,128)} %param.17) | copy-start | bytes 3145732
  7.2 47.5 %all-gather.5.cloned.1.call-start = ((), (), s32[]{:S(2)}) async-start(), calls=%async_computation.2 | async-start | bytes 3538944 | tf_op jit(solution)/shard_map/all_gather | solution.py:30
  7.9 94.1 %all-gather.9.cloned.1.call-start = ((), (), s32[]{:S(2)}) async-start(), calls=%async_computation.5 | async-start | bytes 3538944 | tf_op jit(solution)/shard_map/all_gather | solution.py:30
  8.7 186.0 %reduce-scatter.3.cloned.1.call-start = ((), (), s32[]{:S(2)}) async-start(), calls=%async_computation.3 | async-start | bytes 6684672 | tf_op jit(solution)/shard_map/reduce_scatter | solution.py:36
  56.9 1.6 copy-start.2
  93.5 200.0 %reduce-scatter.5.cloned.1.call-start = ((), (), s32[]{:S(2)}) async-start(), calls=%async_computation.6 | async-start | bytes 6684672 | tf_op jit(solution)/shard_map/reduce_scatter | solution.py:36
  104.2 1.7 copy-start.1
  195.7 9.1 %copy-start.5 = (f32[3072,32]{0,1:T(8,128)}, f32[3072,32]{0,1:T(8,128)S(1)}, u32[]{:S(2)}) copy-start(f32[3072,32]{0,1:T(8,128)S(1)} %neg.9) | copy-start | bytes 1179652
  204.8 155.9 %all-gather.7.cloned.1.call-start = ((), (), s32[]{:S(2)}) async-start(), calls=%async_computation.4 | async-start | bytes 6684672 | tf_op jit(solution)/shard_map/all_gather | solution.py:37
  205.4 219.7 %all-gather.11.cloned.1.call-start = ((), (), s32[]{:S(2)}) async-start(), calls=%async_computation.7 | async-start | bytes 6684672 | tf_op jit(solution)/shard_map/all_gather | solution.py:37
  295.3 276.1 %all-reduce.11.cloned.1.call-start = ((), (), s32[]{:S(2)}) async-start(), calls=%async_computation.10 | async-start | bytes 12582912 | tf_op jit(solution)/shard_map/psum | solution.py:11
  428.9 241.0 %all-reduce.9.cloned.1.call-start = ((), (), s32[]{:S(2)}) async-start(), calls=%async_computation.9 | async-start | bytes 6291456 | tf_op jit(solution)/shard_map/psum | solution.py:58
  581.9 239.8 %copy-start.6 = (f32[512,512]{1,0:T(8,128)S(1)}, f32[512,512]{1,0:T(8,128)}, u32[]{:S(2)}) copy-start(f32[512,512]{1,0:T(8,128)} %param.18) | copy-start | bytes 3145732
  582.0 239.8 %all-reduce.7.cloned.1.call-start = ((), (), s32[]{:S(2)}) async-start(), calls=%async_computation.8 | async-start | bytes 6291456 | tf_op jit(solution)/shard_map/psum | solution.py:61
  821.8 1.6 copy-start.9
  821.8 3.6 copy-start.7
  821.8 3.6 copy-start.8
  823.4 4.8 copy-start.3
  825.3 2.9 copy-start.4
Sparse Core Ops, SparseCore 0:
  9.6 44.9 all-gather.4
  56.3 43.7 all-gather.8
  104.3 90.3 reduce-scatter.2
  204.9 88.5 reduce-scatter.4
  296.4 64.2 all-gather.6
  363.6 61.3 all-gather.10
  429.0 142.3 all-reduce.10
  582.1 87.7 all-reduce.8
  672.7 149.0 all-reduce.6
where the time goes:
time: 835 us
  waiting for transfers between devices  689 us (83%)
  matrix products  94.3 us (11%)
  other arithmetic  32.3 us (4%)
  between operations  14 us (2%)
    psum x1, waiting for transfers between devices, per_device(): diag_part, link_part = lax.psum((column_diag, column_link), 'col')  152 us
    psum x1, waiting for transfers between devices, spread(): return lax.psum(kept, axis)  142 us
    reduce_scatter x2, waiting for transfers between devices, row_sum(): lax.psum_scatter(partial_value, 'col', scatter_dimension=1, tiled=True)  142 us
    all_gather x2, waiting for transfers between devices, row_sum(): complete = lax.all_gather(own_part, 'col', axis=1, tiled=True)  126 us
    dot_general x8, matrix products, product(): jnp.dot(left, right, precision=lax.Precision.HIGHEST, preferred_element_t...  94.3 us
    psum x1, waiting for transfers between devices, per_device(): lax.psum((product(factor_sub_one.T, mirrored_one), product(mirrored_one.T...  87.9 us
    all_gather x2, waiting for transfers between devices, factor(): complete = lax.all_gather(factor_part, 'row', axis=1, tiled=True)  36.9 us
  transfers between devices with their start and end apart: 9, of which 8 were waited for; matrix products, arithmetic and copies ran while one was open for 12% of the time, Pallas kernels for 0%

commit v1 on v0

v1 whole, which is shorter than its diff:
```python
import jax
import jax.numpy as jnp
from jax import lax
from jax.sharding import Mesh, PartitionSpec as P

BLOCK = 128
ROW = ("xl", "z")
COL = ("xh", "y", "core")
ALL = ROW + COL
SIZES = (2, 4, 2, 4, 2)
SWAP = ((0, 1), (1, 0))


def product(left, right, contract=((1,), (0,))):
    return lax.dot_general(left, right, (contract, ((), ())), precision=lax.Precision.HIGH,
                           preferred_element_type=jnp.float32)


def linear(xl, z, xh, y, core):
    return (((xl * 4 + z) * 2 + xh) * 4 + y) * 2 + core


def factor_routes():
    routes = []
    for xl in range(2):
        for z in range(4):
            for xh in range(2):
                for y in range(4):
                    for core in range(2):
                        source = linear(y // 2, (y % 2) * 2 + core, xl, z, xh)
                        routes.append((source, linear(xl, z, xh, y, core)))
    return routes


def per_device(ancestor, lhat_one, lhat_two, link_two, diag_one, diag_two, mask_one, mask_two):
    row_index = lax.axis_index(ROW)
    column_index = lax.axis_index(COL)
    core = lax.axis_index("core")
    xh = lax.axis_index("xh")
    rows, depth = ancestor.shape
    width = link_two.shape[0]
    blocks = depth // BLOCK
    part = rows // 16

    def masked(shard, mask):
        own = lax.dynamic_slice_in_dim(mask, column_index * blocks, blocks).astype(jnp.float32)
        return (shard.reshape(blocks, BLOCK, -1) * own[:, None, None]).reshape(shard.shape)

    def row_sum(factor):
        partial = product(ancestor, factor).reshape(2, 4, 2, part, width)
        keep = lax.dynamic_index_in_dim(partial, core, 2, keepdims=False)
        send = lax.dynamic_index_in_dim(partial, 1 - core, 2, keepdims=False)
        chip = keep + lax.ppermute(send, "core", SWAP)
        chip = chip.transpose(1, 0, 2, 3).reshape(8 * part, width)
        line = lax.psum_scatter(chip, "y", scatter_dimension=0, tiled=True).reshape(2, part, width)
        own = lax.dynamic_index_in_dim(line, xh, 0, keepdims=False)
        other = lax.dynamic_index_in_dim(line, 1 - xh, 0, keepdims=False)
        return own + lax.ppermute(other, "xh", SWAP)

    factor_one = lax.all_gather(masked(lhat_one, mask_one), ROW, axis=1, tiled=True)
    factor_two = lax.all_gather(masked(lhat_two, mask_two), ROW, axis=1, tiled=True)
    local = jnp.concatenate(
        [lax.dynamic_slice_in_dim(f, row_index * part, part, 0) for f in (factor_one, factor_two)], axis=1)
    local = lax.ppermute(local, ALL, factor_routes())
    sum_one = row_sum(factor_one)
    sum_two = row_sum(factor_two)
    gram_one = product(local, sum_one, ((0,), (0,)))
    gram_two = product(local[:, width:], sum_two, ((0,), (0,)))
    grams = jnp.concatenate([gram_one, gram_two], axis=0)
    half = grams.shape[0] // 2
    keep = lax.dynamic_slice_in_dim(grams, core * half, half, 0)
    send = lax.dynamic_slice_in_dim(grams, (1 - core) * half, half, 0)
    piece = keep + lax.ppermute(send, "core", SWAP)
    piece = lax.psum_scatter(piece, "y", scatter_dimension=0, tiled=True)
    piece = lax.psum_scatter(piece, "z", scatter_dimension=0, tiled=True)
    piece = lax.psum(piece, ("xl", "xh"))
    piece = lax.all_gather(piece, "z", axis=0, tiled=True)
    piece = lax.all_gather(piece, "y", axis=0, tiled=True)
    other = lax.ppermute(piece, "core", SWAP)
    grams = jnp.where(core == 0, jnp.concatenate([piece, other], 0), jnp.concatenate([other, piece], 0))
    cross = grams[width:2 * width]
    d_one = diag_one + grams[:width]
    link_inverse = cross.T - product(d_one, link_two)
    d_two = diag_two + grams[2 * width:] - product(cross, link_two) - product(link_two, link_inverse, ((0,), (0,)))
    own_two = product(sum_one, link_two) - sum_two
    out = jnp.stack([-sum_one, own_two], axis=0)
    out = lax.all_to_all(out, COL, split_axis=2, concat_axis=1, tiled=True)
    return (out[0], d_one, out[1], link_inverse, d_two)


def solution(mesh):
    fine = Mesh(mesh.devices.reshape(SIZES), ALL)
    in_specs = (P(ROW, COL), P(COL, ROW), P(COL, ROW), P(), P(), P(), P(), P())
    out_specs = (P(ROW, COL), P(), P(ROW, COL), P(), P())
    return jax.shard_map(
        per_device, mesh=fine, in_specs=in_specs, out_specs=out_specs, check_vma=False
    )
```

time: 835 us -> 408 us (0.49)
  waiting for transfers between devices: 689 us -> 248 us
  matrix products: 94.3 us -> 53.1 us
  local copies, waits for them, and re-layouts: 4.74 us -> 34.9 us
  starting transfers between devices: 0.76 us -> 23.8 us
  blocking collectives: 0 us -> 12.7 us
  other arithmetic: 32.3 us -> 19.9 us
    psum x3 -> x1, waiting for transfers between devices: 382 us -> 43.5 us  [per_device(): piece = lax.psum(piece, ('xl', 'xh'))]
    all_gather x4 -> x3, waiting for transfers between devices: 163 us -> 73.8 us  [the longest x1 43.3 us: per_device(): lax.all_gather(masked(lhat_one, mask_one), ROW, axis=1, tiled=True)]
    reduce_scatter x2 -> x4, waiting for transfers between devices: 142 us -> 92.4 us  [the longest x2 44.6 us: row_sum(): lax.psum_scatter(chip, 'y', scatter_dimension=0, tiled=True)]
    dot_general x8, matrix products: 94.3 us -> 53.1 us  [product(): lax.dot_general(left, right, (contract, ((), ())), precision=lax.Precisio...]
    ppermute x0 -> x7, waiting for transfers between devices: none -> 21.6 us  [the longest x2 10.9 us: row_sum(): chip = keep + lax.ppermute(send, 'core', SWAP)]
    select_n x4 -> x1, other arithmetic: 22.7 us -> 3.66 us  [per_device(): jnp.where(core == 0, jnp.concatenate([piece, other], 0), jnp.concatenate(...]
    ppermute x0 -> x7, starting transfers between devices: none -> 18 us  [the longest x2 6.33 us: row_sum(): chip = keep + lax.ppermute(send, 'core', SWAP)]
    all_to_all x0 -> x1, waiting for transfers between devices: none -> 17.1 us  [per_device(): out = lax.all_to_all(out, COL, split_axis=2, concat_axis=1, tiled=True)]
  transfers between devices with their start and end apart: 9 -> 16, of which waited for: 8 -> 12; matrix products, arithmetic and copies ran while one was open for 12% -> 20% of each run, Pallas kernels for 0% -> 0%
where the time goes in v1:
time: 408 us; the launch traced here: 407 us
  waiting for transfers between devices  248 us (61%)
  matrix products  53.1 us (13%)
  local copies, waits for them, and re-layouts  34.9 us (9%)
  starting transfers between devices  23.8 us (6%)
  other arithmetic  19.9 us (5%)
  between operations  14.4 us (4%)
  blocking collectives  12.7 us (3%)
    dot_general x8, matrix products, product(): lax.dot_general(left, right, (contract, ((), ())), precision=lax.Precisio...  53.1 us
    reduce_scatter x2, waiting for transfers between devices, row_sum(): lax.psum_scatter(chip, 'y', scatter_dimension=0, tiled=True)  44.6 us
    psum x1, waiting for transfers between devices, per_device(): piece = lax.psum(piece, ('xl', 'xh'))  43.5 us
    all_gather x1, waiting for transfers between devices, per_device(): lax.all_gather(masked(lhat_one, mask_one), ROW, axis=1, tiled=True)  43.3 us
    all_gather x1, waiting for transfers between devices, per_device(): piece = lax.all_gather(piece, 'y', axis=0, tiled=True)  30 us
    reduce_scatter x1, waiting for transfers between devices, per_device(): piece = lax.psum_scatter(piece, 'y', scatter_dimension=0, tiled=True)  25.9 us
    reduce_scatter x1, waiting for transfers between devices, per_device(): piece = lax.psum_scatter(piece, 'z', scatter_dimension=0, tiled=True)  21.9 us
    all_to_all x1, waiting for transfers between devices, per_device(): out = lax.all_to_all(out, COL, split_axis=2, concat_axis=1, tiled=True)  17.1 us
  transfers between devices with their start and end apart: 16, of which 12 were waited for; matrix products, arithmetic and copies ran while one was open for 20% of the time, Pallas kernels for 0%

profile of v1, /device:TPU:1, one launch (start us, length us, event | category | flops | bytes accessed | tf_op | source)
XLA Modules:
  0.0 407.2 jit_solution(15928660699130049153)
XLA Ops:
  11.9 43.3 %all-gather.4.cloned.1.call-done = f32[1536,512]{0,1:T(8,128)} async-done(((f32[1536,64]{0,1:T(8,128)}), f32[1536,512]{0,1:T(8,128)}) %all-gather.4.cloned.1.call-update) | async-done | bytes 3145744 | tf_op jit(solution)/shard_map/all_gather | solution.py:60
  55.2 20.6 %convolution_bitcast_fusion.1 = f32[3072,512]{0,1:T(8,128)} fusion(f32[1536,512]{0,1:T(8,128)} %all-gather.4.cloned.1.call-done, f32[3072,1536]{1,0:T(8,128)} %param.8), kind=kOutput, calls=%fused_computation.1 | convolution fusion | flops 14495514624 | bytes 28311552 | tf_op jit(solution)/shard_map/dot_general | solution.py:15
  75.8 6.6 %copy.48 = f32[3072,512]{1,0:T(8,128)} copy(f32[3072,512]{0,1:T(8,128)} %convolution_bitcast_fusion.1) | data formatting | bytes 12582912 | tf_op jit(solution)/shard_map/dot_general | solution.py:15
  82.5 3.9 dynamic-slice_bitcast_fusion.1
  89.4 5.6 %collective-permute-done = f32[2,4,192,512]{3,2,1,0:T(8,128)} collective-permute-done((f32[2,4,192,512]{3,2,1,0:T(8,128)}, f32[2,4,192,512]{3,2,1,0:T(8,128)}, u32[]{:S(2)}, u32[]{:S(2)}) %collective-permute-start) | collective-permute-done | bytes 3145760 | tf_op jit(solution)/shard_map/ppermute | solution.py:53
  95.1 3.6 fusion.1
  101.3 20.6 %convolution_bitcast_fusion = f32[3072,512]{0,1:T(8,128)} fusion(f32[1536,512]{0,1:T(8,128)} %all-gather.6.cloned.1.call-done, f32[3072,1536]{1,0:T(8,128)} %param.8), kind=kOutput, calls=%fused_computation | convolution fusion | flops 14495514624 | bytes 28311552 | tf_op jit(solution)/shard_map/dot_general | solution.py:15
  121.9 6.6 %copy.50 = f32[3072,512]{1,0:T(8,128)} copy(f32[3072,512]{0,1:T(8,128)} %convolution_bitcast_fusion) | data formatting | bytes 12582912 | tf_op jit(solution)/shard_map/dot_general | solution.py:15
  134.2 5.3 %collective-permute-done.2 = f32[2,4,192,512]{3,2,1,0:T(8,128)S(1)} collective-permute-done((f32[2,4,192,512]{3,2,1,0:T(8,128)S(1)}, f32[2,4,192,512]{3,2,1,0:T(8,128)S(1)}, u32[]{:S(2)}, u32[]{:S(2)}) %collective-permute-start.2) | collective-permute-done | bytes 3145760 | tf_op jit(solution)/shard_map/ppermute | solution.py:53
  145.4 4.6 %collective-permute-start.4 = (f32[192,1024]{1,0:T(8,128)S(1)}, f32[192,1024]{1,0:T(8,128)S(1)}, u32[]{:S(2)}, u32[]{:S(2)}) collective-permute-start(f32[192,1024]{1,0:T(8,128)S(1)} %copy.55), channel_id=1, source_target_pairs={{0,0},{16,1},{32,2},{48,3},{64,4},{80,5},{96,6},{112,7},{1,8},{17,... | collective-permute-start | bytes 2359304 | tf_op jit(solution)/shard_map/ppermute | solution.py:64
  151.7 44.6 %reduce-scatter.7.cloned.1.call-done = f32[384,512]{1,0:T(8,128)} async-done(((f32[1536,512]{1,0:T(8,128)}), f32[384,512]{1,0:T(8,128)}) %reduce-scatter.7.cloned.1.call-update) | async-done | bytes 786448 | tf_op jit(solution)/shard_map/reduce_scatter | solution.py:55
  198.1 4.6 %collective-permute-start.3 = (f32[192,512]{1,0:T(8,128)}, f32[192,512]{1,0:T(8,128)S(1)}, u32[]{:S(2)}, u32[]{:S(2)}) collective-permute-start(f32[192,512]{1,0:T(8,128)} %dynamic-slice_bitcast_fusion.2), channel_id=1, source_target_pairs={{0,8},{8,0},{1,9},{9,1},{2,10},{10,2},{3,11},{11,3},{4,12},{12,4},... | collective-permute-start | bytes 1179656 | tf_op jit(solution)/shard_map/ppermute | solution.py:58
  204.6 7.3 %collective-permute-done.3 = f32[192,512]{1,0:T(8,128)S(1)} collective-permute-done((f32[192,512]{1,0:T(8,128)}, f32[192,512]{1,0:T(8,128)S(1)}, u32[]{:S(2)}, u32[]{:S(2)}) %collective-permute-start.3) | collective-permute-done | bytes 393248 | tf_op jit(solution)/shard_map/ppermute | solution.py:58
  219.1 3.4 collective-permute-done.5
  222.5 3.4 fusion.4
  226.0 25.9 %reduce-scatter.9.cloned.1.call-done = f32[192,512]{1,0:T(8,128)} async-done(((f32[768,512]{1,0:T(8,128)}), f32[192,512]{1,0:T(8,128)}) %reduce-scatter.9.cloned.1.call-update) | async-done | bytes 393232 | tf_op jit(solution)/shard_map/reduce_scatter | solution.py:74
  252.0 21.9 %reduce-scatter.11.cloned.1.call-done = f32[48,512]{1,0:T(8,128)} async-done(((f32[192,512]{1,0:T(8,128)}), f32[48,512]{1,0:T(8,128)}) %reduce-scatter.11.cloned.1.call-update) | async-done | bytes 98320 | tf_op jit(solution)/shard_map/reduce_scatter | solution.py:75
  273.9 43.5 %all-reduce.2.cloned.1.call-done = f32[48,512]{1,0:T(8,128)} async-done(((f32[48,512]{1,0:T(8,128)}), f32[48,512]{1,0:T(8,128)}) %all-reduce.2.cloned.1.call-update) | async-done | bytes 98320 | tf_op jit(solution)/shard_map/psum | solution.py:76
  317.4 12.7 %all_gather.14 = f32[192,512]{1,0:T(8,128)} all-gather(f32[48,512]{1,0:T(8,128)} %all-reduce.2.cloned.1.call-done), channel_id=1, replica_groups=mesh['xl'=2,'z'=4,'xh'=2,'y'=4,'core'=2] {'z'}, dimensions={0}, use_global_device_ids=true | all-gather | bytes 491520 | tf_op jit(solution)/shard_map/all_gather | solution.py:77
  330.1 30.0 %all-gather.8.cloned.1.call-done = f32[768,512]{1,0:T(8,128)} async-done(((f32[192,512]{1,0:T(8,128)}), f32[768,512]{1,0:T(8,128)}) %all-gather.8.cloned.1.call-update) | async-done | bytes 1572880 | tf_op jit(solution)/shard_map/all_gather | solution.py:78
  362.8 5.5 %all-to-all-start = ((f32[2,192,512]{1,0,2:T(2,128)}), f32[2,192,512]{1,0,2:T(2,128)S(1)}, u32[]{:S(2)}, u32[]{:S(2)}) async-start(f32[2,192,512]{1,0,2:T(2,128)} %copy.52), calls=%async_computation.2 | async-start | bytes 2097152 | tf_op jit(solution)/shard_map/all_to_all | solution.py:87
  368.3 17.1 %all-to-all-done = f32[2,192,512]{1,0,2:T(2,128)S(1)} async-done(((f32[2,192,512]{1,0,2:T(2,128)}), f32[2,192,512]{1,0,2:T(2,128)S(1)}, u32[]{:S(2)}, u32[]{:S(2)}) %all-to-all-start) | async-done | bytes 786464 | tf_op jit(solution)/shard_map/all_to_all | solution.py:87
  388.1 3.7 maximum_select_fusion
  396.4 3.9 fusion.7
  (80 shorter events, 44.5 us)
Async XLA Ops:
  7.2 353.7 %copy-start = (f32[512,512]{1,0:T(8,128)S(1)}, f32[512,512]{1,0:T(8,128)}, u32[]{:S(2)}) copy-start(f32[512,512]{1,0:T(8,128)} %param.11) | copy-start | bytes 3145732
  7.2 48.0 %all-gather.4.cloned.1.call-start = ((), (), s32[]{:S(2)}) async-start(), calls=%async_computation.5 | async-start | bytes 3538944 | tf_op jit(solution)/shard_map/all_gather | solution.py:60
  10.0 91.3 %all-gather.6.cloned.1.call-start = ((), (), s32[]{:S(2)}) async-start(), calls=%async_computation.7 | async-start | bytes 3538944 | tf_op jit(solution)/shard_map/all_gather | solution.py:61
  11.9 138.2 %reduce-scatter.5.cloned.1.call-start = ((), (), s32[]{:S(2)}) async-start(), calls=%async_computation.6 | async-start | bytes 3932160 | tf_op jit(solution)/shard_map/reduce_scatter | solution.py:55
  86.4 8.7 %collective-permute-start = (f32[2,4,192,512]{3,2,1,0:T(8,128)}, f32[2,4,192,512]{3,2,1,0:T(8,128)}, u32[]{:S(2)}, u32[]{:S(2)}) collective-permute-start(f32[2,4,192,512]{3,2,1,0:T(8,128)} %dynamic-slice_bitcast_fusion.1), channel_id=1, source_target_pairs={{0,1},{1,0},{2,3},{3,2},{4,5},{5,4},{6,7},{7,6},{8,9},{9,8},{10,11... | collective-permute-start | bytes 9437192 | tf_op jit(solution)/shard_map/ppermute | solution.py:53
  100.8 95.5 %reduce-scatter.7.cloned.1.call-start = ((), (), s32[]{:S(2)}) async-start(), calls=%async_computation.8 | async-start | bytes 3932160 | tf_op jit(solution)/shard_map/reduce_scatter | solution.py:55
  128.5 11.0 %copy-start.1 = (f32[3072,512]{1,0:T(8,128)S(1)}, f32[3072,512]{1,0:T(8,128)}, u32[]{:S(2)}) copy-start(f32[3072,512]{1,0:T(8,128)} %copy.50) | copy-start | bytes 18874372
  130.9 8.6 %collective-permute-start.2 = (f32[2,4,192,512]{3,2,1,0:T(8,128)S(1)}, f32[2,4,192,512]{3,2,1,0:T(8,128)S(1)}, u32[]{:S(2)}, u32[]{:S(2)}) collective-permute-start(f32[2,4,192,512]{3,2,1,0:T(8,128)S(1)} %dynamic-slice_bitcast_fusion), channel_id=1, source_target_pairs={{0,1},{1,0},{2,3},{3,2},{4,5},{5,4},{6,7},{7,6},{8,9},{9,8},{10,11... | collective-permute-start | bytes 9437192 | tf_op jit(solution)/shard_map/ppermute | solution.py:53
  142.2 109.7 %reduce-scatter.9.cloned.1.call-start = ((), (), s32[]{:S(2)}) async-start(), calls=%async_computation.9 | async-start | bytes 1966080 | tf_op jit(solution)/shard_map/reduce_scatter | solution.py:74
  145.4 59.2 %collective-permute-start.4 = (f32[192,1024]{1,0:T(8,128)S(1)}, f32[192,1024]{1,0:T(8,128)S(1)}, u32[]{:S(2)}, u32[]{:S(2)}) collective-permute-start(f32[192,1024]{1,0:T(8,128)S(1)} %copy.55), channel_id=1, source_target_pairs={{0,0},{16,1},{32,2},{48,3},{64,4},{80,5},{96,6},{112,7},{1,8},{17,... | collective-permute-start | bytes 2359304 | tf_op jit(solution)/shard_map/ppermute | solution.py:64
  151.1 51.6 %collective-permute-start.1 = (f32[192,512]{1,0:T(8,128)S(1)}, f32[192,512]{1,0:T(8,128)}, u32[]{:S(2)}, u32[]{:S(2)}) collective-permute-start(f32[192,512]{1,0:T(8,128)S(1)} %dynamic-slice_bitcast_fusion.3), channel_id=1, source_target_pairs={{0,8},{8,0},{1,9},{9,1},{2,10},{10,2},{3,11},{11,3},{4,12},{12,4},... | collective-permute-start | bytes 1179656 | tf_op jit(solution)/shard_map/ppermute | solution.py:58
  198.1 13.9 %collective-permute-start.3 = (f32[192,512]{1,0:T(8,128)}, f32[192,512]{1,0:T(8,128)S(1)}, u32[]{:S(2)}, u32[]{:S(2)}) collective-permute-start(f32[192,512]{1,0:T(8,128)} %dynamic-slice_bitcast_fusion.2), channel_id=1, source_target_pairs={{0,8},{8,0},{1,9},{9,1},{2,10},{10,2},{3,11},{11,3},{4,12},{12,4},... | collective-permute-start | bytes 1179656 | tf_op jit(solution)/shard_map/ppermute | solution.py:58
  204.6 9.2 %copy-start.5 = (f32[192,1024]{1,0:T(8,128)}, f32[192,1024]{1,0:T(8,128)S(1)}, u32[]{:S(2)}) copy-start(f32[192,1024]{1,0:T(8,128)S(1)} %collective-permute-done.4) | copy-start | bytes 2359300
  213.8 4.3 %copy-start.3 = (f32[512,512]{1,0:T(8,128)}, f32[512,512]{1,0:T(8,128)S(1)}, u32[]{:S(2)}) copy-start(f32[512,512]{1,0:T(8,128)S(1)} %fusion.10) | copy-start | bytes 3145732
  218.1 4.4 %collective-permute-start.5 = (f32[768,512]{1,0:T(8,128)}, f32[768,512]{1,0:T(8,128)}, u32[]{:S(2)}, u32[]{:S(2)}) collective-permute-start(f32[768,512]{1,0:T(8,128)} %fusion.2), channel_id=1, source_target_pairs={{0,1},{1,0},{2,3},{3,2},{4,5},{5,4},{6,7},{7,6},{8,9},{9,8},{10,11... | collective-permute-start | bytes 4718600 | tf_op jit(solution)/shard_map/ppermute | solution.py:73
  226.0 135.0 %copy-start.6 = (f32[384,512]{1,0:T(8,128)S(1)}, f32[384,512]{1,0:T(8,128)}, u32[]{:S(2)}) copy-start(f32[384,512]{1,0:T(8,128)} %reduce-scatter.7.cloned.1.call-done) | copy-start | bytes 2359300
  226.0 135.0 %copy-start.8 = (f32[192,512]{1,0:T(8,128)S(1)}, f32[192,512]{1,0:T(8,128)}, u32[]{:S(2)}) copy-start(f32[192,512]{1,0:T(8,128)} %copy-done.7) | copy-start | bytes 1179652
  226.0 135.5 %copy-start.9 = (f32[1,192,512]{2,1,0:T(8,128)S(1)}, f32[1,192,512]{2,1,0:T(8,128)}, u32[]{:S(2)}) copy-start(f32[1,192,512]{2,1,0:T(8,128)} %get-tuple-element.30) | copy-start | bytes 1179652
  226.0 47.8 %reduce-scatter.11.cloned.1.call-start = ((), (), s32[]{:S(2)}) async-start(), calls=%async_computation.10 | async-start | bytes 491520 | tf_op jit(solution)/shard_map/reduce_scatter | solution.py:75
  251.9 65.4 %all-reduce.2.cloned.1.call-start = ((), (), s32[]{:S(2)}) async-start(), calls=%async_computation.11 | async-start | bytes 196608 | tf_op jit(solution)/shard_map/psum | solution.py:76
  273.9 86.2 %all-gather.8.cloned.1.call-start = ((), (), s32[]{:S(2)}) async-start(), calls=%async_computation.12 | async-start | bytes 1966080 | tf_op jit(solution)/shard_map/all_gather | solution.py:78
  360.1 28.1 %collective-permute-start.6 = (f32[768,512]{1,0:T(8,128)}, f32[768,512]{1,0:T(8,128)}, u32[]{:S(2)}, u32[]{:S(2)}) collective-permute-start(f32[768,512]{1,0:T(8,128)} %all-gather.8.cloned.1.call-done), channel_id=1, source_target_pairs={{0,1},{1,0},{2,3},{3,2},{4,5},{5,4},{6,7},{7,6},{8,9},{9,8},{10,11... | collective-permute-start | bytes 4718600 | tf_op jit(solution)/shard_map/ppermute | solution.py:79
  362.8 22.6 %all-to-all-start = ((f32[2,192,512]{1,0,2:T(2,128)}), f32[2,192,512]{1,0,2:T(2,128)S(1)}, u32[]{:S(2)}, u32[]{:S(2)}) async-start(f32[2,192,512]{1,0,2:T(2,128)} %copy.52), calls=%async_computation.2 | async-start | bytes 2097152 | tf_op jit(solution)/shard_map/all_to_all | solution.py:87
  394.0 2.4 copy-start.4
  (3 other events, 6.1 us)
Sparse Core Ops, SparseCore 0:
  10.2 44.9 all-gather.3
  57.4 43.7 all-gather.5
  103.7 40.2 reduce-scatter.4
  146.2 50.0 reduce-scatter.6
  226.1 25.7 reduce-scatter.8
  254.2 19.6 reduce-scatter.10
  276.1 41.1 all-reduce.1
  330.2 29.8 all-gather.7

commit v2 on v1

v2 whole, which is shorter than its diff:
```python
import jax
import jax.numpy as jnp
from jax import lax
from jax.experimental import pallas as pl
from jax.experimental.pallas import tpu as pltpu
from jax.sharding import Mesh, PartitionSpec as P

BLOCK = 128
ROW = ("xl", "z")
COL = ("xh", "y", "core")
PLANE = ("xh", "y")
CHIPS = ("xl", "z", "xh", "y")
ALL = ROW + COL
SIZES = (2, 4, 2, 4, 2)
SWAP = ((0, 1), (1, 0))
TILES = 2


def product(left, right, contract=((1,), (0,))):
    return lax.dot_general(left, right, (contract, ((), ())), precision=lax.Precision.HIGH,
                           preferred_element_type=jnp.float32)


def linear(xl, z, xh, y, core):
    return (((xl * 4 + z) * 2 + xh) * 4 + y) * 2 + core


def factor_routes():
    routes = []
    for xl in range(2):
        for z in range(4):
            for xh in range(2):
                for y in range(4):
                    for core in range(2):
                        source = linear(y // 2, (y % 2) * 2 + core, xl, z, xh)
                        routes.append((source, linear(xl, z, xh, y, core)))
    return routes


def split(value):
    high = value.astype(jnp.bfloat16)
    return high, (value - high.astype(jnp.float32)).astype(jnp.bfloat16)


def half_kernel(side_ref, a_ref, factor_ref, after_ref, out_ref, high_ref, low_ref):
    del side_ref, after_ref

    @pl.when(pl.program_id(0) == 0)
    def _():
        high, low = split(factor_ref[...])
        high_ref[...] = high
        low_ref[...] = low

    tiles, part, depth = a_ref.shape
    a_high, a_low = split(a_ref[...].reshape(tiles * part, depth))
    dims = (((1,), (1,)), ((), ()))
    dot = lambda l, r: lax.dot_general(l, r, dims, preferred_element_type=jnp.float32)
    total = dot(a_high, high_ref[...]) + dot(a_high, low_ref[...]) + dot(a_low, high_ref[...])
    out_ref[...] = total.reshape(out_ref.shape)


def half_product(ancestor, factor_t, side, after):
    rows, depth = ancestor.shape
    width = factor_t.shape[0]
    part = rows // 16
    view = ancestor.reshape(8, 2, part, depth)
    return pl.pallas_call(
        half_kernel,
        grid_spec=pltpu.PrefetchScalarGridSpec(
            num_scalar_prefetch=1,
            grid=(8 // TILES,),
            in_specs=[
                pl.BlockSpec((TILES, None, part, depth), lambda i, side: (i, side[0], 0, 0)),
                pl.BlockSpec((width, depth), lambda i, side: (0, 0), pipeline_mode=pl.Buffered(1)),
                pl.BlockSpec(memory_space=pl.ANY),
            ],
            out_specs=pl.BlockSpec((TILES, part, width), lambda i, side: (i, 0, 0)),
            scratch_shapes=[pltpu.VMEM((width, depth), jnp.bfloat16)] * 2,
        ),
        out_shape=jax.ShapeDtypeStruct((8, part, width), jnp.float32),
        cost_estimate=pl.CostEstimate(
            flops=3 * rows * depth * width, transcendentals=0,
            bytes_accessed=2 * rows * depth + 4 * width * depth + 2 * rows * width),
        compiler_params=pltpu.CompilerParams(vmem_limit_bytes=40 * 1024 * 1024),
    )(side.reshape(1), view, factor_t, after)


def per_device(ancestor, lhat_one, lhat_two, link_two, diag_one, diag_two, mask_one, mask_two):
    row_index = lax.axis_index(ROW)
    column_index = lax.axis_index(COL)
    core = lax.axis_index("core")
    rows, depth = ancestor.shape
    width = link_two.shape[0]
    blocks = depth // BLOCK
    part = rows // 16
    half = width // 2

    def masked(shard, mask):
        own = lax.dynamic_slice_in_dim(mask, column_index * blocks, blocks).astype(jnp.float32)
        return shard.T * jnp.broadcast_to(own[:, None], (blocks, BLOCK)).reshape(1, depth)

    def row_sum(factor_t, after):
        send = half_product(ancestor, factor_t, 1 - core, after)
        keep = half_product(ancestor, factor_t, core, send)
        chip = keep + lax.ppermute(send, "core", SWAP)
        pieces = lax.all_to_all(chip, PLANE, split_axis=0, concat_axis=0, tiled=True)
        return pieces.sum(0), keep

    def to_columns(own_rows):
        pieces = lax.all_to_all(own_rows.T, COL, split_axis=0, concat_axis=0, tiled=True)
        return pieces.reshape(16, width // 16, part).transpose(0, 2, 1).reshape(rows, width // 16)

    def half_of(value, side):
        return lax.dynamic_slice_in_dim(value, side * half, half, 0)

    factor_one = lax.all_gather(masked(lhat_one, mask_one), ROW, axis=0, tiled=True)
    factor_two = lax.all_gather(masked(lhat_two, mask_two), ROW, axis=0, tiled=True)
    local = jnp.concatenate(
        [lax.dynamic_slice_in_dim(f, row_index * part, part, 1) for f in (factor_one, factor_two)], axis=0)
    local = lax.ppermute(local, ALL, factor_routes())
    sum_one, done_one = row_sum(factor_one, link_two)
    one_part = product(local[:width], sum_one)
    link_part = product(sum_one, local[width:], ((0,), (1,))) - product(one_part, link_two)
    moved_one = product(sum_one, link_two)
    last_part = product(link_two, link_part, ((0,), (0,))) + product(local[width:], moved_one)
    sum_two, _ = row_sum(factor_two, done_one)
    x_one, sum_two = lax.optimization_barrier((to_columns(-sum_one), sum_two))
    two_part = product(local[width:], sum_two) - last_part
    link_base = -product(diag_one, link_two)
    two_base = diag_two - product(link_two, link_base, ((0,), (0,)))
    parts = (one_part, link_part, two_part)
    keep = jnp.concatenate([half_of(p, core) for p in parts])
    send = jnp.concatenate([half_of(p, 1 - core) for p in parts])
    chip = keep + lax.ppermute(send, "core", SWAP)
    chips = 64
    piece = lax.all_to_all(chip.reshape(chips, 3 * half // chips, width), CHIPS,
                           split_axis=0, concat_axis=0, tiled=True).sum(0)
    whole = lax.all_to_all(jnp.broadcast_to(piece[None], (chips,) + piece.shape), CHIPS,
                           split_axis=0, concat_axis=0, tiled=True).reshape(3 * half, width)
    other = lax.ppermute(whole, "core", SWAP)
    low = jnp.where(core == 0, whole, other)
    high = jnp.where(core == 0, other, whole)

    def joined(index, base):
        cut = slice(index * half, (index + 1) * half)
        return jnp.concatenate([low[cut], high[cut]]) + base

    return (x_one, joined(0, diag_one), to_columns(moved_one - sum_two),
            joined(1, link_base), joined(2, two_base))


def solution(mesh):
    fine = Mesh(mesh.devices.reshape(SIZES), ALL)
    in_specs = (P(ROW, COL), P(COL, ROW), P(COL, ROW), P(), P(), P(), P(), P())
    out_specs = (P(ROW, COL), P(), P(ROW, COL), P(), P())
    return jax.shard_map(
        per_device, mesh=fine, in_specs=in_specs, out_specs=out_specs, check_vma=False
    )
```

time: 408 us -> 376 us (0.922)
  waiting for transfers between devices: 248 us -> 138 us
  blocking collectives: 12.7 us -> 68.3 us
  Pallas kernels: 0 us -> 43.1 us
  matrix products: 53.1 us -> 10.3 us
  starting transfers between devices: 23.8 us -> 52.9 us
  local copies, waits for them, and re-layouts: 34.9 us -> 22.5 us
  other arithmetic: 19.9 us -> 25.8 us
    reduce_scatter x4 -> x0, waiting for transfers between devices: 92.4 us -> none  [the longest x2 44.6 us: row_sum(): lax.psum_scatter(chip, 'y', scatter_dimension=0, tiled=True)]
    all_to_all x0 -> x2, blocking collectives: none -> 68.3 us  [the longest x1 35.6 us: per_device(): lax.all_to_all(jnp.broadcast_to(piece[None], (chips,) + piece.shape), CHI...]
    psum x1 -> x0, waiting for transfers between devices: 43.5 us -> none  [per_device(): piece = lax.psum(piece, ('xl', 'xh'))]
    pallas_call x0 -> x4, Pallas kernels: none -> 43.1 us  [half_product(): pl.pallas_call(half_kernel, grid_spec=pltpu.PrefetchScalarGridSpec(num_sc...]
    dot_general x8 -> x9, matrix products: 53.1 us -> 10.3 us  [product(): lax.dot_general(left, right, (contract, ((), ())), precision=lax.Precisio...]
    all_to_all x1 -> x4, starting transfers between devices: 5.52 us -> 37.5 us  [the longest x2 26 us: to_columns(): lax.all_to_all(own_rows.T, COL, split_axis=0, concat_axis=0, tiled=True)]
    ppermute x1, waiting for transfers between devices: 0.01 us -> 31.8 us  [per_device(): local = lax.ppermute(local, ALL, factor_routes())]
    all_to_all x1 -> x4, waiting for transfers between devices: 17.1 us -> 40.1 us  [the longest x2 22.9 us: row_sum(): lax.all_to_all(chip, PLANE, split_axis=0, concat_axis=0, tiled=True)]
  transfers between devices with their start and end apart: 16 -> 11, of which waited for: 12 -> 7; matrix products, arithmetic and copies ran while one was open for 20% -> 8% of each run, Pallas kernels for 0% -> 11%
where the time goes in v2:
time: 376 us; the launch traced here: 375 us
  waiting for transfers between devices  138 us (37%)
  blocking collectives  68.3 us (18%)
  starting transfers between devices  52.9 us (14%)
  Pallas kernels  43.1 us (11%)
  other arithmetic  25.8 us (7%)
  local copies, waits for them, and re-layouts  22.5 us (6%)
  between operations  14.3 us (4%)
  matrix products  10.3 us (3%)
    all_gather x1, waiting for transfers between devices, per_device(): lax.all_gather(masked(lhat_one, mask_one), ROW, axis=0, tiled=True)  43.3 us
    pallas_call x4, Pallas kernels, half_product(): pl.pallas_call(half_kernel, grid_spec=pltpu.PrefetchScalarGridSpec(num_sc...  43.1 us
    all_to_all x1, blocking collectives, per_device(): lax.all_to_all(jnp.broadcast_to(piece[None], (chips,) + piece.shape), CHI...  35.6 us
    all_to_all x1, blocking collectives, per_device(): lax.all_to_all(chip.reshape(chips, 3 * half // chips, width), CHIPS, spli...  32.6 us
    ppermute x1, waiting for transfers between devices, per_device(): local = lax.ppermute(local, ALL, factor_routes())  31.8 us
    all_to_all x2, starting transfers between devices, to_columns(): lax.all_to_all(own_rows.T, COL, split_axis=0, concat_axis=0, tiled=True)  26 us
    all_to_all x2, waiting for transfers between devices, row_sum(): lax.all_to_all(chip, PLANE, split_axis=0, concat_axis=0, tiled=True)  22.9 us
    all_gather x1, waiting for transfers between devices, per_device(): lax.all_gather(masked(lhat_two, mask_two), ROW, axis=0, tiled=True)  19.6 us
  transfers between devices with their start and end apart: 11, of which 7 were waited for; matrix products, arithmetic and copies ran while one was open for 8% of the time, Pallas kernels for 11%

profile of v2, /device:TPU:1, one launch (start us, length us, event | category | flops | bytes accessed | tf_op | source)
XLA Modules:
  0.0 375.0 jit_solution(10719905301567082119)
XLA Ops:
  11.9 43.3 %all-gather.3.cloned.1.call-done.factor_ref = f32[512,1536]{1,0:T(8,128)} async-done(((f32[64,1536]{1,0:T(8,128)}), f32[512,1536]{1,0:T(8,128)}) %all-gather.3.cloned.1.call-update) | async-done | bytes 3145744 | tf_op jit(solution)/shard_map/all_gather | solution.py:116
  57.1 11.2 %shard_map.119.after_ref = f32[8,192,512]{2,1,0:T(8,128)} custom-call(s32[1]{0:T(128)} %bitcast.4.side_ref, f32[8,2,192,1536]{3,2,1,0:T(8,128)} %bitcast.43, f32[512,1536]{1,0:T(8,128)S(1)} %copy-done.4, f32[512,512]{1,0:T(8,128)S(1)} %copy-done), custom_call_target="tpu_custom_call" | custom-call | flops 7247757312 | bytes 15728640 | tf_op jit(solution)/shard_map/pallas_call | solution.py:67
  68.3 3.1 collective-permute-start
  71.4 10.3 %shard_map.120.after_ref = f32[8,192,512]{2,1,0:T(8,128)S(1)} custom-call(s32[1]{0:T(128)} %bitcast.side_ref, f32[8,2,192,1536]{3,2,1,0:T(8,128)} %bitcast.44, f32[512,1536]{1,0:T(8,128)S(1)} %copy-done.4, f32[8,192,512]{2,1,0:T(8,128)} %shard_map.119.after_ref), custom_call_target="tpu_custom_call" | custom-call | flops 7247757312 | bytes 15728640 | tf_op jit(solution)/shard_map/pallas_call | solution.py:67
  81.7 19.6 %all-gather.5.cloned.1.call-done.factor_ref = f32[512,1536]{1,0:T(8,128)} async-done(((f32[64,1536]{1,0:T(8,128)}), f32[512,1536]{1,0:T(8,128)}) %all-gather.5.cloned.1.call-update) | async-done | bytes 3145744 | tf_op jit(solution)/shard_map/all_gather | solution.py:117
  103.2 11.2 %shard_map.121.after_ref = f32[8,192,512]{2,1,0:T(8,128)} custom-call(s32[1]{0:T(128)} %bitcast.4.side_ref, f32[8,2,192,1536]{3,2,1,0:T(8,128)} %bitcast.45, f32[512,1536]{1,0:T(8,128)S(1)} %copy-done.2, f32[8,192,512]{2,1,0:T(8,128)S(1)} %shard_map.120.after_ref), custom_call_target="tpu_custom_call" | custom-call | flops 7247757312 | bytes 15728640 | tf_op jit(solution)/shard_map/pallas_call | solution.py:67
  114.4 3.0 collective-permute-start.1
  117.4 4.3 %add.51 = f32[8,192,512]{2,1,0:T(8,128)} add(f32[8,192,512]{2,1,0:T(8,128)S(1)} %shard_map.120.after_ref, f32[8,192,512]{2,1,0:T(8,128)} %collective-permute-done) | non-fusion elementwise | flops 786432 | bytes 9437184 | tf_op jit(solution)/shard_map/add | solution.py:105
  121.7 6.4 %all-to-all-start = ((f32[8,192,512]{2,1,0:T(8,128)}), f32[8,192,512]{2,1,0:T(8,128)}, u32[]{:S(2)}, u32[]{:S(2)}) async-start(f32[8,192,512]{2,1,0:T(8,128)} %add.51), calls=%async_computation | async-start | bytes 6291456 | tf_op jit(solution)/shard_map/all_to_all | solution.py:106
  128.1 10.3 %shard_map.122 = f32[8,192,512]{2,1,0:T(8,128)S(1)} custom-call(s32[1]{0:T(128)} %bitcast.side_ref, f32[8,2,192,1536]{3,2,1,0:T(8,128)} %bitcast.46, f32[512,1536]{1,0:T(8,128)S(1)} %copy-done.3, f32[8,192,512]{2,1,0:T(8,128)} %shard_map.121.after_ref), custom_call_target="tpu_custom_call" | custom-call | flops 7247757312 | bytes 15728640 | tf_op jit(solution)/shard_map/pallas_call | solution.py:67
  138.4 4.3 %add.52 = f32[8,192,512]{2,1,0:T(8,128)} add(f32[8,192,512]{2,1,0:T(8,128)S(1)} %shard_map.122, f32[8,192,512]{2,1,0:T(8,128)} %collective-permute-done.1) | non-fusion elementwise | flops 786432 | bytes 9437184 | tf_op jit(solution)/shard_map/add | solution.py:105
  142.8 22.9 %all-to-all-done = f32[8,192,512]{2,1,0:T(8,128)} async-done(((f32[8,192,512]{2,1,0:T(8,128)}), f32[8,192,512]{2,1,0:T(8,128)}, u32[]{:S(2)}, u32[]{:S(2)}) %all-to-all-start) | async-done | bytes 3145760 | tf_op jit(solution)/shard_map/all_to_all | solution.py:106
  165.6 5.2 %all-to-all-start.2 = ((f32[8,192,512]{2,1,0:T(8,128)}), f32[8,192,512]{2,1,0:T(8,128)}, u32[]{:S(2)}, u32[]{:S(2)}) async-start(f32[8,192,512]{2,1,0:T(8,128)} %add.52), calls=%async_computation.2 | async-start | bytes 6291456 | tf_op jit(solution)/shard_map/all_to_all | solution.py:106
  173.6 5.8 %collective-permute-start.2 = (f32[1024,192]{0,1:T(8,128)}, f32[1024,192]{0,1:T(8,128)S(1)}, u32[]{:S(2)}, u32[]{:S(2)}) collective-permute-start(f32[1024,192]{0,1:T(8,128)} %copy.23), channel_id=1, source_target_pairs={{0,0},{16,1},{32,2},{48,3},{64,4},{80,5},{96,6},{112,7},{1,8},{17,... | collective-permute-start | bytes 2359304 | tf_op jit(solution)/shard_map/ppermute | solution.py:120
  179.4 2.3 reduce_sum.27
  182.7 31.8 %collective-permute-done.2 = f32[1024,192]{0,1:T(8,128)S(1)} collective-permute-done((f32[1024,192]{0,1:T(8,128)}, f32[1024,192]{0,1:T(8,128)S(1)}, u32[]{:S(2)}, u32[]{:S(2)}) %collective-permute-start.2) | collective-permute-done | bytes 786464 | tf_op jit(solution)/shard_map/ppermute | solution.py:120
  219.5 20.7 %all-to-all-start.1 = ((f32[16,32,192]{2,1,0:T(8,128)}), f32[16,32,192]{2,1,0:T(8,128)}, u32[]{:S(2)}, u32[]{:S(2)}) async-start(f32[16,32,192]{2,1,0:T(8,128)} %bitcast.47), calls=%async_computation.1 | async-start | bytes 1048576 | tf_op jit(solution)/shard_map/all_to_all | solution.py:110
  240.2 3.0 reduce_sum.28
  245.4 6.1 %all-to-all-done.1 = f32[16,32,192]{2,1,0:T(8,128)} async-done(((f32[16,32,192]{2,1,0:T(8,128)}), f32[16,32,192]{2,1,0:T(8,128)}, u32[]{:S(2)}, u32[]{:S(2)}) %all-to-all-start.1) | async-done | bytes 393248 | tf_op jit(solution)/shard_map/all_to_all | solution.py:110
  258.2 3.0 collective-permute-done.3
  264.2 32.6 %all_to_all.38 = f32[64,12,512]{2,1,0:T(8,128)} all-to-all(f32[64,12,512]{2,1,0:T(8,128)S(1)} %reshape.55), channel_id=1, replica_groups=mesh['xl'=2,'z'=4,'xh'=2,'y'=4,'core'=2] {'xl','z','xh','y'}, dimensions={0} | all-to-all | bytes 3145728 | tf_op jit(solution)/shard_map/all_to_all | solution.py:136
  298.9 35.6 %all_to_all.39 = f32[64,12,512]{2,1,0:T(8,128)S(1)} all-to-all(f32[64,12,512]{2,1,0:T(8,128)S(1)} %broadcast_in_dim.8), channel_id=1, replica_groups=mesh['xl'=2,'z'=4,'xh'=2,'y'=4,'core'=2] {'xl','z','xh','y'}, dimensions={0} | all-to-all | bytes 3145728 | tf_op jit(solution)/shard_map/all_to_all | solution.py:138
  340.0 5.3 %all-to-all-start.5 = ((f32[16,32,192]{2,1,0:T(8,128)}), f32[16,32,192]{2,1,0:T(8,128)S(1)}, u32[]{:S(2)}, u32[]{:S(2)}) async-start(f32[16,32,192]{2,1,0:T(8,128)} %bitcast.12), calls=%async_computation.5 | async-start | bytes 1048576 | tf_op jit(solution)/shard_map/all_to_all | solution.py:110
  345.3 11.2 %all-to-all-done.5 = f32[16,32,192]{2,1,0:T(8,128)S(1)} async-done(((f32[16,32,192]{2,1,0:T(8,128)}), f32[16,32,192]{2,1,0:T(8,128)S(1)}, u32[]{:S(2)}, u32[]{:S(2)}) %all-to-all-start.5) | async-done | bytes 393248 | tf_op jit(solution)/shard_map/all_to_all | solution.py:110
  (81 shorter events, 48.3 us)
Async XLA Ops:
  7.2 48.1 %copy-start = (f32[512,512]{1,0:T(8,128)S(1)}, f32[512,512]{1,0:T(8,128)}, u32[]{:S(2)}) copy-start(f32[512,512]{1,0:T(8,128)} %after_ref.1) | copy-start | bytes 3145732
  7.2 48.0 %all-gather.3.cloned.1.call-start = ((), (), s32[]{:S(2)}) async-start(), calls=%async_computation.6 | async-start | bytes 3538944 | tf_op jit(solution)/shard_map/all_gather | solution.py:116
  10.0 91.3 %all-gather.5.cloned.1.call-start = ((), (), s32[]{:S(2)}) async-start(), calls=%async_computation.7 | async-start | bytes 3538944 | tf_op jit(solution)/shard_map/all_gather | solution.py:117
  55.2 1.9 copy-start.4
  68.3 49.1 %collective-permute-start = (f32[8,192,512]{2,1,0:T(8,128)}, f32[8,192,512]{2,1,0:T(8,128)}, u32[]{:S(2)}, u32[]{:S(2)}) collective-permute-start(f32[8,192,512]{2,1,0:T(8,128)} %shard_map.119.after_ref), channel_id=1, source_target_pairs={{0,1},{1,0},{2,3},{3,2},{4,5},{5,4},{6,7},{7,6},{8,9},{9,8},{10,11... | collective-permute-start | bytes 9437192 | tf_op jit(solution)/shard_map/ppermute | solution.py:105
  101.3 1.9 copy-start.2
  114.4 24.0 %collective-permute-start.1 = (f32[8,192,512]{2,1,0:T(8,128)}, f32[8,192,512]{2,1,0:T(8,128)}, u32[]{:S(2)}, u32[]{:S(2)}) collective-permute-start(f32[8,192,512]{2,1,0:T(8,128)} %shard_map.121.after_ref), channel_id=1, source_target_pairs={{0,1},{1,0},{2,3},{3,2},{4,5},{5,4},{6,7},{7,6},{8,9},{9,8},{10,11... | collective-permute-start | bytes 9437192 | tf_op jit(solution)/shard_map/ppermute | solution.py:105
  121.7 6.4 %copy-start.3 = (f32[512,1536]{1,0:T(8,128)S(1)}, f32[512,1536]{1,0:T(8,128)}, u32[]{:S(2)}) copy-start(f32[512,1536]{1,0:T(8,128)} %all-gather.5.cloned.1.call-done.factor_ref) | copy-start | bytes 9437188
  121.7 43.9 %all-to-all-start = ((f32[8,192,512]{2,1,0:T(8,128)}), f32[8,192,512]{2,1,0:T(8,128)}, u32[]{:S(2)}, u32[]{:S(2)}) async-start(f32[8,192,512]{2,1,0:T(8,128)} %add.51), calls=%async_computation | async-start | bytes 6291456 | tf_op jit(solution)/shard_map/all_to_all | solution.py:106
  165.6 53.9 %all-to-all-start.2 = ((f32[8,192,512]{2,1,0:T(8,128)}), f32[8,192,512]{2,1,0:T(8,128)}, u32[]{:S(2)}, u32[]{:S(2)}) async-start(f32[8,192,512]{2,1,0:T(8,128)} %add.52), calls=%async_computation.2 | async-start | bytes 6291456 | tf_op jit(solution)/shard_map/all_to_all | solution.py:106
  173.6 40.9 %collective-permute-start.2 = (f32[1024,192]{0,1:T(8,128)}, f32[1024,192]{0,1:T(8,128)S(1)}, u32[]{:S(2)}, u32[]{:S(2)}) collective-permute-start(f32[1024,192]{0,1:T(8,128)} %copy.23), channel_id=1, source_target_pairs={{0,0},{16,1},{32,2},{48,3},{64,4},{80,5},{96,6},{112,7},{1,8},{17,... | collective-permute-start | bytes 2359304 | tf_op jit(solution)/shard_map/ppermute | solution.py:120
  181.7 33.5 %copy-start.1 = (f32[512,512]{1,0:T(8,128)S(1)}, f32[512,512]{1,0:T(8,128)}, u32[]{:S(2)}) copy-start(f32[512,512]{1,0:T(8,128)} %after_ref.1) | copy-start | bytes 3145732
  214.5 1.7 copy-start.8
  219.5 32.0 %all-to-all-start.1 = ((f32[16,32,192]{2,1,0:T(8,128)}), f32[16,32,192]{2,1,0:T(8,128)}, u32[]{:S(2)}, u32[]{:S(2)}) async-start(f32[16,32,192]{2,1,0:T(8,128)} %bitcast.47), calls=%async_computation.1 | async-start | bytes 1048576 | tf_op jit(solution)/shard_map/all_to_all | solution.py:110
  243.2 1.5 copy-start.9
  245.4 8.4 %copy-start.7 = (f32[192,512]{1,0:T(8,128)S(1)}, f32[192,512]{1,0:T(8,128)}, u32[]{:S(2)}) copy-start(f32[192,512]{1,0:T(8,128)} %reduce_sum.28) | copy-start | bytes 1179652
  256.7 4.5 %copy-start.10 = (f32[256,512]{1,0:T(8,128)S(1)}, f32[256,512]{1,0:T(8,128)}, u32[]{:S(2)}) copy-start(f32[256,512]{1,0:T(8,128)} %get-tuple-element.19) | copy-start | bytes 1572868
  256.7 4.5 %copy-start.11 = (f32[256,512]{1,0:T(8,128)S(1)}, f32[256,512]{1,0:T(8,128)}, u32[]{:S(2)}) copy-start(f32[256,512]{1,0:T(8,128)} %get-tuple-element.17) | copy-start | bytes 1572868
  256.8 4.4 %collective-permute-start.3 = (f32[768,512]{1,0:T(8,128)S(1)}, f32[768,512]{1,0:T(8,128)S(1)}, u32[]{:S(2)}, u32[]{:S(2)}) collective-permute-start(f32[768,512]{1,0:T(8,128)S(1)} %pad_maximum_fusion), channel_id=1, source_target_pairs={{0,1},{1,0},{2,3},{3,2},{4,5},{5,4},{6,7},{7,6},{8,9},{9,8},{10,11... | collective-permute-start | bytes 4718600 | tf_op jit(solution)/shard_map/ppermute | solution.py:134
  335.9 23.7 %collective-permute-start.4 = (f32[768,512]{1,0:T(8,128)}, f32[768,512]{1,0:T(8,128)}, u32[]{:S(2)}, u32[]{:S(2)}) collective-permute-start(f32[768,512]{1,0:T(8,128)} %reshape.56), channel_id=1, source_target_pairs={{0,1},{1,0},{2,3},{3,2},{4,5},{5,4},{6,7},{7,6},{8,9},{9,8},{10,11... | collective-permute-start | bytes 4718600 | tf_op jit(solution)/shard_map/ppermute | solution.py:140
  340.0 19.5 %copy-start.5 = (f32[768,512]{1,0:T(8,128)S(1)}, f32[768,512]{1,0:T(8,128)}, u32[]{:S(2)}) copy-start(f32[768,512]{1,0:T(8,128)} %reshape.56) | copy-start | bytes 4718596
  340.0 16.4 %all-to-all-start.5 = ((f32[16,32,192]{2,1,0:T(8,128)}), f32[16,32,192]{2,1,0:T(8,128)S(1)}, u32[]{:S(2)}, u32[]{:S(2)}) async-start(f32[16,32,192]{2,1,0:T(8,128)} %bitcast.12), calls=%async_computation.5 | async-start | bytes 1048576 | tf_op jit(solution)/shard_map/all_to_all | solution.py:110
  361.4 1.2 copy-start.6
  364.7 1.4 copy-start.15
  (3 other events, 3.0 us)
Sparse Core Ops, SparseCore 0:
  10.2 44.9 all-gather.2
  57.4 43.7 all-gather.4

commit v3 on v2

--- a/solution.py
+++ b/solution.py
@@ -4,6 +4,7 @@
 from jax.experimental import pallas as pl
 from jax.experimental.pallas import tpu as pltpu
 from jax.sharding import Mesh, PartitionSpec as P
+
 
 BLOCK = 128
 ROW = ("xl", "z")
@@ -101,33 +102,40 @@
 
     def row_sum(factor_t, after):
         send = half_product(ancestor, factor_t, 1 - core, after)
+        received = lax.ppermute(send, "core", SWAP)
         keep = half_product(ancestor, factor_t, core, send)
-        chip = keep + lax.ppermute(send, "core", SWAP)
+        chip = keep + received
         pieces = lax.all_to_all(chip, PLANE, split_axis=0, concat_axis=0, tiled=True)
         return pieces.sum(0), keep
 
     def to_columns(own_rows):
-        pieces = lax.all_to_all(own_rows.T, COL, split_axis=0, concat_axis=0, tiled=True)
-        return pieces.reshape(16, width // 16, part).transpose(0, 2, 1).reshape(rows, width // 16)
+        own_rows = jnp.concatenate([value.T for value in own_rows], axis=1)
+        pieces = lax.all_to_all(own_rows, COL, split_axis=0, concat_axis=0, tiled=True)
+        pieces = pieces.reshape(16, width // 16, 2, part).transpose(2, 0, 3, 1)
+        return pieces.reshape(2, rows, width // 16)
 
     def half_of(value, side):
         return lax.dynamic_slice_in_dim(value, side * half, half, 0)
 
-    factor_one = lax.all_gather(masked(lhat_one, mask_one), ROW, axis=0, tiled=True)
-    factor_two = lax.all_gather(masked(lhat_two, mask_two), ROW, axis=0, tiled=True)
-    local = jnp.concatenate(
-        [lax.dynamic_slice_in_dim(f, row_index * part, part, 1) for f in (factor_one, factor_two)], axis=0)
-    local = lax.ppermute(local, ALL, factor_routes())
+    def gathered(shard, mask):
+        shard = masked(shard, mask)
+        full = lax.all_gather(shard, ROW, axis=0, tiled=True)
+        rows_here = lax.dynamic_slice_in_dim(full, row_index * part, part, 1)
+        local = lax.ppermute(rows_here, ALL, factor_routes())
+        return full, local
+
+    factor_one, local_one = gathered(lhat_one, mask_one)
+    factor_two, local_two = gathered(lhat_two, mask_two)
     sum_one, done_one = row_sum(factor_one, link_two)
-    one_part = product(local[:width], sum_one)
-    link_part = product(sum_one, local[width:], ((0,), (1,))) - product(one_part, link_two)
+    sum_two, _ = row_sum(factor_two, done_one)
+    one_part = product(local_one, sum_one)
+    link_part = product(sum_one, local_two, ((0,), (1,))) - product(one_part, link_two)
     moved_one = product(sum_one, link_two)
-    last_part = product(link_two, link_part, ((0,), (0,))) + product(local[width:], moved_one)
-    sum_two, _ = row_sum(factor_two, done_one)
-    x_one, sum_two = lax.optimization_barrier((to_columns(-sum_one), sum_two))
-    two_part = product(local[width:], sum_two) - last_part
+    last_part = product(link_two, link_part, ((0,), (0,))) + product(local_two, moved_one)
+    two_part = product(local_two, sum_two) - last_part
     link_base = -product(diag_one, link_two)
     two_base = diag_two - product(link_two, link_base, ((0,), (0,)))
+    link_base, two_base = lax.optimization_barrier((link_base, two_base))
     parts = (one_part, link_part, two_part)
     keep = jnp.concatenate([half_of(p, core) for p in parts])
     send = jnp.concatenate([half_of(p, 1 - core) for p in parts])
@@ -145,8 +153,8 @@
         cut = slice(index * half, (index + 1) * half)
         return jnp.concatenate([low[cut], high[cut]]) + base
 
-    return (x_one, joined(0, diag_one), to_columns(moved_one - sum_two),
-            joined(1, link_base), joined(2, two_base))
+    x_one, x_two = to_columns((-sum_one, moved_one - sum_two))
+    return (x_one, joined(0, diag_one), x_two, joined(1, link_base), joined(2, two_base))
 
 
 def solution(mesh):

time: 376 us -> 371 us (0.987)
  blocking collectives: 68.3 us -> 90.3 us
  starting transfers between devices: 52.9 us -> 33 us
  waiting for transfers between devices: 138 us -> 129 us
    all_to_all x1, blocking collectives: 32.6 us -> 54.6 us  [per_device(): lax.all_to_all(chip.reshape(chips, 3 * half // chips, width), CHIPS, spli...]
    all_to_all x2 -> x1, starting transfers between devices: 26 us -> 5.2 us  [to_columns(): lax.all_to_all(own_rows, COL, split_axis=0, concat_axis=0, tiled=True)]
    all_to_all x2 -> x1, waiting for transfers between devices: 17.2 us -> 10.8 us  [to_columns(): lax.all_to_all(own_rows, COL, split_axis=0, concat_axis=0, tiled=True)]
    another operation x0 -> x5, local copies, waits for them, and re-layouts: none -> 4.14 us  [per_device(): x_one, x_two = to_columns((-sum_one, moved_one - sum_two))]
    ppermute x3 -> x4, waiting for transfers between devices: 31.8 us -> 28.9 us  [the longest x2 28.9 us: gathered(): local = lax.ppermute(rows_here, ALL, factor_routes())]
    ppermute x3 -> x4, starting transfers between devices: 11.9 us -> 14 us  [the longest x2 7.86 us: gathered(): local = lax.ppermute(rows_here, ALL, factor_routes())]
    unnamed x32 -> x30, local copies, waits for them, and re-layouts: 7.53 us -> 5.76 us
  transfers between devices with their start and end apart: 11 -> 11, of which waited for: 7 -> 7; matrix products, arithmetic and copies ran while one was open for 8% -> 9% of each run, Pallas kernels for 11% -> 12%
where the time goes in v3:
time: 371 us; the launch traced here: 369 us
  waiting for transfers between devices  129 us (35%)
  blocking collectives  90.3 us (24%)
  Pallas kernels  43.1 us (12%)
  starting transfers between devices  33 us (9%)
  other arithmetic  28.7 us (8%)
  local copies, waits for them, and re-layouts  21.7 us (6%)
  between operations  14.4 us (4%)
  matrix products  9.4 us (3%)
    all_gather x2, waiting for transfers between devices, gathered(): full = lax.all_gather(shard, ROW, axis=0, tiled=True)  62.9 us
    all_to_all x1, blocking collectives, per_device(): lax.all_to_all(chip.reshape(chips, 3 * half // chips, width), CHIPS, spli...  54.6 us
    pallas_call x4, Pallas kernels, half_product(): pl.pallas_call(half_kernel, grid_spec=pltpu.PrefetchScalarGridSpec(num_sc...  43.1 us
    all_to_all x1, blocking collectives, per_device(): lax.all_to_all(jnp.broadcast_to(piece[None], (chips,) + piece.shape), CHI...  35.6 us
    ppermute x2, waiting for transfers between devices, gathered(): local = lax.ppermute(rows_here, ALL, factor_routes())  28.9 us
    all_to_all x2, waiting for transfers between devices, row_sum(): lax.all_to_all(chip, PLANE, split_axis=0, concat_axis=0, tiled=True)  22.8 us
    all_to_all x2, starting transfers between devices, row_sum(): lax.all_to_all(chip, PLANE, split_axis=0, concat_axis=0, tiled=True)  11.6 us
    all_to_all x1, waiting for transfers between devices, to_columns(): lax.all_to_all(own_rows, COL, split_axis=0, concat_axis=0, tiled=True)  10.8 us
  transfers between devices with their start and end apart: 11, of which 7 were waited for; matrix products, arithmetic and copies ran while one was open for 9% of the time, Pallas kernels for 12%

profile of v3, /device:TPU:1, one launch (start us, length us, event | category | flops | bytes accessed | tf_op | source)
XLA Modules:
  0.0 369.4 jit_solution(16135764130735136051)
XLA Ops:
  11.9 43.3 %all-gather.3.cloned.1.call-done.factor_ref = f32[512,1536]{1,0:T(8,128)} async-done(((f32[64,1536]{1,0:T(8,128)}), f32[512,1536]{1,0:T(8,128)}) %all-gather.3.cloned.1.call-update) | async-done | bytes 3145744 | tf_op jit(solution)/shard_map/all_gather | solution.py:122
  57.1 11.2 %shard_map.119.after_ref = f32[8,192,512]{2,1,0:T(8,128)} custom-call(s32[1]{0:T(128)} %bitcast.4.side_ref, f32[8,2,192,1536]{3,2,1,0:T(8,128)} %bitcast.49, f32[512,1536]{1,0:T(8,128)S(1)} %copy-done.4, f32[512,512]{1,0:T(8,128)S(1)} %copy-done), custom_call_target="tpu_custom_call" | custom-call | flops 7247757312 | bytes 15728640 | tf_op jit(solution)/shard_map/pallas_call | solution.py:68
  68.3 3.1 collective-permute-start
  71.4 10.3 %shard_map.120.after_ref = f32[8,192,512]{2,1,0:T(8,128)S(1)} custom-call(s32[1]{0:T(128)} %bitcast.side_ref, f32[8,2,192,1536]{3,2,1,0:T(8,128)} %bitcast.50, f32[512,1536]{1,0:T(8,128)S(1)} %copy-done.4, f32[8,192,512]{2,1,0:T(8,128)} %shard_map.119.after_ref), custom_call_target="tpu_custom_call" | custom-call | flops 7247757312 | bytes 15728640 | tf_op jit(solution)/shard_map/pallas_call | solution.py:68
  81.7 19.5 %all-gather.5.cloned.1.call-done.factor_ref = f32[512,1536]{1,0:T(8,128)} async-done(((f32[64,1536]{1,0:T(8,128)}), f32[512,1536]{1,0:T(8,128)}) %all-gather.5.cloned.1.call-update) | async-done | bytes 3145744 | tf_op jit(solution)/shard_map/all_gather | solution.py:122
  103.2 11.2 %shard_map.121.after_ref = f32[8,192,512]{2,1,0:T(8,128)} custom-call(s32[1]{0:T(128)} %bitcast.4.side_ref, f32[8,2,192,1536]{3,2,1,0:T(8,128)} %bitcast.51, f32[512,1536]{1,0:T(8,128)S(1)} %copy-done.2, f32[8,192,512]{2,1,0:T(8,128)S(1)} %shard_map.120.after_ref), custom_call_target="tpu_custom_call" | custom-call | flops 7247757312 | bytes 15728640 | tf_op jit(solution)/shard_map/pallas_call | solution.py:68
  114.4 3.0 collective-permute-start.1
  117.4 4.3 %add.51 = f32[8,192,512]{2,1,0:T(8,128)} add(f32[8,192,512]{2,1,0:T(8,128)S(1)} %shard_map.120.after_ref, f32[8,192,512]{2,1,0:T(8,128)} %collective-permute-done) | non-fusion elementwise | flops 786432 | bytes 9437184 | tf_op jit(solution)/shard_map/add | solution.py:107
  121.7 6.4 %all-to-all-start = ((f32[8,192,512]{2,1,0:T(8,128)}), f32[8,192,512]{2,1,0:T(8,128)}, u32[]{:S(2)}, u32[]{:S(2)}) async-start(f32[8,192,512]{2,1,0:T(8,128)} %add.51), calls=%async_computation | async-start | bytes 6291456 | tf_op jit(solution)/shard_map/all_to_all | solution.py:108
  128.1 10.3 %shard_map.122 = f32[8,192,512]{2,1,0:T(8,128)S(1)} custom-call(s32[1]{0:T(128)} %bitcast.side_ref, f32[8,2,192,1536]{3,2,1,0:T(8,128)} %bitcast.52, f32[512,1536]{1,0:T(8,128)S(1)} %copy-done.3, f32[8,192,512]{2,1,0:T(8,128)} %shard_map.121.after_ref), custom_call_target="tpu_custom_call" | custom-call | flops 7247757312 | bytes 15728640 | tf_op jit(solution)/shard_map/pallas_call | solution.py:68
  138.5 4.3 %add.52 = f32[8,192,512]{2,1,0:T(8,128)} add(f32[8,192,512]{2,1,0:T(8,128)S(1)} %shard_map.122, f32[8,192,512]{2,1,0:T(8,128)} %collective-permute-done.1) | non-fusion elementwise | flops 786432 | bytes 9437184 | tf_op jit(solution)/shard_map/add | solution.py:107
  142.8 22.8 %all-to-all-done = f32[8,192,512]{2,1,0:T(8,128)} async-done(((f32[8,192,512]{2,1,0:T(8,128)}), f32[8,192,512]{2,1,0:T(8,128)}, u32[]{:S(2)}, u32[]{:S(2)}) %all-to-all-start) | async-done | bytes 3145760 | tf_op jit(solution)/shard_map/all_to_all | solution.py:108
  165.6 5.2 %all-to-all-start.1 = ((f32[8,192,512]{2,1,0:T(8,128)}), f32[8,192,512]{2,1,0:T(8,128)}, u32[]{:S(2)}, u32[]{:S(2)}) async-start(f32[8,192,512]{2,1,0:T(8,128)} %add.52), calls=%async_computation.1 | async-start | bytes 6291456 | tf_op jit(solution)/shard_map/all_to_all | solution.py:108
  170.8 2.1 constant_dynamic-slice_fusion.7
  172.9 6.0 %collective-permute-start.2 = (f32[512,192]{1,0:T(8,128)}, f32[512,192]{1,0:T(8,128)}, u32[]{:S(2)}, u32[]{:S(2)}) collective-permute-start(f32[512,192]{1,0:T(8,128)} %constant_dynamic-slice_fusion.7), channel_id=1, source_target_pairs={{0,0},{16,1},{32,2},{48,3},{64,4},{80,5},{96,6},{112,7},{1,8},{17,... | collective-permute-start | bytes 1179656 | tf_op jit(solution)/shard_map/ppermute | solution.py:124
  181.8 2.3 reduce_sum.27
  184.1 26.9 %collective-permute-done.2 = f32[512,192]{1,0:T(8,128)} collective-permute-done((f32[512,192]{1,0:T(8,128)}, f32[512,192]{1,0:T(8,128)}, u32[]{:S(2)}, u32[]{:S(2)}) %collective-permute-start.2) | collective-permute-done | bytes 393248 | tf_op jit(solution)/shard_map/ppermute | solution.py:124
  220.4 3.0 reduce_sum.28
  226.4 3.4 collective-permute-done.4
  232.8 54.6 %all_to_all.29 = f32[64,12,512]{2,1,0:T(8,128)} all-to-all(f32[64,12,512]{2,1,0:T(8,128)S(1)} %reshape.52), channel_id=1, replica_groups=mesh['xl'=2,'z'=4,'xh'=2,'y'=4,'core'=2] {'xl','z','xh','y'}, dimensions={0} | all-to-all | bytes 3145728 | tf_op jit(solution)/shard_map/all_to_all | solution.py:144
  289.4 35.6 %all_to_all.30 = f32[64,12,512]{2,1,0:T(8,128)S(1)} all-to-all(f32[64,12,512]{2,1,0:T(8,128)S(1)} %broadcast_in_dim.8), channel_id=1, replica_groups=mesh['xl'=2,'z'=4,'xh'=2,'y'=4,'core'=2] {'xl','z','xh','y'}, dimensions={0} | all-to-all | bytes 3145728 | tf_op jit(solution)/shard_map/all_to_all | solution.py:146
  331.0 5.2 %all-to-all-start.2 = ((f32[16,32,384]{2,1,0:T(8,128)}), f32[16,32,384]{2,1,0:T(8,128)}, u32[]{:S(2)}, u32[]{:S(2)}) async-start(f32[16,32,384]{2,1,0:T(8,128)} %bitcast.9), calls=%async_computation.2 | async-start | bytes 1572864 | tf_op jit(solution)/shard_map/all_to_all | solution.py:113
  339.4 10.8 %all-to-all-done.2 = f32[16,32,384]{2,1,0:T(8,128)} async-done(((f32[16,32,384]{2,1,0:T(8,128)}), f32[16,32,384]{2,1,0:T(8,128)}, u32[]{:S(2)}, u32[]{:S(2)}) %all-to-all-start.2) | async-done | bytes 786464 | tf_op jit(solution)/shard_map/all_to_all | solution.py:113
  356.3 2.2 broadcast_select_fusion.1
  (81 shorter events, 47.7 us)
Async XLA Ops:
  7.2 48.1 %copy-start = (f32[512,512]{1,0:T(8,128)S(1)}, f32[512,512]{1,0:T(8,128)}, u32[]{:S(2)}) copy-start(f32[512,512]{1,0:T(8,128)} %after_ref.1) | copy-start | bytes 3145732
  7.2 48.0 %all-gather.3.cloned.1.call-start = ((), (), s32[]{:S(2)}) async-start(), calls=%async_computation.5 | async-start | bytes 3538944 | tf_op jit(solution)/shard_map/all_gather | solution.py:122
  10.0 91.3 %all-gather.5.cloned.1.call-start = ((), (), s32[]{:S(2)}) async-start(), calls=%async_computation.6 | async-start | bytes 3538944 | tf_op jit(solution)/shard_map/all_gather | solution.py:122
  55.2 1.9 copy-start.4
  68.3 49.1 %collective-permute-start = (f32[8,192,512]{2,1,0:T(8,128)}, f32[8,192,512]{2,1,0:T(8,128)}, u32[]{:S(2)}, u32[]{:S(2)}) collective-permute-start(f32[8,192,512]{2,1,0:T(8,128)} %shard_map.119.after_ref), channel_id=1, source_target_pairs={{0,1},{1,0},{2,3},{3,2},{4,5},{5,4},{6,7},{7,6},{8,9},{9,8},{10,11... | collective-permute-start | bytes 9437192 | tf_op jit(solution)/shard_map/ppermute | solution.py:105
  101.3 1.9 copy-start.2
  114.4 24.1 %collective-permute-start.1 = (f32[8,192,512]{2,1,0:T(8,128)}, f32[8,192,512]{2,1,0:T(8,128)}, u32[]{:S(2)}, u32[]{:S(2)}) collective-permute-start(f32[8,192,512]{2,1,0:T(8,128)} %shard_map.121.after_ref), channel_id=1, source_target_pairs={{0,1},{1,0},{2,3},{3,2},{4,5},{5,4},{6,7},{7,6},{8,9},{9,8},{10,11... | collective-permute-start | bytes 9437192 | tf_op jit(solution)/shard_map/ppermute | solution.py:105
  121.7 6.4 %copy-start.3 = (f32[512,1536]{1,0:T(8,128)S(1)}, f32[512,1536]{1,0:T(8,128)}, u32[]{:S(2)}) copy-start(f32[512,1536]{1,0:T(8,128)} %all-gather.5.cloned.1.call-done.factor_ref) | copy-start | bytes 9437188
  121.7 43.9 %all-to-all-start = ((f32[8,192,512]{2,1,0:T(8,128)}), f32[8,192,512]{2,1,0:T(8,128)}, u32[]{:S(2)}, u32[]{:S(2)}) async-start(f32[8,192,512]{2,1,0:T(8,128)} %add.51), calls=%async_computation | async-start | bytes 6291456 | tf_op jit(solution)/shard_map/all_to_all | solution.py:108
  165.6 54.7 %all-to-all-start.1 = ((f32[8,192,512]{2,1,0:T(8,128)}), f32[8,192,512]{2,1,0:T(8,128)}, u32[]{:S(2)}, u32[]{:S(2)}) async-start(f32[8,192,512]{2,1,0:T(8,128)} %add.52), calls=%async_computation.1 | async-start | bytes 6291456 | tf_op jit(solution)/shard_map/all_to_all | solution.py:108
  172.9 38.1 %collective-permute-start.2 = (f32[512,192]{1,0:T(8,128)}, f32[512,192]{1,0:T(8,128)}, u32[]{:S(2)}, u32[]{:S(2)}) collective-permute-start(f32[512,192]{1,0:T(8,128)} %constant_dynamic-slice_fusion.7), channel_id=1, source_target_pairs={{0,0},{16,1},{32,2},{48,3},{64,4},{80,5},{96,6},{112,7},{1,8},{17,... | collective-permute-start | bytes 1179656 | tf_op jit(solution)/shard_map/ppermute | solution.py:124
  179.9 36.7 %collective-permute-start.3 = (f32[512,192]{1,0:T(8,128)}, f32[512,192]{1,0:T(8,128)S(1)}, u32[]{:S(2)}, u32[]{:S(2)}) collective-permute-start(f32[512,192]{1,0:T(8,128)} %constant_dynamic-slice_fusion.5), channel_id=1, source_target_pairs={{0,0},{16,1},{32,2},{48,3},{64,4},{80,5},{96,6},{112,7},{1,8},{17,... | collective-permute-start | bytes 1179656 | tf_op jit(solution)/shard_map/ppermute | solution.py:124
  184.1 29.6 %copy-start.1 = (f32[512,512]{1,0:T(8,128)S(1)}, f32[512,512]{1,0:T(8,128)}, u32[]{:S(2)}) copy-start(f32[512,512]{1,0:T(8,128)} %after_ref.1) | copy-start | bytes 3145732
  219.3 4.1 %copy-start.7 = (f32[192,512]{1,0:T(8,128)}, f32[192,512]{1,0:T(8,128)S(1)}, u32[]{:S(2)}) copy-start(f32[192,512]{1,0:T(8,128)S(1)} %fusion.4) | copy-start | bytes 1179652
  225.0 1.2 copy-start.13
  226.2 3.6 copy-start.9
  226.2 3.6 copy-start.10
  226.3 3.5 collective-permute-start.4
  326.4 29.8 %collective-permute-start.5 = (f32[768,512]{1,0:T(8,128)}, f32[768,512]{1,0:T(8,128)}, u32[]{:S(2)}, u32[]{:S(2)}) collective-permute-start(f32[768,512]{1,0:T(8,128)} %reshape.53), channel_id=1, source_target_pairs={{0,1},{1,0},{2,3},{3,2},{4,5},{5,4},{6,7},{7,6},{8,9},{9,8},{10,11... | collective-permute-start | bytes 4718600 | tf_op jit(solution)/shard_map/ppermute | solution.py:148
  329.8 6.4 %copy-start.5 = (f32[512,512]{1,0:T(8,128)S(1)}, f32[512,512]{1,0:T(8,128)}, u32[]{:S(2)}) copy-start(f32[512,512]{1,0:T(8,128)} %param.12) | copy-start | bytes 3145732
  331.0 19.3 %all-to-all-start.2 = ((f32[16,32,384]{2,1,0:T(8,128)}), f32[16,32,384]{2,1,0:T(8,128)}, u32[]{:S(2)}, u32[]{:S(2)}) async-start(f32[16,32,384]{2,1,0:T(8,128)} %bitcast.9), calls=%async_computation.2 | async-start | bytes 1572864 | tf_op jit(solution)/shard_map/all_to_all | solution.py:113
  336.2 1.2 copy-start.14
  353.7 1.3 copy-start.11
  358.8 1.4 copy-start.6
  (2 other events, 2.0 us)
Sparse Core Ops, SparseCore 0:
  10.2 44.9 all-gather.2
  57.4 43.7 all-gather.4

commit v4 on v3

--- a/solution.py
+++ b/solution.py
@@ -14,7 +14,6 @@
 ALL = ROW + COL
 SIZES = (2, 4, 2, 4, 2)
 SWAP = ((0, 1), (1, 0))
-TILES = 2
 
 
 def product(left, right, contract=((1,), (0,))):
@@ -33,7 +32,7 @@
             for xh in range(2):
                 for y in range(4):
                     for core in range(2):
-                        source = linear(y // 2, (y % 2) * 2 + core, xl, z, xh)
+                        source = linear(xh, (y - z) % 4, xl, z, core)
                         routes.append((source, linear(xl, z, xh, y, core)))
     return routes
 
@@ -43,8 +42,33 @@
     return high, (value - high.astype(jnp.float32)).astype(jnp.bfloat16)
 
 
-def half_kernel(side_ref, a_ref, factor_ref, after_ref, out_ref, high_ref, low_ref):
-    del side_ref, after_ref
+def multiply(a_ref, high_ref, low_ref, out_ref):
+    a_high, a_low = split(a_ref[...])
+    dims = (((1,), (1,)), ((), ()))
+    dot = lambda l, r: lax.dot_general(l, r, dims, preferred_element_type=jnp.float32)
+    out_ref[...] = dot(a_high, high_ref[...]) + dot(a_high, low_ref[...]) + dot(a_low, high_ref[...])
+
+
+def first_kernel(place_ref, a_ref, *refs):
+    pieces, (after_ref, out_ref, factor_ref, high_ref, low_ref) = refs[:8], refs[8:]
+    del after_ref
+
+    @pl.when(pl.program_id(0) == 0)
+    def _():
+        for index, piece_ref in enumerate(pieces):
+            size = piece_ref.shape[0]
+            span = pl.ds(pl.multiple_of(place_ref[1 + index] * size, size), size)
+            value = piece_ref[...]
+            high, low = split(value)
+            factor_ref[span, :] = value
+            high_ref[span, :] = high
+            low_ref[span, :] = low
+
+    multiply(a_ref, high_ref, low_ref, out_ref)
+
+
+def second_kernel(place_ref, a_ref, factor_ref, after_ref, out_ref, high_ref, low_ref):
+    del place_ref, after_ref
 
     @pl.when(pl.program_id(0) == 0)
     def _():
@@ -52,42 +76,44 @@
         high_ref[...] = high
         low_ref[...] = low
 
-    tiles, part, depth = a_ref.shape
-    a_high, a_low = split(a_ref[...].reshape(tiles * part, depth))
-    dims = (((1,), (1,)), ((), ()))
-    dot = lambda l, r: lax.dot_general(l, r, dims, preferred_element_type=jnp.float32)
-    total = dot(a_high, high_ref[...]) + dot(a_high, low_ref[...]) + dot(a_low, high_ref[...])
-    out_ref[...] = total.reshape(out_ref.shape)
-
-
-def half_product(ancestor, factor_t, side, after):
+    multiply(a_ref, high_ref, low_ref, out_ref)
+
+
+def half_product(ancestor, factors, places, after):
     rows, depth = ancestor.shape
-    width = factor_t.shape[0]
-    part = rows // 16
-    view = ancestor.reshape(8, 2, part, depth)
-    return pl.pallas_call(
-        half_kernel,
+    width = sum(f.shape[0] for f in factors)
+    tile = rows // 8
+    whole = pl.BlockSpec((width, depth), lambda i, places: (0, 0), pipeline_mode=pl.Buffered(1))
+    piece = pl.BlockSpec((width // 8, depth), lambda i, places: (0, 0), pipeline_mode=pl.Buffered(1))
+    first = len(factors) == 8
+    out_shape = [jax.ShapeDtypeStruct((rows // 2, width), jnp.float32)]
+    out_specs = [pl.BlockSpec((tile, width), lambda i, places: (i, 0))]
+    if first:
+        out_shape.append(jax.ShapeDtypeStruct((width, depth), jnp.float32))
+        out_specs.append(whole)
+    result = pl.pallas_call(
+        first_kernel if first else second_kernel,
         grid_spec=pltpu.PrefetchScalarGridSpec(
             num_scalar_prefetch=1,
-            grid=(8 // TILES,),
+            grid=(4,),
             in_specs=[
-                pl.BlockSpec((TILES, None, part, depth), lambda i, side: (i, side[0], 0, 0)),
-                pl.BlockSpec((width, depth), lambda i, side: (0, 0), pipeline_mode=pl.Buffered(1)),
+                pl.BlockSpec((tile, depth), lambda i, places: (places[0] * 4 + i, 0)),
+                *([piece] * 8 if first else [whole]),
                 pl.BlockSpec(memory_space=pl.ANY),
             ],
-            out_specs=pl.BlockSpec((TILES, part, width), lambda i, side: (i, 0, 0)),
+            out_specs=out_specs,
             scratch_shapes=[pltpu.VMEM((width, depth), jnp.bfloat16)] * 2,
         ),
-        out_shape=jax.ShapeDtypeStruct((8, part, width), jnp.float32),
+        out_shape=out_shape,
         cost_estimate=pl.CostEstimate(
             flops=3 * rows * depth * width, transcendentals=0,
             bytes_accessed=2 * rows * depth + 4 * width * depth + 2 * rows * width),
         compiler_params=pltpu.CompilerParams(vmem_limit_bytes=40 * 1024 * 1024),
-    )(side.reshape(1), view, factor_t, after)
+    )(places, ancestor, *factors, after)
+    return result if first else result[0]
 
 
 def per_device(ancestor, lhat_one, lhat_two, link_two, diag_one, diag_two, mask_one, mask_two):
-    row_index = lax.axis_index(ROW)
     column_index = lax.axis_index(COL)
     core = lax.axis_index("core")
     rows, depth = ancestor.shape
@@ -96,38 +122,57 @@
     part = rows // 16
     half = width // 2
 
+    xl, z = lax.axis_index("xl"), lax.axis_index("z")
+    up = [(i, (i + 1) % 4) for i in range(4)]
+    down = [(i, (i - 1) % 4) for i in range(4)]
+    here = [xl * 4 + (z + step) % 4 for step in range(4)]
+    there = [(1 - xl) * 4 + (z + step) % 4 for step in range(4)]
+    places = [here[0], there[0], here[3], here[1], there[3], there[1], here[2], there[2]]
+    places = {side: jnp.stack([chosen] + places).astype(jnp.int32)
+              for side, chosen in (("own", core), ("other", 1 - core))}
+    sub = xl * 4 + (z + lax.axis_index("y")) % 4
+
     def masked(shard, mask):
         own = lax.dynamic_slice_in_dim(mask, column_index * blocks, blocks).astype(jnp.float32)
         return shard.T * jnp.broadcast_to(own[:, None], (blocks, BLOCK)).reshape(1, depth)
 
-    def row_sum(factor_t, after):
-        send = half_product(ancestor, factor_t, 1 - core, after)
+    def gathered(piece):
+        below = lax.ppermute(piece, "z", up)
+        above = lax.ppermute(piece, "z", down)
+        side = lax.ppermute(piece, "xl", SWAP)
+        side_below = lax.ppermute(side, "z", up)
+        side_above = lax.ppermute(side, "z", down)
+        far = lax.ppermute(below, "z", up)
+        side_far = lax.ppermute(side_above, "z", down)
+        return [piece, side, below, above, side_below, side_above, far, side_far]
+
+    def row_sum(pieces, after):
+        send, factor_t = half_product(ancestor, pieces, places["other"], after)
         received = lax.ppermute(send, "core", SWAP)
-        keep = half_product(ancestor, factor_t, core, send)
-        chip = keep + received
+        local = lax.dynamic_slice_in_dim(factor_t, sub * part, part, 1)
+        local = lax.ppermute(local, ALL, factor_routes())
+        keep = half_product(ancestor, [factor_t], places["own"], send)
+        chip = (keep + received).reshape(8, part, width)
         pieces = lax.all_to_all(chip, PLANE, split_axis=0, concat_axis=0, tiled=True)
-        return pieces.sum(0), keep
+        return pieces.sum(0), local, send
 
     def to_columns(own_rows):
         own_rows = jnp.concatenate([value.T for value in own_rows], axis=1)
         pieces = lax.all_to_all(own_rows, COL, split_axis=0, concat_axis=0, tiled=True)
-        pieces = pieces.reshape(16, width // 16, 2, part).transpose(2, 0, 3, 1)
-        return pieces.reshape(2, rows, width // 16)
+        pieces = pieces.reshape(8, 2, width // 16, 2 * part)
+        return [pieces[..., i * part:(i + 1) * part].transpose(2, 1, 0, 3).reshape(width // 16, rows).T
+                for i in range(2)]
 
     def half_of(value, side):
         return lax.dynamic_slice_in_dim(value, side * half, half, 0)
 
-    def gathered(shard, mask):
-        shard = masked(shard, mask)
-        full = lax.all_gather(shard, ROW, axis=0, tiled=True)
-        rows_here = lax.dynamic_slice_in_dim(full, row_index * part, part, 1)
-        local = lax.ppermute(rows_here, ALL, factor_routes())
-        return full, local
-
-    factor_one, local_one = gathered(lhat_one, mask_one)
-    factor_two, local_two = gathered(lhat_two, mask_two)
-    sum_one, done_one = row_sum(factor_one, link_two)
-    sum_two, _ = row_sum(factor_two, done_one)
+    piece_one = masked(lhat_one, mask_one)
+    piece_two = masked(lhat_two, mask_two)
+    pieces_one = gathered(piece_one)
+    piece_two, *pieces_one = lax.optimization_barrier((piece_two, *pieces_one))
+    pieces_two = gathered(piece_two)
+    sum_one, local_one, done_one = row_sum(pieces_one, link_two)
+    sum_two, local_two, _ = row_sum(pieces_two, done_one)
     one_part = product(local_one, sum_one)
     link_part = product(sum_one, local_two, ((0,), (1,))) - product(one_part, link_two)
     moved_one = product(sum_one, link_two)

time: 371 us -> 362 us (0.976)
  waiting for transfers between devices: 129 us -> 110 us
  starting transfers between devices: 33 us -> 48.7 us
  between operations: 14.4 us -> 0.98 us
  blocking collectives: 90.3 us -> 99.1 us
    all_gather x2 -> x0, waiting for transfers between devices: 62.9 us -> none  [gathered(): full = lax.all_gather(shard, ROW, axis=0, tiled=True)]
    ppermute x2 -> x16, waiting for transfers between devices: 28.9 us -> 53.1 us  [the longest x2 16 us: gathered(): side = lax.ppermute(piece, 'xl', SWAP)]
    all_to_all x2, waiting for transfers between devices: 22.8 us -> 44.5 us  [row_sum(): lax.all_to_all(chip, PLANE, split_axis=0, concat_axis=0, tiled=True)]
    ppermute x2 -> x16, starting transfers between devices: 7.86 us -> 24.2 us  [the longest x2 7.54 us: gathered(): side_above = lax.ppermute(side, 'z', down)]
    all_to_all x1, blocking collectives: 54.6 us -> 63.5 us  [per_device(): lax.all_to_all(chip.reshape(chips, 3 * half // chips, width), CHIPS, spli...]
    another operation x5 -> x2, local copies, waits for them, and re-layouts: 4.14 us -> 0.17 us  [per_device(): jnp.stack([chosen] + places).astype(jnp.int32)]
    unnamed x30 -> x28, local copies, waits for them, and re-layouts: 5.76 us -> 7.7 us
  transfers between devices with their start and end apart: 11 -> 23, of which waited for: 7 -> 14; matrix products, arithmetic and copies ran while one was open for 9% -> 9% of each run, Pallas kernels for 12% -> 9%
where the time goes in v4:
time: 362 us; the launch traced here: 361 us
  waiting for transfers between devices  110 us (30%)
  blocking collectives  99.1 us (27%)
  starting transfers between devices  48.7 us (13%)
  Pallas kernels  46 us (13%)
  other arithmetic  26.5 us (7%)
  local copies, waits for them, and re-layouts  20 us (6%)
  matrix products  9.69 us (3%)
    all_to_all x1, blocking collectives, per_device(): lax.all_to_all(chip.reshape(chips, 3 * half // chips, width), CHIPS, spli...  63.5 us
    pallas_call x4, Pallas kernels, half_product(): pl.pallas_call(first_kernel if first else second_kernel, grid_spec=pltpu....  46 us
    all_to_all x2, waiting for transfers between devices, row_sum(): lax.all_to_all(chip, PLANE, split_axis=0, concat_axis=0, tiled=True)  44.5 us
    all_to_all x1, blocking collectives, per_device(): lax.all_to_all(jnp.broadcast_to(piece[None], (chips,) + piece.shape), CHI...  35.6 us
    ppermute x2, waiting for transfers between devices, gathered(): side = lax.ppermute(piece, 'xl', SWAP)  16 us
    all_to_all x2, starting transfers between devices, row_sum(): lax.all_to_all(chip, PLANE, split_axis=0, concat_axis=0, tiled=True)  11.9 us
    ppermute x2, waiting for transfers between devices, gathered(): side_above = lax.ppermute(side, 'z', down)  11.3 us
    ppermute x2, waiting for transfers between devices, gathered(): side_far = lax.ppermute(side_above, 'z', down)  10.5 us
  transfers between devices with their start and end apart: 23, of which 14 were waited for; matrix products, arithmetic and copies ran while one was open for 9% of the time, Pallas kernels for 9%

profile of v4, /device:TPU:1, one launch (start us, length us, event | category | flops | bytes accessed | tf_op | source)
XLA Modules:
  0.0 361.2 jit_solution(5750129945364433274)
XLA Ops:
  6.4 6.8 %collective-permute-done.refs_1_ = f32[64,1536]{1,0:T(8,128)S(1)} collective-permute-done((f32[64,1536]{1,0:T(8,128)S(1)}, f32[64,1536]{1,0:T(8,128)S(1)}, u32[]{:S(2)}, u32[]{:S(2)}) %collective-permute-start) | collective-permute-done | bytes 393248 | tf_op jit(solution)/shard_map/ppermute | solution.py:142
  13.1 4.1 %collective-permute-start.4 = (f32[64,1536]{1,0:T(8,128)S(1)}, f32[64,1536]{1,0:T(8,128)S(1)}, u32[]{:S(2)}, u32[]{:S(2)}) collective-permute-start(f32[64,1536]{1,0:T(8,128)S(1)} %collective-permute-done.refs_1_), channel_id=1, source_target_pairs={{0,48},{16,0},{32,16},{48,32},{1,49},{17,1},{33,17},{49,33},{2,50}... | collective-permute-start | bytes 1179656 | tf_op jit(solution)/shard_map/ppermute | solution.py:144
  19.0 5.2 %collective-permute-done.4.refs_5_ = f32[64,1536]{1,0:T(8,128)S(1)} collective-permute-done((f32[64,1536]{1,0:T(8,128)S(1)}, f32[64,1536]{1,0:T(8,128)S(1)}, u32[]{:S(2)}, u32[]{:S(2)}) %collective-permute-start.4) | collective-permute-done | bytes 393248 | tf_op jit(solution)/shard_map/ppermute | solution.py:144
  24.2 3.4 collective-permute-start.6
  28.7 4.0 %collective-permute-done.2.refs_3_ = f32[64,1536]{1,0:T(8,128)S(1)} collective-permute-done((f32[64,1536]{1,0:T(8,128)S(1)}, f32[64,1536]{1,0:T(8,128)S(1)}, u32[]{:S(2)}, u32[]{:S(2)}) %collective-permute-start.2) | collective-permute-done | bytes 393248 | tf_op jit(solution)/shard_map/ppermute | solution.py:141
  35.8 5.3 %collective-permute-done.6.refs_7_ = f32[64,1536]{1,0:T(8,128)S(1)} collective-permute-done((f32[64,1536]{1,0:T(8,128)S(1)}, f32[64,1536]{1,0:T(8,128)S(1)}, u32[]{:S(2)}, u32[]{:S(2)}) %collective-permute-start.6) | collective-permute-done | bytes 393248 | tf_op jit(solution)/shard_map/ppermute | solution.py:146
  41.1 12.0 %shard_map.119 = (f32[1536,512]{1,0:T(8,128)}, f32[512,1536]{1,0:T(8,128)S(1)}) custom-call(s32[9]{0:T(128)S(1)} %stack.55.place_ref, f32[3072,1536]{1,0:T(8,128)} %a_ref.7, f32[64,1536]{1,0:T(8,128)S(1)} %multiply_bitcast_fusion.refs_0_, f32[64,1536]{1,0:T(8,128)S(1)} %collective-permute-done.refs_1_, f32[64,1536]{1,0:T(8,128)S(1)} %collective-permute-done.1.refs_2_, ...), custom_call_target="tpu_custom_call" | custom-call | flops 7247757312 | bytes 15728640 | tf_op jit(solution)/shard_map/pallas_call | solution.py:94
  58.6 9.2 %collective-permute-done.8.refs_1_ = f32[64,1536]{1,0:T(8,128)S(1)} collective-permute-done((f32[64,1536]{1,0:T(8,128)S(1)}, f32[64,1536]{1,0:T(8,128)S(1)}, u32[]{:S(2)}, u32[]{:S(2)}) %collective-permute-start.8) | collective-permute-done | bytes 393248 | tf_op jit(solution)/shard_map/ppermute | solution.py:142
  72.6 6.1 %collective-permute-done.12.refs_5_ = f32[64,1536]{1,0:T(8,128)S(1)} collective-permute-done((f32[64,1536]{1,0:T(8,128)S(1)}, f32[64,1536]{1,0:T(8,128)S(1)}, u32[]{:S(2)}, u32[]{:S(2)}) %collective-permute-start.12) | collective-permute-done | bytes 393248 | tf_op jit(solution)/shard_map/ppermute | solution.py:144
  82.3 4.9 %collective-permute-done.10.refs_3_ = f32[64,1536]{1,0:T(8,128)S(1)} collective-permute-done((f32[64,1536]{1,0:T(8,128)S(1)}, f32[64,1536]{1,0:T(8,128)S(1)}, u32[]{:S(2)}, u32[]{:S(2)}) %collective-permute-start.10) | collective-permute-done | bytes 393248 | tf_op jit(solution)/shard_map/ppermute | solution.py:141
  90.4 5.2 %collective-permute-done.14.refs_7_ = f32[64,1536]{1,0:T(8,128)} collective-permute-done((f32[64,1536]{1,0:T(8,128)S(1)}, f32[64,1536]{1,0:T(8,128)}, u32[]{:S(2)}, u32[]{:S(2)}) %collective-permute-start.14) | collective-permute-done | bytes 393248 | tf_op jit(solution)/shard_map/ppermute | solution.py:146
  95.6 12.3 %shard_map.121 = (f32[1536,512]{1,0:T(8,128)}, f32[512,1536]{1,0:T(8,128)S(1)}) custom-call(s32[9]{0:T(128)S(1)} %stack.55.place_ref, f32[3072,1536]{1,0:T(8,128)} %a_ref.7, f32[64,1536]{1,0:T(8,128)S(1)} %multiply_bitcast_fusion.1.refs_0_, f32[64,1536]{1,0:T(8,128)S(1)} %collective-permute-done.8.refs_1_, f32[64,1536]{1,0:T(8,128)S(1)} %collective-permute-done.9.refs_2_, ...), custom_call_target="tpu_custom_call" | custom-call | flops 7247757312 | bytes 15728640 | tf_op jit(solution)/shard_map/pallas_call | solution.py:94
  111.3 10.9 %shard_map.120 = f32[1536,512]{1,0:T(8,128)S(1)} custom-call(s32[9]{0:T(128)S(1)} %stack.53.place_ref, f32[3072,1536]{1,0:T(8,128)} %a_ref.7, f32[512,1536]{1,0:T(8,128)S(1)} %copy-done.2, f32[1536,512]{1,0:T(8,128)} %get-tuple-element.29.after_ref.refs_8_), custom_call_target="tpu_custom_call" | custom-call | flops 7247757312 | bytes 15728640 | tf_op jit(solution)/shard_map/pallas_call | solution.py:94
  122.2 4.3 %add.125 = f32[1536,512]{1,0:T(8,128)} add(f32[1536,512]{1,0:T(8,128)S(1)} %shard_map.120, f32[1536,512]{1,0:T(8,128)} %collective-permute-done.7) | non-fusion elementwise | flops 786432 | bytes 9437184 | tf_op jit(solution)/shard_map/add | solution.py:155
  126.5 6.7 %all-to-all-start = ((f32[8,192,512]{2,1,0:T(8,128)}), f32[8,192,512]{2,1,0:T(8,128)}, u32[]{:S(2)}, u32[]{:S(2)}) async-start(f32[8,192,512]{2,1,0:T(8,128)} %bitcast.61), calls=%async_computation | async-start | bytes 6291456 | tf_op jit(solution)/shard_map/all_to_all | solution.py:156
  135.1 10.9 %shard_map.122 = f32[1536,512]{1,0:T(8,128)S(1)} custom-call(s32[9]{0:T(128)S(1)} %stack.53.place_ref, f32[3072,1536]{1,0:T(8,128)} %a_ref.7, f32[512,1536]{1,0:T(8,128)S(1)} %copy-done.4, f32[1536,512]{1,0:T(8,128)} %get-tuple-element.32.after_ref), custom_call_target="tpu_custom_call" | custom-call | flops 7247757312 | bytes 15728640 | tf_op jit(solution)/shard_map/pallas_call | solution.py:94
  146.0 4.3 %add.126 = f32[1536,512]{1,0:T(8,128)} add(f32[1536,512]{1,0:T(8,128)S(1)} %shard_map.122, f32[1536,512]{1,0:T(8,128)} %collective-permute-done.15) | non-fusion elementwise | flops 786432 | bytes 9437184 | tf_op jit(solution)/shard_map/add | solution.py:155
  150.3 20.4 %all-to-all-done = f32[8,192,512]{2,1,0:T(8,128)} async-done(((f32[8,192,512]{2,1,0:T(8,128)}), f32[8,192,512]{2,1,0:T(8,128)}, u32[]{:S(2)}, u32[]{:S(2)}) %all-to-all-start) | async-done | bytes 3145760 | tf_op jit(solution)/shard_map/all_to_all | solution.py:156
  170.7 5.2 %all-to-all-start.1 = ((f32[8,192,512]{2,1,0:T(8,128)}), f32[8,192,512]{2,1,0:T(8,128)}, u32[]{:S(2)}, u32[]{:S(2)}) async-start(f32[8,192,512]{2,1,0:T(8,128)} %bitcast.60), calls=%async_computation.1 | async-start | bytes 6291456 | tf_op jit(solution)/shard_map/all_to_all | solution.py:156
  189.4 24.0 %all-to-all-done.1 = f32[8,192,512]{2,1,0:T(8,128)} async-done(((f32[8,192,512]{2,1,0:T(8,128)}), f32[8,192,512]{2,1,0:T(8,128)}, u32[]{:S(2)}, u32[]{:S(2)}) %all-to-all-start.1) | async-done | bytes 3145760 | tf_op jit(solution)/shard_map/all_to_all | solution.py:156
  224.9 63.5 %all_to_all.29 = f32[64,12,512]{2,1,0:T(8,128)} all-to-all(f32[64,12,512]{2,1,0:T(8,128)S(1)} %reshape.45), channel_id=1, replica_groups=mesh['xl'=2,'z'=4,'xh'=2,'y'=4,'core'=2] {'xl','z','xh','y'}, dimensions={0} | all-to-all | bytes 3145728 | tf_op jit(solution)/shard_map/all_to_all | solution.py:189
  290.4 35.6 %all_to_all.30 = f32[64,12,512]{2,1,0:T(8,128)S(1)} all-to-all(f32[64,12,512]{2,1,0:T(8,128)S(1)} %broadcast_in_dim.8), channel_id=1, replica_groups=mesh['xl'=2,'z'=4,'xh'=2,'y'=4,'core'=2] {'xl','z','xh','y'}, dimensions={0} | all-to-all | bytes 3145728 | tf_op jit(solution)/shard_map/all_to_all | solution.py:191
  331.9 5.1 %all-to-all-start.2 = ((f32[16,32,384]{2,1,0:T(8,128)}), f32[16,32,384]{2,1,0:T(8,128)S(1)}, u32[]{:S(2)}, u32[]{:S(2)}) async-start(f32[16,32,384]{2,1,0:T(8,128)} %bitcast.18), calls=%async_computation.2 | async-start | bytes 1572864 | tf_op jit(solution)/shard_map/all_to_all | solution.py:161
  341.4 9.6 %all-to-all-done.2 = f32[16,32,384]{2,1,0:T(8,128)S(1)} async-done(((f32[16,32,384]{2,1,0:T(8,128)}), f32[16,32,384]{2,1,0:T(8,128)S(1)}, u32[]{:S(2)}, u32[]{:S(2)}) %all-to-all-start.2) | async-done | bytes 786464 | tf_op jit(solution)/shard_map/all_to_all | solution.py:161
  (102 shorter events, 81.1 us)
Async XLA Ops:
  0.6 40.4 %copy-start = (f32[512,512]{1,0:T(8,128)S(1)}, f32[512,512]{1,0:T(8,128)}, u32[]{:S(2)}) copy-start(f32[512,512]{1,0:T(8,128)} %refs_8_.1) | copy-start | bytes 3145732
  2.6 10.5 %collective-permute-start = (f32[64,1536]{1,0:T(8,128)S(1)}, f32[64,1536]{1,0:T(8,128)S(1)}, u32[]{:S(2)}, u32[]{:S(2)}) collective-permute-start(f32[64,1536]{1,0:T(8,128)S(1)} %multiply_bitcast_fusion.refs_0_), channel_id=1, source_target_pairs={{0,64},{64,0},{1,65},{65,1},{2,66},{66,2},{3,67},{67,3},{4,68},{68... | collective-permute-start | bytes 1179656 | tf_op jit(solution)/shard_map/ppermute | solution.py:142
  4.7 14.2 %collective-permute-start.1 = (f32[64,1536]{1,0:T(8,128)S(1)}, f32[64,1536]{1,0:T(8,128)S(1)}, u32[]{:S(2)}, u32[]{:S(2)}) collective-permute-start(f32[64,1536]{1,0:T(8,128)S(1)} %multiply_bitcast_fusion.refs_0_), channel_id=1, source_target_pairs={{0,16},{16,32},{32,48},{48,0},{1,17},{17,33},{33,49},{49,1},{2,18}... | collective-permute-start | bytes 1179656 | tf_op jit(solution)/shard_map/ppermute | solution.py:140
  13.1 11.1 %collective-permute-start.4 = (f32[64,1536]{1,0:T(8,128)S(1)}, f32[64,1536]{1,0:T(8,128)S(1)}, u32[]{:S(2)}, u32[]{:S(2)}) collective-permute-start(f32[64,1536]{1,0:T(8,128)S(1)} %collective-permute-done.refs_1_), channel_id=1, source_target_pairs={{0,48},{16,0},{32,16},{48,32},{1,49},{17,1},{33,17},{49,33},{2,50}... | collective-permute-start | bytes 1179656 | tf_op jit(solution)/shard_map/ppermute | solution.py:144
  17.3 15.4 %collective-permute-start.2 = (f32[64,1536]{1,0:T(8,128)S(1)}, f32[64,1536]{1,0:T(8,128)S(1)}, u32[]{:S(2)}, u32[]{:S(2)}) collective-permute-start(f32[64,1536]{1,0:T(8,128)S(1)} %multiply_bitcast_fusion.refs_0_), channel_id=1, source_target_pairs={{0,48},{16,0},{32,16},{48,32},{1,49},{17,1},{33,17},{49,33},{2,50}... | collective-permute-start | bytes 1179656 | tf_op jit(solution)/shard_map/ppermute | solution.py:141
  17.5 15.1 %collective-permute-start.3 = (f32[64,1536]{1,0:T(8,128)S(1)}, f32[64,1536]{1,0:T(8,128)S(1)}, u32[]{:S(2)}, u32[]{:S(2)}) collective-permute-start(f32[64,1536]{1,0:T(8,128)S(1)} %collective-permute-done.refs_1_), channel_id=1, source_target_pairs={{0,16},{16,32},{32,48},{48,0},{1,17},{17,33},{33,49},{49,1},{2,18}... | collective-permute-start | bytes 1179656 | tf_op jit(solution)/shard_map/ppermute | solution.py:143
  18.9 16.9 %collective-permute-start.5 = (f32[64,1536]{1,0:T(8,128)S(1)}, f32[64,1536]{1,0:T(8,128)S(1)}, u32[]{:S(2)}, u32[]{:S(2)}) collective-permute-start(f32[64,1536]{1,0:T(8,128)S(1)} %collective-permute-done.1.refs_2_), channel_id=1, source_target_pairs={{0,16},{16,32},{32,48},{48,0},{1,17},{17,33},{33,49},{49,1},{2,18}... | collective-permute-start | bytes 1179656 | tf_op jit(solution)/shard_map/ppermute | solution.py:145
  24.2 16.9 %collective-permute-start.6 = (f32[64,1536]{1,0:T(8,128)S(1)}, f32[64,1536]{1,0:T(8,128)S(1)}, u32[]{:S(2)}, u32[]{:S(2)}) collective-permute-start(f32[64,1536]{1,0:T(8,128)S(1)} %collective-permute-done.4.refs_5_), channel_id=1, source_target_pairs={{0,48},{16,0},{32,16},{48,32},{1,49},{17,1},{33,17},{49,33},{2,50}... | collective-permute-start | bytes 1179656 | tf_op jit(solution)/shard_map/ppermute | solution.py:146
  54.7 67.5 %collective-permute-start.7 = (f32[1536,512]{1,0:T(8,128)}, f32[1536,512]{1,0:T(8,128)}, u32[]{:S(2)}, u32[]{:S(2)}) collective-permute-start(f32[1536,512]{1,0:T(8,128)} %get-tuple-element.29.after_ref.refs_8_), channel_id=1, source_target_pairs={{0,1},{1,0},{2,3},{3,2},{4,5},{5,4},{6,7},{7,6},{8,9},{9,8},{10,11... | collective-permute-start | bytes 9437192 | tf_op jit(solution)/shard_map/ppermute | solution.py:151
  57.1 10.7 %collective-permute-start.8 = (f32[64,1536]{1,0:T(8,128)S(1)}, f32[64,1536]{1,0:T(8,128)S(1)}, u32[]{:S(2)}, u32[]{:S(2)}) collective-permute-start(f32[64,1536]{1,0:T(8,128)S(1)} %multiply_bitcast_fusion.1.refs_0_), channel_id=1, source_target_pairs={{0,64},{64,0},{1,65},{65,1},{2,66},{66,2},{3,67},{67,3},{4,68},{68... | collective-permute-start | bytes 1179656 | tf_op jit(solution)/shard_map/ppermute | solution.py:142
  58.3 14.3 %collective-permute-start.9 = (f32[64,1536]{1,0:T(8,128)S(1)}, f32[64,1536]{1,0:T(8,128)S(1)}, u32[]{:S(2)}, u32[]{:S(2)}) collective-permute-start(f32[64,1536]{1,0:T(8,128)S(1)} %multiply_bitcast_fusion.1.refs_0_), channel_id=1, source_target_pairs={{0,16},{16,32},{32,48},{48,0},{1,17},{17,33},{33,49},{49,1},{2,18}... | collective-permute-start | bytes 1179656 | tf_op jit(solution)/shard_map/ppermute | solution.py:140
  67.8 11.0 %collective-permute-start.12 = (f32[64,1536]{1,0:T(8,128)S(1)}, f32[64,1536]{1,0:T(8,128)S(1)}, u32[]{:S(2)}, u32[]{:S(2)}) collective-permute-start(f32[64,1536]{1,0:T(8,128)S(1)} %collective-permute-done.8.refs_1_), channel_id=1, source_target_pairs={{0,48},{16,0},{32,16},{48,32},{1,49},{17,1},{33,17},{49,33},{2,50}... | collective-permute-start | bytes 1179656 | tf_op jit(solution)/shard_map/ppermute | solution.py:144
  71.1 16.0 %collective-permute-start.10 = (f32[64,1536]{1,0:T(8,128)S(1)}, f32[64,1536]{1,0:T(8,128)S(1)}, u32[]{:S(2)}, u32[]{:S(2)}) collective-permute-start(f32[64,1536]{1,0:T(8,128)S(1)} %multiply_bitcast_fusion.1.refs_0_), channel_id=1, source_target_pairs={{0,48},{16,0},{32,16},{48,32},{1,49},{17,1},{33,17},{49,33},{2,50}... | collective-permute-start | bytes 1179656 | tf_op jit(solution)/shard_map/ppermute | solution.py:141
  71.2 16.0 %collective-permute-start.11 = (f32[64,1536]{1,0:T(8,128)S(1)}, f32[64,1536]{1,0:T(8,128)}, u32[]{:S(2)}, u32[]{:S(2)}) collective-permute-start(f32[64,1536]{1,0:T(8,128)S(1)} %collective-permute-done.8.refs_1_), channel_id=1, source_target_pairs={{0,16},{16,32},{32,48},{48,0},{1,17},{17,33},{33,49},{49,1},{2,18}... | collective-permute-start | bytes 1179656 | tf_op jit(solution)/shard_map/ppermute | solution.py:143
  72.6 17.8 %collective-permute-start.13 = (f32[64,1536]{1,0:T(8,128)S(1)}, f32[64,1536]{1,0:T(8,128)}, u32[]{:S(2)}, u32[]{:S(2)}) collective-permute-start(f32[64,1536]{1,0:T(8,128)S(1)} %collective-permute-done.9.refs_2_), channel_id=1, source_target_pairs={{0,16},{16,32},{32,48},{48,0},{1,17},{17,33},{33,49},{49,1},{2,18}... | collective-permute-start | bytes 1179656 | tf_op jit(solution)/shard_map/ppermute | solution.py:145
  78.8 16.9 %collective-permute-start.14 = (f32[64,1536]{1,0:T(8,128)S(1)}, f32[64,1536]{1,0:T(8,128)}, u32[]{:S(2)}, u32[]{:S(2)}) collective-permute-start(f32[64,1536]{1,0:T(8,128)S(1)} %collective-permute-done.12.refs_5_), channel_id=1, source_target_pairs={{0,48},{16,0},{32,16},{48,32},{1,49},{17,1},{33,17},{49,33},{2,50}... | collective-permute-start | bytes 1179656 | tf_op jit(solution)/shard_map/ppermute | solution.py:146
  109.6 36.4 %collective-permute-start.15 = (f32[1536,512]{1,0:T(8,128)}, f32[1536,512]{1,0:T(8,128)}, u32[]{:S(2)}, u32[]{:S(2)}) collective-permute-start(f32[1536,512]{1,0:T(8,128)} %get-tuple-element.32.after_ref), channel_id=1, source_target_pairs={{0,1},{1,0},{2,3},{3,2},{4,5},{5,4},{6,7},{7,6},{8,9},{9,8},{10,11... | collective-permute-start | bytes 9437192 | tf_op jit(solution)/shard_map/ppermute | solution.py:151
  126.5 44.2 %all-to-all-start = ((f32[8,192,512]{2,1,0:T(8,128)}), f32[8,192,512]{2,1,0:T(8,128)}, u32[]{:S(2)}, u32[]{:S(2)}) async-start(f32[8,192,512]{2,1,0:T(8,128)} %bitcast.61), calls=%async_computation | async-start | bytes 6291456 | tf_op jit(solution)/shard_map/all_to_all | solution.py:156
  170.7 42.7 %all-to-all-start.1 = ((f32[8,192,512]{2,1,0:T(8,128)}), f32[8,192,512]{2,1,0:T(8,128)}, u32[]{:S(2)}, u32[]{:S(2)}) async-start(f32[8,192,512]{2,1,0:T(8,128)} %bitcast.60), calls=%async_computation.1 | async-start | bytes 6291456 | tf_op jit(solution)/shard_map/all_to_all | solution.py:156
  177.3 5.2 %collective-permute-start.16 = (f32[512,192]{1,0:T(8,128)S(1)}, f32[512,192]{1,0:T(8,128)S(1)}, u32[]{:S(2)}, u32[]{:S(2)}) collective-permute-start(f32[512,192]{1,0:T(8,128)S(1)} %constant_dynamic-slice_fusion.7), channel_id=1, source_target_pairs={{0,0},{1,1},{16,2},{17,3},{32,4},{33,5},{48,6},{49,7},{64,8},{65,9... | collective-permute-start | bytes 1179656 | tf_op jit(solution)/shard_map/ppermute | solution.py:153
  179.3 5.8 %collective-permute-start.17 = (f32[512,192]{1,0:T(8,128)S(1)}, f32[512,192]{1,0:T(8,128)S(1)}, u32[]{:S(2)}, u32[]{:S(2)}) collective-permute-start(f32[512,192]{1,0:T(8,128)S(1)} %constant_dynamic-slice_fusion.5), channel_id=1, source_target_pairs={{0,0},{1,1},{16,2},{17,3},{32,4},{33,5},{48,6},{49,7},{64,8},{65,9... | collective-permute-start | bytes 1179656 | tf_op jit(solution)/shard_map/ppermute | solution.py:153
  217.7 4.3 %collective-permute-start.18 = (f32[768,512]{1,0:T(8,128)S(1)}, f32[768,512]{1,0:T(8,128)S(1)}, u32[]{:S(2)}, u32[]{:S(2)}) collective-permute-start(f32[768,512]{1,0:T(8,128)S(1)} %pad_maximum_fusion), channel_id=1, source_target_pairs={{0,1},{1,0},{2,3},{3,2},{4,5},{5,4},{6,7},{7,6},{8,9},{9,8},{10,11... | collective-permute-start | bytes 4718600 | tf_op jit(solution)/shard_map/ppermute | solution.py:187
  327.4 26.4 %collective-permute-start.19 = (f32[768,512]{1,0:T(8,128)}, f32[768,512]{1,0:T(8,128)}, u32[]{:S(2)}, u32[]{:S(2)}) collective-permute-start(f32[768,512]{1,0:T(8,128)} %reshape.46), channel_id=1, source_target_pairs={{0,1},{1,0},{2,3},{3,2},{4,5},{5,4},{6,7},{7,6},{8,9},{9,8},{10,11... | collective-permute-start | bytes 4718600 | tf_op jit(solution)/shard_map/ppermute | solution.py:193
  331.9 19.1 %all-to-all-start.2 = ((f32[16,32,384]{2,1,0:T(8,128)}), f32[16,32,384]{2,1,0:T(8,128)S(1)}, u32[]{:S(2)}, u32[]{:S(2)}) async-start(f32[16,32,384]{2,1,0:T(8,128)} %bitcast.18), calls=%async_computation.2 | async-start | bytes 1572864 | tf_op jit(solution)/shard_map/all_to_all | solution.py:161
  (13 other events, 52.2 us)

commit v5 on v1

v5 whole, which is shorter than its diff:
```python
import functools

import jax
import jax.numpy as jnp
from jax import lax
from jax.experimental import pallas as pl
from jax.experimental.pallas import tpu as pltpu
from jax.sharding import Mesh, PartitionSpec as P


BLOCK = 128
ROW = ("xl", "z")
COL = ("xh", "y", "core")
PLANE = ("xh", "y")
CHIPS = ("xl", "z", "xh", "y")
ALL = ROW + COL
SIZES = (2, 4, 2, 4, 2)
SWAP = ((0, 1), (1, 0))


def product(left, right, contract=((1,), (0,))):
    return lax.dot_general(left, right, (contract, ((), ())), precision=lax.Precision.HIGH,
                           preferred_element_type=jnp.float32)


def linear(xl, z, xh, y, core):
    return (((xl * 4 + z) * 2 + xh) * 4 + y) * 2 + core


def raw_routes():
    routes = []
    for xl in range(2):
        for z in range(4):
            for xh in range(2):
                for y in range(4):
                    for core in range(2):
                        source = linear(xh, (y - z) % 4, xl, z, core)
                        routes.append((source, linear(xl, z, xh, y, core)))
    return routes


def split(value):
    high = value.astype(jnp.bfloat16)
    return high, (value - high.astype(jnp.float32)).astype(jnp.bfloat16)


def half_kernel(minus, added, kept, place_ref, a_ref, *refs):
    refs = list(refs)
    pieces = [refs.pop(0) for _ in range(8)]
    minus_ref = refs.pop(0) if minus else None
    added_ref = refs.pop(0) if added else None
    out_ref = refs.pop(0)
    factor_ref = refs.pop(0) if kept else None
    high_ref, low_ref = refs

    @pl.when(pl.program_id(0) == 0)
    def _():
        for index, piece_ref in enumerate(pieces):
            size = piece_ref.shape[0]
            span = pl.ds(pl.multiple_of(place_ref[1 + index] * size, size), size)
            value = piece_ref[...]
            if minus:
                value = value - minus_ref[span, :]
            high, low = split(value)
            if kept:
                factor_ref[span, :] = value
            high_ref[span, :] = high
            low_ref[span, :] = low

    a_high, a_low = split(a_ref[...])
    dims = (((1,), (1,)), ((), ()))
    dot = lambda l, r: lax.dot_general(l, r, dims, preferred_element_type=jnp.float32)
    total = dot(high_ref[...], a_high) + dot(low_ref[...], a_high) + dot(high_ref[...], a_low)
    out_ref[...] = total + added_ref[...] if added else total


def half_product(ancestor, pieces, places, minus=None, added=None, kept=False):
    rows, depth = ancestor.shape
    width = 8 * pieces[0].shape[0]
    tile = rows // 12
    once = dict(pipeline_mode=pl.Buffered(1))
    whole = pl.BlockSpec((width, depth), lambda i, places: (0, 0), **once)
    piece = pl.BlockSpec((width // 8, depth), lambda i, places: (0, 0), **once)
    column = pl.BlockSpec((width, tile), lambda i, places: (0, i))
    operands, in_specs = [places, ancestor, *pieces], [
        pl.BlockSpec((tile, depth), lambda i, places: (places[0] * 6 + i, 0)), *[piece] * 8]
    if minus is not None:
        operands.append(minus)
        in_specs.append(whole)
    if added is not None:
        operands.append(added)
        in_specs.append(column)
    out_shape, out_specs = [jax.ShapeDtypeStruct((width, rows // 2), jnp.float32)], [column]
    if kept:
        out_shape.append(jax.ShapeDtypeStruct((width, depth), jnp.float32))
        out_specs.append(whole)
    result = pl.pallas_call(
        functools.partial(half_kernel, minus is not None, added is not None, kept),
        grid_spec=pltpu.PrefetchScalarGridSpec(
            num_scalar_prefetch=1,
            grid=(6,),
            in_specs=in_specs,
            out_specs=out_specs,
            scratch_shapes=[pltpu.VMEM((width, depth), jnp.bfloat16)] * 2,
        ),
        out_shape=out_shape,
        cost_estimate=pl.CostEstimate(
            flops=3 * rows * depth * width, transcendentals=0,
            bytes_accessed=2 * rows * depth + 4 * width * depth + 2 * rows * width),
        compiler_params=pltpu.CompilerParams(vmem_limit_bytes=40 * 1024 * 1024),
    )(*operands)
    return result if kept else result[0]


def order_kernel(place_ref, *refs):
    pieces, (one_ref, two_ref) = refs[:8], refs[8:]
    for index, piece_ref in enumerate(pieces):
        size = piece_ref.shape[0] // 2
        span = pl.ds(pl.multiple_of(place_ref[index] * size, size), size)
        one_ref[span, :] = piece_ref[:size, :]
        two_ref[span, :] = piece_ref[size:, :]


def ordered(pieces, places):
    size, depth = pieces[0].shape
    spec = pl.BlockSpec((size, depth), lambda i, places: (0, 0), pipeline_mode=pl.Buffered(1))
    whole = pl.BlockSpec((4 * size, depth), lambda i, places: (0, 0), pipeline_mode=pl.Buffered(1))
    return pl.pallas_call(
        order_kernel,
        grid_spec=pltpu.PrefetchScalarGridSpec(
            num_scalar_prefetch=1, grid=(1,), in_specs=[spec] * 8, out_specs=[whole] * 2),
        out_shape=[jax.ShapeDtypeStruct((4 * size, depth), jnp.float32)] * 2,
        cost_estimate=pl.CostEstimate(flops=0, transcendentals=0, bytes_accessed=64 * size * depth),
        compiler_params=pltpu.CompilerParams(vmem_limit_bytes=40 * 1024 * 1024),
    )(places, *pieces)


def per_device(ancestor, lhat_one, lhat_two, link_two, diag_one, diag_two, mask_one, mask_two):
    column_index = lax.axis_index(COL)
    core = lax.axis_index("core")
    xl, z = lax.axis_index("xl"), lax.axis_index("z")
    xh, y = lax.axis_index("xh"), lax.axis_index("y")
    rows, depth = ancestor.shape
    width = link_two.shape[0]
    blocks = depth // BLOCK
    strip, half = width // 8, width // 2
    up = [(i, (i + 1) % 4) for i in range(4)]
    down = [(i, (i - 1) % 4) for i in range(4)]

    def places_of(side, ring):
        here = [side * 4 + (ring + step) % 4 for step in range(4)]
        there = [(1 - side) * 4 + (ring + step) % 4 for step in range(4)]
        return [here[0], there[0], here[3], here[1], there[3], there[1], here[2], there[2]]

    row_places = places_of(xl, z)
    own_places = jnp.stack([core] + row_places).astype(jnp.int32)
    other_places = jnp.stack([1 - core] + row_places).astype(jnp.int32)
    plane_places = jnp.stack(places_of(xh, y - z + 4)).astype(jnp.int32)

    def masked(shard, mask):
        own = lax.dynamic_slice_in_dim(mask, column_index * blocks, blocks).astype(jnp.float32)
        return shard.T * jnp.broadcast_to(own[:, None], (blocks, BLOCK)).reshape(1, depth)

    def gathered(piece, side_axis, ring_axis):
        below = lax.ppermute(piece, ring_axis, up)
        above = lax.ppermute(piece, ring_axis, down)
        side = lax.ppermute(piece, side_axis, SWAP)
        side_below = lax.ppermute(side, ring_axis, up)
        side_above = lax.ppermute(side, ring_axis, down)
        far = lax.ppermute(below, ring_axis, up)
        side_far = lax.ppermute(side_above, ring_axis, down)
        return [piece, side, below, above, side_below, side_above, far, side_far]

    def scattered(chip):
        pieces = lax.all_to_all(chip.reshape(8, strip, rows // 2), PLANE,
                                split_axis=0, concat_axis=0, tiled=True)
        return -pieces.sum(0)

    def halves(value, axis):
        size = value.shape[axis] // 2
        cut = lambda side: lax.dynamic_slice_in_dim(value, side * size, size, axis)
        return cut(core), cut(1 - core)

    def to_rows(part_t):
        keep, send = halves(part_t, 0)
        received = lax.ppermute(send, "core", SWAP)
        full = jnp.where(core == 0, jnp.concatenate([keep, received], 1),
                         jnp.concatenate([received, keep], 1))
        return full.T

    def strips(left, right):
        return product(left, right, ((1,), (1,)))

    piece_one = masked(lhat_one, mask_one)
    piece_two = masked(lhat_two, mask_two)
    pieces_one = gathered(piece_one, "xl", "z")
    raw = lax.ppermute(jnp.concatenate([piece_one, piece_two]), ALL, raw_routes())
    row_pieces = gathered(raw, "xh", "y")
    link_base = lax.optimization_barrier(-product(diag_one, link_two))
    piece_two, *pieces_one = lax.optimization_barrier((piece_two, *pieces_one))
    pieces_two = gathered(piece_two, "xl", "z")

    send_one, factor_one = half_product(ancestor, pieces_one, other_places, kept=True)
    received_one = lax.ppermute(send_one, "core", SWAP)
    chip_one = half_product(ancestor, pieces_one, own_places, added=received_one)
    x_one = scattered(chip_one)
    mixed = product(link_two, factor_one, ((0,), (0,)))
    send_two = half_product(ancestor, pieces_two, other_places, minus=mixed)
    received_two = lax.ppermute(send_two, "core", SWAP)
    chip_two = half_product(ancestor, pieces_two, own_places, minus=mixed, added=received_two)
    x_two = scattered(chip_two)

    rows_one, rows_two = ordered(row_pieces, plane_places)
    parts = jnp.stack([strips(x_one, rows_one), strips(x_one, rows_two), strips(x_two, rows_two)])
    keep, send = halves(parts, 2)
    chip = keep + lax.ppermute(send, "core", SWAP)
    chip = chip.reshape(3, 8, strip // 8, half).transpose(1, 0, 2, 3)
    piece = lax.all_to_all(chip, ROW, split_axis=0, concat_axis=0, tiled=True).sum(0)
    spread = lax.all_to_all(jnp.broadcast_to(piece[None], (64,) + piece.shape), CHIPS,
                            split_axis=0, concat_axis=0, tiled=True)
    spread = spread.reshape(8, 8, 3, strip // 8, half).transpose(2, 1, 0, 3, 4).reshape(3, width, half)
    other = lax.ppermute(spread, "core", SWAP)
    sums = jnp.where(core == 0, jnp.concatenate([spread, other], 2), jnp.concatenate([other, spread], 2))
    d_one = diag_one - sums[0].T
    link_inverse = link_base - sums[1] + product(sums[0], link_two, ((0,), (0,)))
    d_two = diag_two - sums[2].T - product(link_two, link_inverse, ((0,), (0,)))
    return (to_rows(x_one), d_one, to_rows(x_two), link_inverse, d_two)


def solution(mesh):
    fine = Mesh(mesh.devices.reshape(SIZES), ALL)
    in_specs = (P(ROW, COL), P(COL, ROW), P(COL, ROW), P(), P(), P(), P(), P())
    out_specs = (P(ROW, COL), P(), P(ROW, COL), P(), P())
    return jax.shard_map(
        per_device, mesh=fine, in_specs=in_specs, out_specs=out_specs, check_vma=False
    )
```

time: 408 us -> 389 us (0.953)
  waiting for transfers between devices: 248 us -> 133 us
  starting transfers between devices: 23.8 us -> 109 us
  Pallas kernels: 0 us -> 51 us
  matrix products: 53.1 us -> 16.9 us
  blocking collectives: 12.7 us -> 37.3 us
  between operations: 14.4 us -> 0.98 us
  other arithmetic: 19.9 us -> 11.4 us
  local copies, waits for them, and re-layouts: 34.9 us -> 27.5 us
    ppermute x7 -> x28, waiting for transfers between devices: 21.6 us -> 133 us  [the longest x3 50.1 us: gathered(): below = lax.ppermute(piece, ring_axis, up)]
    reduce_scatter x4 -> x0, waiting for transfers between devices: 92.4 us -> none  [the longest x2 44.6 us: row_sum(): lax.psum_scatter(chip, 'y', scatter_dimension=0, tiled=True)]
    ppermute x7 -> x28, starting transfers between devices: 18 us -> 93.8 us  [the longest x3 56.7 us: gathered(): side = lax.ppermute(piece, side_axis, SWAP)]
    all_gather x3 -> x0, waiting for transfers between devices: 73.8 us -> none  [the longest x1 43.3 us: per_device(): lax.all_gather(masked(lhat_one, mask_one), ROW, axis=1, tiled=True)]
    pallas_call x0 -> x5, Pallas kernels: none -> 51 us  [the longest x4 48 us: half_product(): pl.pallas_call(functools.partial(half_kernel, minus is not None, added is...]
    psum x1 -> x0, waiting for transfers between devices: 43.5 us -> none  [per_device(): piece = lax.psum(piece, ('xl', 'xh'))]
    all_to_all x0 -> x2, blocking collectives: none -> 37.3 us  [the longest x1 28.1 us: per_device(): lax.all_to_all(jnp.broadcast_to(piece[None], (64,) + piece.shape), CHIPS,...]
    dot_general x8 -> x7, matrix products: 53.1 us -> 16.9 us  [product(): lax.dot_general(left, right, (contract, ((), ())), precision=lax.Precisio...]
  transfers between devices with their start and end apart: 16 -> 30, of which waited for: 12 -> 16; matrix products, arithmetic and copies ran while one was open for 20% -> 6% of each run, Pallas kernels for 0% -> 10%
where the time goes in v5:
time: 389 us; the launch traced here: 387 us
  waiting for transfers between devices  133 us (34%)
  starting transfers between devices  109 us (28%)
  Pallas kernels  51 us (13%)
  blocking collectives  37.3 us (10%)
  local copies, waits for them, and re-layouts  27.5 us (7%)
  matrix products  16.9 us (4%)
  other arithmetic  11.4 us (3%)
    ppermute x3, starting transfers between devices, gathered(): side = lax.ppermute(piece, side_axis, SWAP)  56.7 us
    ppermute x3, waiting for transfers between devices, gathered(): below = lax.ppermute(piece, ring_axis, up)  50.1 us
    pallas_call x4, Pallas kernels, half_product(): pl.pallas_call(functools.partial(half_kernel, minus is not None, added is...  48 us
    all_to_all x1, blocking collectives, per_device(): lax.all_to_all(jnp.broadcast_to(piece[None], (64,) + piece.shape), CHIPS,...  28.1 us
    unnamed x68, local copies, waits for them, and re-layouts  26.7 us
    ppermute x3, waiting for transfers between devices, gathered(): far = lax.ppermute(below, ring_axis, up)  23.1 us
    ppermute x3, waiting for transfers between devices, gathered(): above = lax.ppermute(piece, ring_axis, down)  17.4 us
    dot_general x7, matrix products, product(): lax.dot_general(left, right, (contract, ((), ())), precision=lax.Precisio...  16.9 us
  transfers between devices with their start and end apart: 30, of which 16 were waited for; matrix products, arithmetic and copies ran while one was open for 6% of the time, Pallas kernels for 10%

profile of v5, /device:TPU:1, one launch (start us, length us, event | category | flops | bytes accessed | tf_op | source)
XLA Modules:
  0.0 386.9 jit_solution(17261236622569695929)
XLA Ops:
  6.4 6.8 %collective-permute-done.refs_1_ = f32[64,1536]{1,0:T(8,128)S(1)} collective-permute-done((f32[64,1536]{1,0:T(8,128)S(1)}, f32[64,1536]{1,0:T(8,128)S(1)}, u32[]{:S(2)}, u32[]{:S(2)}) %collective-permute-start) | collective-permute-done | bytes 393248 | tf_op jit(solution)/shard_map/ppermute | solution.py:167
  13.1 4.1 %collective-permute-start.4 = (f32[64,1536]{1,0:T(8,128)S(1)}, f32[64,1536]{1,0:T(8,128)S(1)}, u32[]{:S(2)}, u32[]{:S(2)}) collective-permute-start(f32[64,1536]{1,0:T(8,128)S(1)} %collective-permute-done.refs_1_), channel_id=1, source_target_pairs={{0,48},{16,0},{32,16},{48,32},{1,49},{17,1},{33,17},{49,33},{2,50}... | collective-permute-start | bytes 1179656 | tf_op jit(solution)/shard_map/ppermute | solution.py:169
  19.0 5.2 %collective-permute-done.4.refs_5_ = f32[64,1536]{1,0:T(8,128)S(1)} collective-permute-done((f32[64,1536]{1,0:T(8,128)S(1)}, f32[64,1536]{1,0:T(8,128)S(1)}, u32[]{:S(2)}, u32[]{:S(2)}) %collective-permute-start.4) | collective-permute-done | bytes 393248 | tf_op jit(solution)/shard_map/ppermute | solution.py:169
  24.2 3.4 collective-permute-start.6
  28.7 4.0 %collective-permute-done.2.refs_3_ = f32[64,1536]{1,0:T(8,128)S(1)} collective-permute-done((f32[64,1536]{1,0:T(8,128)S(1)}, f32[64,1536]{1,0:T(8,128)S(1)}, u32[]{:S(2)}, u32[]{:S(2)}) %collective-permute-start.2) | collective-permute-done | bytes 393248 | tf_op jit(solution)/shard_map/ppermute | solution.py:166
  35.8 5.3 %collective-permute-done.6.refs_7_ = f32[64,1536]{1,0:T(8,128)S(1)} collective-permute-done((f32[64,1536]{1,0:T(8,128)S(1)}, f32[64,1536]{1,0:T(8,128)S(1)}, u32[]{:S(2)}, u32[]{:S(2)}) %collective-permute-start.6) | collective-permute-done | bytes 393248 | tf_op jit(solution)/shard_map/ppermute | solution.py:171
  41.1 12.5 %shard_map.119 = (f32[512,1536]{1,0:T(8,128)}, f32[512,1536]{1,0:T(8,128)S(1)}) custom-call(s32[9]{0:T(128)S(1)} %stack.94.place_ref, f32[3072,1536]{1,0:T(8,128)} %a_ref.7, f32[64,1536]{1,0:T(8,128)S(1)} %multiply_bitcast_fusion.refs_0_, f32[64,1536]{1,0:T(8,128)S(1)} %collective-permute-done.refs_1_, f32[64,1536]{1,0:T(8,128)S(1)} %collective-permute-done.1.refs_2_, ...), custom_call_target="tpu_custom_call" | custom-call | flops 7247757312 | bytes 15728640 | tf_op jit(solution)/shard_map/pallas_call | solution.py:97
  57.6 9.1 %collective-permute-done.17.refs_1_ = f32[64,1536]{1,0:T(8,128)S(1)} collective-permute-done((f32[64,1536]{1,0:T(8,128)S(1)}, f32[64,1536]{1,0:T(8,128)S(1)}, u32[]{:S(2)}, u32[]{:S(2)}) %collective-permute-start.17) | collective-permute-done | bytes 393248 | tf_op jit(solution)/shard_map/ppermute | solution.py:167
  66.7 3.4 collective-permute-start.21
  71.6 6.0 %collective-permute-done.21.refs_5_ = f32[64,1536]{1,0:T(8,128)S(1)} collective-permute-done((f32[64,1536]{1,0:T(8,128)S(1)}, f32[64,1536]{1,0:T(8,128)S(1)}, u32[]{:S(2)}, u32[]{:S(2)}) %collective-permute-start.21) | collective-permute-done | bytes 393248 | tf_op jit(solution)/shard_map/ppermute | solution.py:169
  89.2 5.3 %collective-permute-done.23.refs_7_ = f32[64,1536]{1,0:T(8,128)S(1)} collective-permute-done((f32[64,1536]{1,0:T(8,128)S(1)}, f32[64,1536]{1,0:T(8,128)S(1)}, u32[]{:S(2)}, u32[]{:S(2)}) %collective-permute-start.23) | collective-permute-done | bytes 393248 | tf_op jit(solution)/shard_map/ppermute | solution.py:171
  94.5 12.4 %shard_map.122 = f32[512,1536]{1,0:T(8,128)} custom-call(s32[9]{0:T(128)S(1)} %stack.94.place_ref, f32[3072,1536]{1,0:T(8,128)} %a_ref.7, f32[64,1536]{1,0:T(8,128)S(1)} %multiply_bitcast_fusion.1.refs_0_, f32[64,1536]{1,0:T(8,128)S(1)} %collective-permute-done.17.refs_1_, f32[64,1536]{1,0:T(8,128)S(1)} %collective-permute-done.18.refs_2_, ...), custom_call_target="tpu_custom_call" | custom-call | flops 7247757312 | bytes 15728640 | tf_op jit(solution)/shard_map/pallas_call | solution.py:97
  116.0 11.5 %shard_map.120 = f32[512,1536]{1,0:T(8,128)S(1)} custom-call(s32[9]{0:T(128)S(1)} %stack.92.place_ref, f32[3072,1536]{1,0:T(8,128)} %a_ref.7, f32[64,1536]{1,0:T(8,128)S(1)} %multiply_bitcast_fusion.refs_0_, f32[64,1536]{1,0:T(8,128)S(1)} %copy-done.15, f32[64,1536]{1,0:T(8,128)S(1)} %copy-done.17, f32[64,1536]{1,0:T(8,128)S(1)} %copy-done.21, ...), custom_call_target="tpu_custom_call" | custom-call | flops 7247757312 | bytes 15728640 | tf_op jit(solution)/shard_map/pallas_call | solution.py:97
  129.2 6.7 %all-to-all-start = ((f32[8,64,1536]{2,1,0:T(8,128)}), f32[8,64,1536]{2,1,0:T(8,128)}, u32[]{:S(2)}, u32[]{:S(2)}) async-start(f32[8,64,1536]{2,1,0:T(8,128)} %bitcast.84), calls=%async_computation | async-start | bytes 6291456 | tf_op jit(solution)/shard_map/all_to_all | solution.py:175
  137.5 53.4 %collective-permute-start.10 = (f32[128,1536]{1,0:T(8,128)}, f32[128,1536]{1,0:T(8,128)}, u32[]{:S(2)}, u32[]{:S(2)}) collective-permute-start(f32[128,1536]{1,0:T(8,128)} %collective-permute-done.9.refs_0_), channel_id=1, source_target_pairs={{0,8},{8,0},{1,9},{9,1},{2,10},{10,2},{3,11},{11,3},{4,12},{12,4},... | collective-permute-start | bytes 2359304 | tf_op jit(solution)/shard_map/ppermute | solution.py:167
  195.8 11.5 %shard_map.123 = f32[512,1536]{1,0:T(8,128)S(1)} custom-call(s32[9]{0:T(128)S(1)} %stack.92.place_ref, f32[3072,1536]{1,0:T(8,128)} %a_ref.7, f32[64,1536]{1,0:T(8,128)S(1)} %multiply_bitcast_fusion.1.refs_0_, f32[64,1536]{1,0:T(8,128)S(1)} %collective-permute-done.17.refs_1_, f32[64,1536]{1,0:T(8,128)S(1)} %collective-permute-done.18.refs_2_, ...), custom_call_target="tpu_custom_call" | custom-call | flops 7247757312 | bytes 15728640 | tf_op jit(solution)/shard_map/pallas_call | solution.py:97
  209.0 8.2 %all-to-all-start.1 = ((f32[8,64,1536]{2,1,0:T(8,128)}), f32[8,64,1536]{2,1,0:T(8,128)}, u32[]{:S(2)}, u32[]{:S(2)}) async-start(f32[8,64,1536]{2,1,0:T(8,128)} %bitcast.83), calls=%async_computation.1 | async-start | bytes 6291456 | tf_op jit(solution)/shard_map/all_to_all | solution.py:175
  222.0 50.1 %collective-permute-done.11.refs_2_ = f32[128,1536]{1,0:T(8,128)S(1)} collective-permute-done((f32[128,1536]{1,0:T(8,128)}, f32[128,1536]{1,0:T(8,128)S(1)}, u32[]{:S(2)}, u32[]{:S(2)}) %collective-permute-start.11) | collective-permute-done | bytes 786464 | tf_op jit(solution)/shard_map/ppermute | solution.py:165
  274.8 11.1 %collective-permute-done.12.refs_3_ = f32[128,1536]{1,0:T(8,128)S(1)} collective-permute-done((f32[128,1536]{1,0:T(8,128)}, f32[128,1536]{1,0:T(8,128)S(1)}, u32[]{:S(2)}, u32[]{:S(2)}) %collective-permute-start.12) | collective-permute-done | bytes 786464 | tf_op jit(solution)/shard_map/ppermute | solution.py:166
  289.0 16.9 %collective-permute-done.15.refs_6_ = f32[128,1536]{1,0:T(8,128)} collective-permute-done((f32[128,1536]{1,0:T(8,128)S(1)}, f32[128,1536]{1,0:T(8,128)}, u32[]{:S(2)}, u32[]{:S(2)}) %collective-permute-start.15) | collective-permute-done | bytes 786464 | tf_op jit(solution)/shard_map/ppermute | solution.py:170
  314.4 3.6 convolution_bitcast_fusion.4
  321.8 3.4 convolution_bitcast_fusion.2
  327.0 9.2 %all_to_all.20 = f32[8,3,8,256]{3,2,1,0:T(8,128)S(1)} all-to-all(f32[8,3,8,256]{3,2,1,0:T(8,128)S(1)} %copy_bitcast_fusion), channel_id=1, replica_groups=mesh['xl'=2,'z'=4,'xh'=2,'y'=4,'core'=2] {'xl','z'}, dimensions={0} | all-to-all | bytes 393216 | tf_op jit(solution)/shard_map/all_to_all | solution.py:218
  336.3 28.1 %all_to_all.21 = f32[64,3,8,256]{3,2,1,0:T(8,128)S(1)} all-to-all(f32[64,3,8,256]{3,2,1,0:T(8,128)S(1)} %broadcast_in_dim.8), channel_id=1, replica_groups=mesh['xl'=2,'z'=4,'xh'=2,'y'=4,'core'=2] {'xl','z','xh','y'}, dimensions={0} | all-to-all | bytes 3145728 | tf_op jit(solution)/shard_map/all_to_all | solution.py:219
  (142 shorter events, 94.7 us)
Async XLA Ops:
  4.7 14.2 %collective-permute-start.1 = (f32[64,1536]{1,0:T(8,128)S(1)}, f32[64,1536]{1,0:T(8,128)S(1)}, u32[]{:S(2)}, u32[]{:S(2)}) collective-permute-start(f32[64,1536]{1,0:T(8,128)S(1)} %multiply_bitcast_fusion.refs_0_), channel_id=1, source_target_pairs={{0,16},{16,32},{32,48},{48,0},{1,17},{17,33},{33,49},{49,1},{2,18}... | collective-permute-start | bytes 1179656 | tf_op jit(solution)/shard_map/ppermute | solution.py:165
  13.1 11.1 %collective-permute-start.4 = (f32[64,1536]{1,0:T(8,128)S(1)}, f32[64,1536]{1,0:T(8,128)S(1)}, u32[]{:S(2)}, u32[]{:S(2)}) collective-permute-start(f32[64,1536]{1,0:T(8,128)S(1)} %collective-permute-done.refs_1_), channel_id=1, source_target_pairs={{0,48},{16,0},{32,16},{48,32},{1,49},{17,1},{33,17},{49,33},{2,50}... | collective-permute-start | bytes 1179656 | tf_op jit(solution)/shard_map/ppermute | solution.py:169
  17.3 15.4 %collective-permute-start.2 = (f32[64,1536]{1,0:T(8,128)S(1)}, f32[64,1536]{1,0:T(8,128)S(1)}, u32[]{:S(2)}, u32[]{:S(2)}) collective-permute-start(f32[64,1536]{1,0:T(8,128)S(1)} %multiply_bitcast_fusion.refs_0_), channel_id=1, source_target_pairs={{0,48},{16,0},{32,16},{48,32},{1,49},{17,1},{33,17},{49,33},{2,50}... | collective-permute-start | bytes 1179656 | tf_op jit(solution)/shard_map/ppermute | solution.py:166
  17.6 15.1 %collective-permute-start.3 = (f32[64,1536]{1,0:T(8,128)S(1)}, f32[64,1536]{1,0:T(8,128)S(1)}, u32[]{:S(2)}, u32[]{:S(2)}) collective-permute-start(f32[64,1536]{1,0:T(8,128)S(1)} %collective-permute-done.refs_1_), channel_id=1, source_target_pairs={{0,16},{16,32},{32,48},{48,0},{1,17},{17,33},{33,49},{49,1},{2,18}... | collective-permute-start | bytes 1179656 | tf_op jit(solution)/shard_map/ppermute | solution.py:168
  18.9 16.9 %collective-permute-start.5 = (f32[64,1536]{1,0:T(8,128)S(1)}, f32[64,1536]{1,0:T(8,128)S(1)}, u32[]{:S(2)}, u32[]{:S(2)}) collective-permute-start(f32[64,1536]{1,0:T(8,128)S(1)} %collective-permute-done.1.refs_2_), channel_id=1, source_target_pairs={{0,16},{16,32},{32,48},{48,0},{1,17},{17,33},{33,49},{49,1},{2,18}... | collective-permute-start | bytes 1179656 | tf_op jit(solution)/shard_map/ppermute | solution.py:170
  24.2 16.9 %collective-permute-start.6 = (f32[64,1536]{1,0:T(8,128)S(1)}, f32[64,1536]{1,0:T(8,128)S(1)}, u32[]{:S(2)}, u32[]{:S(2)}) collective-permute-start(f32[64,1536]{1,0:T(8,128)S(1)} %collective-permute-done.4.refs_5_), channel_id=1, source_target_pairs={{0,48},{16,0},{32,16},{48,32},{1,49},{17,1},{33,17},{49,33},{2,50}... | collective-permute-start | bytes 1179656 | tf_op jit(solution)/shard_map/ppermute | solution.py:171
  53.6 55.4 %collective-permute-start.7 = (f32[512,1536]{1,0:T(8,128)}, f32[512,1536]{1,0:T(8,128)}, u32[]{:S(2)}, u32[]{:S(2)}) collective-permute-start(f32[512,1536]{1,0:T(8,128)} %get-tuple-element.26), channel_id=1, source_target_pairs={{0,1},{1,0},{2,3},{3,2},{4,5},{5,4},{6,7},{7,6},{8,9},{9,8},{10,11... | collective-permute-start | bytes 9437192 | tf_op jit(solution)/shard_map/ppermute | solution.py:204
  57.3 14.3 %collective-permute-start.18 = (f32[64,1536]{1,0:T(8,128)S(1)}, f32[64,1536]{1,0:T(8,128)S(1)}, u32[]{:S(2)}, u32[]{:S(2)}) collective-permute-start(f32[64,1536]{1,0:T(8,128)S(1)} %multiply_bitcast_fusion.1.refs_0_), channel_id=1, source_target_pairs={{0,16},{16,32},{32,48},{48,0},{1,17},{17,33},{33,49},{49,1},{2,18}... | collective-permute-start | bytes 1179656 | tf_op jit(solution)/shard_map/ppermute | solution.py:165
  66.7 10.9 %collective-permute-start.21 = (f32[64,1536]{1,0:T(8,128)S(1)}, f32[64,1536]{1,0:T(8,128)S(1)}, u32[]{:S(2)}, u32[]{:S(2)}) collective-permute-start(f32[64,1536]{1,0:T(8,128)S(1)} %collective-permute-done.17.refs_1_), channel_id=1, source_target_pairs={{0,48},{16,0},{32,16},{48,32},{1,49},{17,1},{33,17},{49,33},{2,50}... | collective-permute-start | bytes 1179656 | tf_op jit(solution)/shard_map/ppermute | solution.py:169
  70.1 16.0 %collective-permute-start.19 = (f32[64,1536]{1,0:T(8,128)S(1)}, f32[64,1536]{1,0:T(8,128)S(1)}, u32[]{:S(2)}, u32[]{:S(2)}) collective-permute-start(f32[64,1536]{1,0:T(8,128)S(1)} %multiply_bitcast_fusion.1.refs_0_), channel_id=1, source_target_pairs={{0,48},{16,0},{32,16},{48,32},{1,49},{17,1},{33,17},{49,33},{2,50}... | collective-permute-start | bytes 1179656 | tf_op jit(solution)/shard_map/ppermute | solution.py:166
  70.1 15.9 %collective-permute-start.20 = (f32[64,1536]{1,0:T(8,128)S(1)}, f32[64,1536]{1,0:T(8,128)S(1)}, u32[]{:S(2)}, u32[]{:S(2)}) collective-permute-start(f32[64,1536]{1,0:T(8,128)S(1)} %collective-permute-done.17.refs_1_), channel_id=1, source_target_pairs={{0,16},{16,32},{32,48},{48,0},{1,17},{17,33},{33,49},{49,1},{2,18}... | collective-permute-start | bytes 1179656 | tf_op jit(solution)/shard_map/ppermute | solution.py:168
  71.6 17.6 %collective-permute-start.22 = (f32[64,1536]{1,0:T(8,128)S(1)}, f32[64,1536]{1,0:T(8,128)S(1)}, u32[]{:S(2)}, u32[]{:S(2)}) collective-permute-start(f32[64,1536]{1,0:T(8,128)S(1)} %collective-permute-done.18.refs_2_), channel_id=1, source_target_pairs={{0,16},{16,32},{32,48},{48,0},{1,17},{17,33},{33,49},{49,1},{2,18}... | collective-permute-start | bytes 1179656 | tf_op jit(solution)/shard_map/ppermute | solution.py:170
  77.6 16.9 %collective-permute-start.23 = (f32[64,1536]{1,0:T(8,128)S(1)}, f32[64,1536]{1,0:T(8,128)S(1)}, u32[]{:S(2)}, u32[]{:S(2)}) collective-permute-start(f32[64,1536]{1,0:T(8,128)S(1)} %collective-permute-done.21.refs_5_), channel_id=1, source_target_pairs={{0,48},{16,0},{32,16},{48,32},{1,49},{17,1},{33,17},{49,33},{2,50}... | collective-permute-start | bytes 1179656 | tf_op jit(solution)/shard_map/ppermute | solution.py:171
  106.9 84.0 %collective-permute-start.24 = (f32[512,1536]{1,0:T(8,128)}, f32[512,1536]{1,0:T(8,128)}, u32[]{:S(2)}, u32[]{:S(2)}) collective-permute-start(f32[512,1536]{1,0:T(8,128)} %shard_map.122), channel_id=1, source_target_pairs={{0,1},{1,0},{2,3},{3,2},{4,5},{5,4},{6,7},{7,6},{8,9},{9,8},{10,11... | collective-permute-start | bytes 9437192 | tf_op jit(solution)/shard_map/ppermute | solution.py:209
  129.2 79.8 %all-to-all-start = ((f32[8,64,1536]{2,1,0:T(8,128)}), f32[8,64,1536]{2,1,0:T(8,128)}, u32[]{:S(2)}, u32[]{:S(2)}) async-start(f32[8,64,1536]{2,1,0:T(8,128)} %bitcast.84), calls=%async_computation | async-start | bytes 6291456 | tf_op jit(solution)/shard_map/all_to_all | solution.py:175
  137.5 81.2 %collective-permute-start.10 = (f32[128,1536]{1,0:T(8,128)}, f32[128,1536]{1,0:T(8,128)}, u32[]{:S(2)}, u32[]{:S(2)}) collective-permute-start(f32[128,1536]{1,0:T(8,128)} %collective-permute-done.9.refs_0_), channel_id=1, source_target_pairs={{0,8},{8,0},{1,9},{9,1},{2,10},{10,2},{3,11},{11,3},{4,12},{12,4},... | collective-permute-start | bytes 2359304 | tf_op jit(solution)/shard_map/ppermute | solution.py:167
  209.0 110.7 %all-to-all-start.1 = ((f32[8,64,1536]{2,1,0:T(8,128)}), f32[8,64,1536]{2,1,0:T(8,128)}, u32[]{:S(2)}, u32[]{:S(2)}) async-start(f32[8,64,1536]{2,1,0:T(8,128)} %bitcast.83), calls=%async_computation.1 | async-start | bytes 6291456 | tf_op jit(solution)/shard_map/all_to_all | solution.py:175
  217.2 54.9 %collective-permute-start.11 = (f32[128,1536]{1,0:T(8,128)}, f32[128,1536]{1,0:T(8,128)S(1)}, u32[]{:S(2)}, u32[]{:S(2)}) collective-permute-start(f32[128,1536]{1,0:T(8,128)} %collective-permute-done.9.refs_0_), channel_id=1, source_target_pairs={{0,2},{2,4},{4,6},{6,0},{1,3},{3,5},{5,7},{7,1},{8,10},{10,12},{12... | collective-permute-start | bytes 2359304 | tf_op jit(solution)/shard_map/ppermute | solution.py:165
  218.7 53.4 %collective-permute-start.14 = (f32[128,1536]{1,0:T(8,128)}, f32[128,1536]{1,0:T(8,128)S(1)}, u32[]{:S(2)}, u32[]{:S(2)}) collective-permute-start(f32[128,1536]{1,0:T(8,128)} %collective-permute-done.10.refs_1_), channel_id=1, source_target_pairs={{0,6},{2,0},{4,2},{6,4},{1,7},{3,1},{5,3},{7,5},{8,14},{10,8},{12,... | collective-permute-start | bytes 2359304 | tf_op jit(solution)/shard_map/ppermute | solution.py:169
  220.5 65.4 %collective-permute-start.12 = (f32[128,1536]{1,0:T(8,128)}, f32[128,1536]{1,0:T(8,128)S(1)}, u32[]{:S(2)}, u32[]{:S(2)}) collective-permute-start(f32[128,1536]{1,0:T(8,128)} %collective-permute-done.9.refs_0_), channel_id=1, source_target_pairs={{0,6},{2,0},{4,2},{6,4},{1,7},{3,1},{5,3},{7,5},{8,14},{10,8},{12,... | collective-permute-start | bytes 2359304 | tf_op jit(solution)/shard_map/ppermute | solution.py:166
  221.9 67.1 %collective-permute-start.13 = (f32[128,1536]{1,0:T(8,128)}, f32[128,1536]{1,0:T(8,128)}, u32[]{:S(2)}, u32[]{:S(2)}) collective-permute-start(f32[128,1536]{1,0:T(8,128)} %collective-permute-done.10.refs_1_), channel_id=1, source_target_pairs={{0,2},{2,4},{4,6},{6,0},{1,3},{3,5},{5,7},{7,1},{8,10},{10,12},{12... | collective-permute-start | bytes 2359304 | tf_op jit(solution)/shard_map/ppermute | solution.py:168
  272.1 33.8 %collective-permute-start.15 = (f32[128,1536]{1,0:T(8,128)S(1)}, f32[128,1536]{1,0:T(8,128)}, u32[]{:S(2)}, u32[]{:S(2)}) collective-permute-start(f32[128,1536]{1,0:T(8,128)S(1)} %collective-permute-done.11.refs_2_), channel_id=1, source_target_pairs={{0,2},{2,4},{4,6},{6,0},{1,3},{3,5},{5,7},{7,1},{8,10},{10,12},{12... | collective-permute-start | bytes 2359304 | tf_op jit(solution)/shard_map/ppermute | solution.py:170
  272.1 33.8 %collective-permute-start.16 = (f32[128,1536]{1,0:T(8,128)S(1)}, f32[128,1536]{1,0:T(8,128)}, u32[]{:S(2)}, u32[]{:S(2)}) collective-permute-start(f32[128,1536]{1,0:T(8,128)S(1)} %collective-permute-done.14.refs_5_), channel_id=1, source_target_pairs={{0,6},{2,0},{4,2},{6,4},{1,7},{3,1},{5,3},{7,5},{8,14},{10,8},{12,... | collective-permute-start | bytes 2359304 | tf_op jit(solution)/shard_map/ppermute | solution.py:171
  364.6 14.4 %collective-permute-start.26 = (f32[3,512,256]{2,1,0:T(8,128)S(1)}, f32[3,512,256]{2,1,0:T(8,128)}, u32[]{:S(2)}, u32[]{:S(2)}) collective-permute-start(f32[3,512,256]{2,1,0:T(8,128)S(1)} %bitcast.86), channel_id=1, source_target_pairs={{0,1},{1,0},{2,3},{3,2},{4,5},{5,4},{6,7},{7,6},{8,9},{9,8},{10,11... | collective-permute-start | bytes 4718600 | tf_op jit(solution)/shard_map/ppermute | solution.py:222
  (38 other events, 387.9 us)

commit v6 on v5

--- a/solution.py
+++ b/solution.py
@@ -51,26 +51,29 @@
     added_ref = refs.pop(0) if added else None
     out_ref = refs.pop(0)
     factor_ref = refs.pop(0) if kept else None
-    high_ref, low_ref = refs
+    (both_ref,) = refs
+    width = both_ref.shape[0] // 2
 
     @pl.when(pl.program_id(0) == 0)
     def _():
         for index, piece_ref in enumerate(pieces):
             size = piece_ref.shape[0]
-            span = pl.ds(pl.multiple_of(place_ref[1 + index] * size, size), size)
+            start = pl.multiple_of(place_ref[1 + index] * size, size)
+            span = pl.ds(start, size)
             value = piece_ref[...]
             if minus:
                 value = value - minus_ref[span, :]
             high, low = split(value)
             if kept:
                 factor_ref[span, :] = value
-            high_ref[span, :] = high
-            low_ref[span, :] = low
+            both_ref[span, :] = high
+            both_ref[pl.ds(pl.multiple_of(start + width, size), size), :] = low
 
     a_high, a_low = split(a_ref[...])
     dims = (((1,), (1,)), ((), ()))
     dot = lambda l, r: lax.dot_general(l, r, dims, preferred_element_type=jnp.float32)
-    total = dot(high_ref[...], a_high) + dot(low_ref[...], a_high) + dot(high_ref[...], a_low)
+    stacked = dot(both_ref[...], a_high)
+    total = stacked[:width] + stacked[width:] + dot(both_ref[:width, :], a_low)
     out_ref[...] = total + added_ref[...] if added else total
 
 
@@ -101,13 +104,13 @@
             grid=(6,),
             in_specs=in_specs,
             out_specs=out_specs,
-            scratch_shapes=[pltpu.VMEM((width, depth), jnp.bfloat16)] * 2,
+            scratch_shapes=[pltpu.VMEM((2 * width, depth), jnp.bfloat16)],
         ),
         out_shape=out_shape,
         cost_estimate=pl.CostEstimate(
             flops=3 * rows * depth * width, transcendentals=0,
             bytes_accessed=2 * rows * depth + 4 * width * depth + 2 * rows * width),
-        compiler_params=pltpu.CompilerParams(vmem_limit_bytes=40 * 1024 * 1024),
+        compiler_params=pltpu.CompilerParams(vmem_limit_bytes=60 * 1024 * 1024),
     )(*operands)
     return result if kept else result[0]
 
@@ -161,10 +164,11 @@
         own = lax.dynamic_slice_in_dim(mask, column_index * blocks, blocks).astype(jnp.float32)
         return shard.T * jnp.broadcast_to(own[:, None], (blocks, BLOCK)).reshape(1, depth)
 
-    def gathered(piece, side_axis, ring_axis):
+    def gathered(piece, side_axis, ring_axis, side=None):
         below = lax.ppermute(piece, ring_axis, up)
         above = lax.ppermute(piece, ring_axis, down)
-        side = lax.ppermute(piece, side_axis, SWAP)
+        if side is None:
+            side = lax.ppermute(piece, side_axis, SWAP)
         side_below = lax.ppermute(side, ring_axis, up)
         side_above = lax.ppermute(side, ring_axis, down)
         far = lax.ppermute(below, ring_axis, up)
@@ -196,9 +200,11 @@
     pieces_one = gathered(piece_one, "xl", "z")
     raw = lax.ppermute(jnp.concatenate([piece_one, piece_two]), ALL, raw_routes())
     row_pieces = gathered(raw, "xh", "y")
-    link_base = lax.optimization_barrier(-product(diag_one, link_two))
-    piece_two, *pieces_one = lax.optimization_barrier((piece_two, *pieces_one))
-    pieces_two = gathered(piece_two, "xl", "z")
+    link_base, one_base, two_base = lax.optimization_barrier(
+        (-product(diag_one, link_two), diag_one.T, diag_two.T))
+    side_two = lax.ppermute(piece_two, "xl", SWAP)
+    piece_two, side_two, *pieces_one = lax.optimization_barrier((piece_two, side_two, *pieces_one))
+    pieces_two = gathered(piece_two, "xl", "z", side_two)
 
     send_one, factor_one = half_product(ancestor, pieces_one, other_places, kept=True)
     received_one = lax.ppermute(send_one, "core", SWAP)
@@ -221,9 +227,9 @@
     spread = spread.reshape(8, 8, 3, strip // 8, half).transpose(2, 1, 0, 3, 4).reshape(3, width, half)
     other = lax.ppermute(spread, "core", SWAP)
     sums = jnp.where(core == 0, jnp.concatenate([spread, other], 2), jnp.concatenate([other, spread], 2))
-    d_one = diag_one - sums[0].T
+    d_one = (one_base - sums[0]).T
     link_inverse = link_base - sums[1] + product(sums[0], link_two, ((0,), (0,)))
-    d_two = diag_two - sums[2].T - product(link_two, link_inverse, ((0,), (0,)))
+    d_two = (two_base - sums[2] - product(link_inverse, link_two, ((0,), (0,)))).T
     return (to_rows(x_one), d_one, to_rows(x_two), link_inverse, d_two)
 
 

time: 389 us -> 368 us (0.946)
  waiting for transfers between devices: 133 us -> 118 us
  local copies, waits for them, and re-layouts: 27.5 us -> 14.2 us
  Pallas kernels: 51 us -> 60.3 us
  starting transfers between devices: 109 us -> 105 us
    unnamed x68 -> x46, local copies, waits for them, and re-layouts: 26.7 us -> 12.3 us
    ppermute x3 -> x2, waiting for transfers between devices: 15.9 us -> 4.57 us  [gathered(): side = lax.ppermute(piece, side_axis, SWAP)]
    ppermute x3, waiting for transfers between devices: 10.6 us -> 0.01 us  [gathered(): side_far = lax.ppermute(side_above, ring_axis, down)]
    ppermute x3, waiting for transfers between devices: 23.1 us -> 33.1 us  [gathered(): far = lax.ppermute(below, ring_axis, up)]
    pallas_call x4, Pallas kernels: 48 us -> 57.3 us  [half_product(): pl.pallas_call(functools.partial(half_kernel, minus is not None, added is...]
    ppermute x3, waiting for transfers between devices: 50.1 us -> 57.8 us  [gathered(): below = lax.ppermute(piece, ring_axis, up)]
    ppermute x3, waiting for transfers between devices: 17.4 us -> 11.3 us  [gathered(): above = lax.ppermute(piece, ring_axis, down)]
    ppermute x3, waiting for transfers between devices: 11.3 us -> 5.23 us  [gathered(): side_above = lax.ppermute(side, ring_axis, down)]
  transfers between devices with their start and end apart: 30 -> 30, of which waited for: 16 -> 12; matrix products, arithmetic and copies ran while one was open for 6% -> 7% of each run, Pallas kernels for 10% -> 13%
where the time goes in v6:
time: 368 us; the launch traced here: 367 us
  waiting for transfers between devices  118 us (32%)
  starting transfers between devices  105 us (29%)
  Pallas kernels  60.3 us (16%)
  blocking collectives  36.9 us (10%)
  matrix products  20.5 us (6%)
  local copies, waits for them, and re-layouts  14.2 us (4%)
  other arithmetic  11.4 us (3%)
    ppermute x3, waiting for transfers between devices, gathered(): below = lax.ppermute(piece, ring_axis, up)  57.8 us
    pallas_call x4, Pallas kernels, half_product(): pl.pallas_call(functools.partial(half_kernel, minus is not None, added is...  57.3 us
    ppermute x2, starting transfers between devices, gathered(): side = lax.ppermute(piece, side_axis, SWAP)  56.2 us
    ppermute x3, waiting for transfers between devices, gathered(): far = lax.ppermute(below, ring_axis, up)  33.1 us
    all_to_all x1, blocking collectives, per_device(): lax.all_to_all(jnp.broadcast_to(piece[None], (64,) + piece.shape), CHIPS,...  27.9 us
    dot_general x7, matrix products, product(): lax.dot_general(left, right, (contract, ((), ())), precision=lax.Precisio...  20.5 us
    all_to_all x2, starting transfers between devices, scattered(): lax.all_to_all(chip.reshape(8, strip, rows // 2), PLANE, split_axis=0, co...  13.2 us
    unnamed x46, local copies, waits for them, and re-layouts  12.3 us
  transfers between devices with their start and end apart: 30, of which 12 were waited for; matrix products, arithmetic and copies ran while one was open for 7% of the time, Pallas kernels for 13%

profile of v6, /device:TPU:1, one launch (start us, length us, event | category | flops | bytes accessed | tf_op | source)
XLA Modules:
  0.0 366.7 jit_solution(15841711322705669403)
XLA Ops:
  8.6 4.6 %collective-permute-done.1.refs_1_ = f32[64,1536]{1,0:T(8,128)S(1)} collective-permute-done((f32[64,1536]{1,0:T(8,128)S(1)}, f32[64,1536]{1,0:T(8,128)S(1)}, u32[]{:S(2)}, u32[]{:S(2)}) %collective-permute-start.1) | collective-permute-done | bytes 393248 | tf_op jit(solution)/shard_map/ppermute | solution.py:171
  13.1 4.1 %collective-permute-start.5 = (f32[64,1536]{1,0:T(8,128)S(1)}, f32[64,1536]{1,0:T(8,128)}, u32[]{:S(2)}, u32[]{:S(2)}) collective-permute-start(f32[64,1536]{1,0:T(8,128)S(1)} %collective-permute-done.1.refs_1_), channel_id=1, source_target_pairs={{0,48},{16,0},{32,16},{48,32},{1,49},{17,1},{33,17},{49,33},{2,50}... | collective-permute-start | bytes 1179656 | tf_op jit(solution)/shard_map/ppermute | solution.py:173
  19.7 5.2 %collective-permute-done.5.refs_5_ = f32[64,1536]{1,0:T(8,128)} collective-permute-done((f32[64,1536]{1,0:T(8,128)S(1)}, f32[64,1536]{1,0:T(8,128)}, u32[]{:S(2)}, u32[]{:S(2)}) %collective-permute-start.5) | collective-permute-done | bytes 393248 | tf_op jit(solution)/shard_map/ppermute | solution.py:173
  29.5 8.4 %collective-permute-done.6.refs_6_ = f32[64,1536]{1,0:T(8,128)} collective-permute-done((f32[64,1536]{1,0:T(8,128)S(1)}, f32[64,1536]{1,0:T(8,128)}, u32[]{:S(2)}, u32[]{:S(2)}) %collective-permute-start.6) | collective-permute-done | bytes 393248 | tf_op jit(solution)/shard_map/ppermute | solution.py:174
  38.0 14.3 %shard_map.119 = (f32[512,1536]{1,0:T(8,128)}, f32[512,1536]{1,0:T(8,128)}) custom-call(s32[9]{0:T(128)} %stack.94.place_ref, f32[3072,1536]{1,0:T(8,128)} %a_ref.7, f32[64,1536]{1,0:T(8,128)} %copy-done.10, f32[64,1536]{1,0:T(8,128)} %copy-done.18, f32[64,1536]{1,0:T(8,128)} %copy-done.19, f32[64,1536]{1,0:T(8,128)} %copy-done.20, ...), custom_call_target="tpu_custom_call" | custom-call | flops 7247757312 | bytes 15728640 | tf_op jit(solution)/shard_map/pallas_call | solution.py:100
  59.4 7.7 %collective-permute-done.18.refs_2_ = f32[64,1536]{1,0:T(8,128)S(1)} collective-permute-done((f32[64,1536]{1,0:T(8,128)S(1)}, f32[64,1536]{1,0:T(8,128)S(1)}, u32[]{:S(2)}, u32[]{:S(2)}) %collective-permute-start.18) | collective-permute-done | bytes 393248 | tf_op jit(solution)/shard_map/ppermute | solution.py:168
  69.7 6.3 %convolution_bitcast_fusion.refs_8_ = f32[512,1536]{1,0:T(8,128)} fusion(f32[512,1536]{1,0:T(8,128)} %get-tuple-element.36, f32[512,512]{1,0:T(8,128)S(1)} %copy-done), kind=kOutput, calls=%fused_computation | convolution fusion | flops 2415919104 | bytes 7340032 | tf_op jit(solution)/shard_map/dot_general | solution.py:22
  76.1 7.8 %collective-permute-done.22.refs_6_ = f32[64,1536]{1,0:T(8,128)S(1)} collective-permute-done((f32[64,1536]{1,0:T(8,128)S(1)}, f32[64,1536]{1,0:T(8,128)S(1)}, u32[]{:S(2)}, u32[]{:S(2)}) %collective-permute-start.22) | collective-permute-done | bytes 393248 | tf_op jit(solution)/shard_map/ppermute | solution.py:174
  84.6 14.3 %shard_map.122 = f32[512,1536]{1,0:T(8,128)} custom-call(s32[9]{0:T(128)} %stack.94.place_ref, f32[3072,1536]{1,0:T(8,128)} %a_ref.7, f32[64,1536]{1,0:T(8,128)} %copy-done.4, f32[64,1536]{1,0:T(8,128)} %copy-done.12, f32[64,1536]{1,0:T(8,128)} %copy-done.13, f32[64,1536]{1,0:T(8,128)} %copy-done.15, f32[64,1536]{1,0:T(8,128)} %copy-done.16, ...), custom_call_target="tpu_custom_call" | custom-call | flops 7247757312 | bytes 15728640 | tf_op jit(solution)/shard_map/pallas_call | solution.py:100
  100.6 13.8 %shard_map.120 = f32[512,1536]{1,0:T(8,128)} custom-call(s32[9]{0:T(128)} %stack.92.place_ref, f32[3072,1536]{1,0:T(8,128)} %a_ref.7, f32[64,1536]{1,0:T(8,128)} %copy-done.10, f32[64,1536]{1,0:T(8,128)} %copy-done.18, f32[64,1536]{1,0:T(8,128)} %copy-done.19, f32[64,1536]{1,0:T(8,128)} %copy-done.20, f32[64,1536]{1,0:T(8,128)} %collective-permute-done.4.refs_4_, ...), custom_call_target="tpu_custom_call" | custom-call | flops 7247757312 | bytes 15728640 | tf_op jit(solution)/shard_map/pallas_call | solution.py:100
  114.3 6.5 %all-to-all-start = ((f32[8,64,1536]{2,1,0:T(8,128)}), f32[8,64,1536]{2,1,0:T(8,128)}, u32[]{:S(2)}, u32[]{:S(2)}) async-start(f32[8,64,1536]{2,1,0:T(8,128)} %bitcast.87), calls=%async_computation | async-start | bytes 6291456 | tf_op jit(solution)/shard_map/all_to_all | solution.py:179
  121.7 54.1 %collective-permute-start.11 = (f32[128,1536]{1,0:T(8,128)S(1)}, f32[128,1536]{1,0:T(8,128)S(1)}, u32[]{:S(2)}, u32[]{:S(2)}) collective-permute-start(f32[128,1536]{1,0:T(8,128)S(1)} %collective-permute-done.10.refs_0_), channel_id=1, source_target_pairs={{0,8},{8,0},{1,9},{9,1},{2,10},{10,2},{3,11},{11,3},{4,12},{12,4},... | collective-permute-start | bytes 2359304 | tf_op jit(solution)/shard_map/ppermute | solution.py:171
  175.8 14.9 %shard_map.123 = f32[512,1536]{1,0:T(8,128)} custom-call(s32[9]{0:T(128)} %stack.92.place_ref, f32[3072,1536]{1,0:T(8,128)} %a_ref.7, f32[64,1536]{1,0:T(8,128)} %copy-done.4, f32[64,1536]{1,0:T(8,128)} %copy-done.12, f32[64,1536]{1,0:T(8,128)} %copy-done.13, f32[64,1536]{1,0:T(8,128)} %copy-done.15, f32[64,1536]{1,0:T(8,128)} %copy-done.16, ...), custom_call_target="tpu_custom_call" | custom-call | flops 7247757312 | bytes 15728640 | tf_op jit(solution)/shard_map/pallas_call | solution.py:100
  190.7 6.7 %all-to-all-start.1 = ((f32[8,64,1536]{2,1,0:T(8,128)}), f32[8,64,1536]{2,1,0:T(8,128)}, u32[]{:S(2)}, u32[]{:S(2)}) async-start(f32[8,64,1536]{2,1,0:T(8,128)} %bitcast.86), calls=%async_computation.1 | async-start | bytes 6291456 | tf_op jit(solution)/shard_map/all_to_all | solution.py:179
  202.2 50.1 %collective-permute-done.12.refs_2_ = f32[128,1536]{1,0:T(8,128)S(1)} collective-permute-done((f32[128,1536]{1,0:T(8,128)S(1)}, f32[128,1536]{1,0:T(8,128)S(1)}, u32[]{:S(2)}, u32[]{:S(2)}) %collective-permute-start.12) | collective-permute-done | bytes 786464 | tf_op jit(solution)/shard_map/ppermute | solution.py:168
  255.0 11.3 %collective-permute-done.13.refs_3_ = f32[128,1536]{1,0:T(8,128)} collective-permute-done((f32[128,1536]{1,0:T(8,128)S(1)}, f32[128,1536]{1,0:T(8,128)}, u32[]{:S(2)}, u32[]{:S(2)}) %collective-permute-start.13) | collective-permute-done | bytes 786464 | tf_op jit(solution)/shard_map/ppermute | solution.py:169
  269.2 16.9 %collective-permute-done.16.refs_6_ = f32[128,1536]{1,0:T(8,128)} collective-permute-done((f32[128,1536]{1,0:T(8,128)S(1)}, f32[128,1536]{1,0:T(8,128)}, u32[]{:S(2)}, u32[]{:S(2)}) %collective-permute-start.16) | collective-permute-done | bytes 786464 | tf_op jit(solution)/shard_map/ppermute | solution.py:174
  286.1 3.0 shard_map.121
  294.6 3.6 convolution_bitcast_fusion.3
  302.0 3.4 convolution_bitcast_fusion.1
  307.2 9.1 %all_to_all.20 = f32[8,3,8,256]{3,2,1,0:T(8,128)S(1)} all-to-all(f32[8,3,8,256]{3,2,1,0:T(8,128)S(1)} %copy_bitcast_fusion), channel_id=1, replica_groups=mesh['xl'=2,'z'=4,'xh'=2,'y'=4,'core'=2] {'xl','z'}, dimensions={0} | all-to-all | bytes 393216 | tf_op jit(solution)/shard_map/all_to_all | solution.py:224
  316.4 27.9 %all_to_all.21 = f32[64,3,8,256]{3,2,1,0:T(8,128)S(1)} all-to-all(f32[64,3,8,256]{3,2,1,0:T(8,128)S(1)} %broadcast_in_dim.8), channel_id=1, replica_groups=mesh['xl'=2,'z'=4,'xh'=2,'y'=4,'core'=2] {'xl','z','xh','y'}, dimensions={0} | all-to-all | bytes 3145728 | tf_op jit(solution)/shard_map/all_to_all | solution.py:225
  344.4 3.0 collective-permute-start.26
  352.5 3.2 convolution_negate_fusion
  (120 shorter events, 65.6 us)
Async XLA Ops:
  2.6 10.5 %collective-permute-start.1 = (f32[64,1536]{1,0:T(8,128)S(1)}, f32[64,1536]{1,0:T(8,128)S(1)}, u32[]{:S(2)}, u32[]{:S(2)}) collective-permute-start(f32[64,1536]{1,0:T(8,128)S(1)} %multiply_bitcast_fusion.refs_0_), channel_id=1, source_target_pairs={{0,64},{64,0},{1,65},{65,1},{2,66},{66,2},{3,67},{67,3},{4,68},{68... | collective-permute-start | bytes 1179656 | tf_op jit(solution)/shard_map/ppermute | solution.py:171
  4.7 14.9 %collective-permute-start.2 = (f32[64,1536]{1,0:T(8,128)S(1)}, f32[64,1536]{1,0:T(8,128)S(1)}, u32[]{:S(2)}, u32[]{:S(2)}) collective-permute-start(f32[64,1536]{1,0:T(8,128)S(1)} %multiply_bitcast_fusion.refs_0_), channel_id=1, source_target_pairs={{0,16},{16,32},{32,48},{48,0},{1,17},{17,33},{33,49},{49,1},{2,18}... | collective-permute-start | bytes 1179656 | tf_op jit(solution)/shard_map/ppermute | solution.py:168
  6.4 22.0 %collective-permute-start.3 = (f32[64,1536]{1,0:T(8,128)S(1)}, f32[64,1536]{1,0:T(8,128)S(1)}, u32[]{:S(2)}, u32[]{:S(2)}) collective-permute-start(f32[64,1536]{1,0:T(8,128)S(1)} %multiply_bitcast_fusion.refs_0_), channel_id=1, source_target_pairs={{0,48},{16,0},{32,16},{48,32},{1,49},{17,1},{33,17},{49,33},{2,50}... | collective-permute-start | bytes 1179656 | tf_op jit(solution)/shard_map/ppermute | solution.py:169
  13.1 11.8 %collective-permute-start.5 = (f32[64,1536]{1,0:T(8,128)S(1)}, f32[64,1536]{1,0:T(8,128)}, u32[]{:S(2)}, u32[]{:S(2)}) collective-permute-start(f32[64,1536]{1,0:T(8,128)S(1)} %collective-permute-done.1.refs_1_), channel_id=1, source_target_pairs={{0,48},{16,0},{32,16},{48,32},{1,49},{17,1},{33,17},{49,33},{2,50}... | collective-permute-start | bytes 1179656 | tf_op jit(solution)/shard_map/ppermute | solution.py:173
  19.6 18.3 %collective-permute-start.6 = (f32[64,1536]{1,0:T(8,128)S(1)}, f32[64,1536]{1,0:T(8,128)}, u32[]{:S(2)}, u32[]{:S(2)}) collective-permute-start(f32[64,1536]{1,0:T(8,128)S(1)} %collective-permute-done.2.refs_2_), channel_id=1, source_target_pairs={{0,16},{16,32},{32,48},{48,0},{1,17},{17,33},{33,49},{49,1},{2,18}... | collective-permute-start | bytes 1179656 | tf_op jit(solution)/shard_map/ppermute | solution.py:174
  24.9 13.0 %collective-permute-start.7 = (f32[64,1536]{1,0:T(8,128)}, f32[64,1536]{1,0:T(8,128)}, u32[]{:S(2)}, u32[]{:S(2)}) collective-permute-start(f32[64,1536]{1,0:T(8,128)} %collective-permute-done.5.refs_5_), channel_id=1, source_target_pairs={{0,48},{16,0},{32,16},{48,32},{1,49},{17,1},{33,17},{49,33},{2,50}... | collective-permute-start | bytes 1179656 | tf_op jit(solution)/shard_map/ppermute | solution.py:175
  52.3 48.3 %collective-permute-start.8 = (f32[512,1536]{1,0:T(8,128)}, f32[512,1536]{1,0:T(8,128)}, u32[]{:S(2)}, u32[]{:S(2)}) collective-permute-start(f32[512,1536]{1,0:T(8,128)} %get-tuple-element.30), channel_id=1, source_target_pairs={{0,1},{1,0},{2,3},{3,2},{4,5},{5,4},{6,7},{7,6},{8,9},{9,8},{10,11... | collective-permute-start | bytes 9437192 | tf_op jit(solution)/shard_map/ppermute | solution.py:210
  55.2 11.8 %collective-permute-start.18 = (f32[64,1536]{1,0:T(8,128)S(1)}, f32[64,1536]{1,0:T(8,128)S(1)}, u32[]{:S(2)}, u32[]{:S(2)}) collective-permute-start(f32[64,1536]{1,0:T(8,128)S(1)} %multiply_bitcast_fusion.1.refs_0_), channel_id=1, source_target_pairs={{0,16},{16,32},{32,48},{48,0},{1,17},{17,33},{33,49},{49,1},{2,18}... | collective-permute-start | bytes 1179656 | tf_op jit(solution)/shard_map/ppermute | solution.py:168
  55.2 11.8 %collective-permute-start.21 = (f32[64,1536]{1,0:T(8,128)S(1)}, f32[64,1536]{1,0:T(8,128)S(1)}, u32[]{:S(2)}, u32[]{:S(2)}) collective-permute-start(f32[64,1536]{1,0:T(8,128)S(1)} %collective-permute-done.refs_1_), channel_id=1, source_target_pairs={{0,48},{16,0},{32,16},{48,32},{1,49},{17,1},{33,17},{49,33},{2,50}... | collective-permute-start | bytes 1179656 | tf_op jit(solution)/shard_map/ppermute | solution.py:173
  57.9 18.1 %collective-permute-start.19 = (f32[64,1536]{1,0:T(8,128)S(1)}, f32[64,1536]{1,0:T(8,128)S(1)}, u32[]{:S(2)}, u32[]{:S(2)}) collective-permute-start(f32[64,1536]{1,0:T(8,128)S(1)} %multiply_bitcast_fusion.1.refs_0_), channel_id=1, source_target_pairs={{0,48},{16,0},{32,16},{48,32},{1,49},{17,1},{33,17},{49,33},{2,50}... | collective-permute-start | bytes 1179656 | tf_op jit(solution)/shard_map/ppermute | solution.py:169
  57.9 18.1 %collective-permute-start.20 = (f32[64,1536]{1,0:T(8,128)S(1)}, f32[64,1536]{1,0:T(8,128)S(1)}, u32[]{:S(2)}, u32[]{:S(2)}) collective-permute-start(f32[64,1536]{1,0:T(8,128)S(1)} %collective-permute-done.refs_1_), channel_id=1, source_target_pairs={{0,16},{16,32},{32,48},{48,0},{1,17},{17,33},{33,49},{49,1},{2,18}... | collective-permute-start | bytes 1179656 | tf_op jit(solution)/shard_map/ppermute | solution.py:172
  67.0 16.9 %collective-permute-start.22 = (f32[64,1536]{1,0:T(8,128)S(1)}, f32[64,1536]{1,0:T(8,128)S(1)}, u32[]{:S(2)}, u32[]{:S(2)}) collective-permute-start(f32[64,1536]{1,0:T(8,128)S(1)} %collective-permute-done.18.refs_2_), channel_id=1, source_target_pairs={{0,16},{16,32},{32,48},{48,0},{1,17},{17,33},{33,49},{49,1},{2,18}... | collective-permute-start | bytes 1179656 | tf_op jit(solution)/shard_map/ppermute | solution.py:174
  67.0 16.8 %collective-permute-start.23 = (f32[64,1536]{1,0:T(8,128)S(1)}, f32[64,1536]{1,0:T(8,128)}, u32[]{:S(2)}, u32[]{:S(2)}) collective-permute-start(f32[64,1536]{1,0:T(8,128)S(1)} %collective-permute-done.21.refs_5_), channel_id=1, source_target_pairs={{0,48},{16,0},{32,16},{48,32},{1,49},{17,1},{33,17},{49,33},{2,50}... | collective-permute-start | bytes 1179656 | tf_op jit(solution)/shard_map/ppermute | solution.py:175
  99.0 76.8 %collective-permute-start.24 = (f32[512,1536]{1,0:T(8,128)}, f32[512,1536]{1,0:T(8,128)}, u32[]{:S(2)}, u32[]{:S(2)}) collective-permute-start(f32[512,1536]{1,0:T(8,128)} %shard_map.122), channel_id=1, source_target_pairs={{0,1},{1,0},{2,3},{3,2},{4,5},{5,4},{6,7},{7,6},{8,9},{9,8},{10,11... | collective-permute-start | bytes 9437192 | tf_op jit(solution)/shard_map/ppermute | solution.py:215
  114.3 76.4 %all-to-all-start = ((f32[8,64,1536]{2,1,0:T(8,128)}), f32[8,64,1536]{2,1,0:T(8,128)}, u32[]{:S(2)}, u32[]{:S(2)}) async-start(f32[8,64,1536]{2,1,0:T(8,128)} %bitcast.87), calls=%async_computation | async-start | bytes 6291456 | tf_op jit(solution)/shard_map/all_to_all | solution.py:179
  121.7 77.2 %collective-permute-start.11 = (f32[128,1536]{1,0:T(8,128)S(1)}, f32[128,1536]{1,0:T(8,128)S(1)}, u32[]{:S(2)}, u32[]{:S(2)}) collective-permute-start(f32[128,1536]{1,0:T(8,128)S(1)} %collective-permute-done.10.refs_0_), channel_id=1, source_target_pairs={{0,8},{8,0},{1,9},{9,1},{2,10},{10,2},{3,11},{11,3},{4,12},{12,4},... | collective-permute-start | bytes 2359304 | tf_op jit(solution)/shard_map/ppermute | solution.py:171
  190.7 109.1 %all-to-all-start.1 = ((f32[8,64,1536]{2,1,0:T(8,128)}), f32[8,64,1536]{2,1,0:T(8,128)}, u32[]{:S(2)}, u32[]{:S(2)}) async-start(f32[8,64,1536]{2,1,0:T(8,128)} %bitcast.86), calls=%async_computation.1 | async-start | bytes 6291456 | tf_op jit(solution)/shard_map/all_to_all | solution.py:179
  197.4 54.9 %collective-permute-start.12 = (f32[128,1536]{1,0:T(8,128)S(1)}, f32[128,1536]{1,0:T(8,128)S(1)}, u32[]{:S(2)}, u32[]{:S(2)}) collective-permute-start(f32[128,1536]{1,0:T(8,128)S(1)} %collective-permute-done.10.refs_0_), channel_id=1, source_target_pairs={{0,2},{2,4},{4,6},{6,0},{1,3},{3,5},{5,7},{7,1},{8,10},{10,12},{12... | collective-permute-start | bytes 2359304 | tf_op jit(solution)/shard_map/ppermute | solution.py:168
  198.8 53.4 %collective-permute-start.15 = (f32[128,1536]{1,0:T(8,128)S(1)}, f32[128,1536]{1,0:T(8,128)}, u32[]{:S(2)}, u32[]{:S(2)}) collective-permute-start(f32[128,1536]{1,0:T(8,128)S(1)} %collective-permute-done.11.refs_1_), channel_id=1, source_target_pairs={{0,6},{2,0},{4,2},{6,4},{1,7},{3,1},{5,3},{7,5},{8,14},{10,8},{12,... | collective-permute-start | bytes 2359304 | tf_op jit(solution)/shard_map/ppermute | solution.py:173
  200.7 65.6 %collective-permute-start.13 = (f32[128,1536]{1,0:T(8,128)S(1)}, f32[128,1536]{1,0:T(8,128)}, u32[]{:S(2)}, u32[]{:S(2)}) collective-permute-start(f32[128,1536]{1,0:T(8,128)S(1)} %collective-permute-done.10.refs_0_), channel_id=1, source_target_pairs={{0,6},{2,0},{4,2},{6,4},{1,7},{3,1},{5,3},{7,5},{8,14},{10,8},{12,... | collective-permute-start | bytes 2359304 | tf_op jit(solution)/shard_map/ppermute | solution.py:169
  202.1 67.1 %collective-permute-start.14 = (f32[128,1536]{1,0:T(8,128)S(1)}, f32[128,1536]{1,0:T(8,128)}, u32[]{:S(2)}, u32[]{:S(2)}) collective-permute-start(f32[128,1536]{1,0:T(8,128)S(1)} %collective-permute-done.11.refs_1_), channel_id=1, source_target_pairs={{0,2},{2,4},{4,6},{6,0},{1,3},{3,5},{5,7},{7,1},{8,10},{10,12},{12... | collective-permute-start | bytes 2359304 | tf_op jit(solution)/shard_map/ppermute | solution.py:172
  252.2 33.8 %collective-permute-start.16 = (f32[128,1536]{1,0:T(8,128)S(1)}, f32[128,1536]{1,0:T(8,128)}, u32[]{:S(2)}, u32[]{:S(2)}) collective-permute-start(f32[128,1536]{1,0:T(8,128)S(1)} %collective-permute-done.12.refs_2_), channel_id=1, source_target_pairs={{0,2},{2,4},{4,6},{6,0},{1,3},{3,5},{5,7},{7,1},{8,10},{10,12},{12... | collective-permute-start | bytes 2359304 | tf_op jit(solution)/shard_map/ppermute | solution.py:174
  252.2 33.8 %collective-permute-start.17 = (f32[128,1536]{1,0:T(8,128)}, f32[128,1536]{1,0:T(8,128)}, u32[]{:S(2)}, u32[]{:S(2)}) collective-permute-start(f32[128,1536]{1,0:T(8,128)} %collective-permute-done.15.refs_5_), channel_id=1, source_target_pairs={{0,6},{2,0},{4,2},{6,4},{1,7},{3,1},{5,3},{7,5},{8,14},{10,8},{12,... | collective-permute-start | bytes 2359304 | tf_op jit(solution)/shard_map/ppermute | solution.py:175
  344.4 14.4 %collective-permute-start.26 = (f32[3,512,256]{2,1,0:T(8,128)S(1)}, f32[3,512,256]{2,1,0:T(8,128)}, u32[]{:S(2)}, u32[]{:S(2)}) collective-permute-start(f32[3,512,256]{2,1,0:T(8,128)S(1)} %bitcast.89), channel_id=1, source_target_pairs={{0,1},{1,0},{2,3},{3,2},{4,5},{5,4},{6,7},{7,6},{8,9},{9,8},{10,11... | collective-permute-start | bytes 4718600 | tf_op jit(solution)/shard_map/ppermute | solution.py:228
  (27 other events, 313.1 us)

commit v7 on v5

--- a/solution.py
+++ b/solution.py
@@ -9,6 +9,7 @@
 
 
 BLOCK = 128
+LIMIT = 60 * 1024 * 1024
 ROW = ("xl", "z")
 COL = ("xh", "y", "core")
 PLANE = ("xh", "y")
@@ -51,16 +52,28 @@
     added_ref = refs.pop(0) if added else None
     out_ref = refs.pop(0)
     factor_ref = refs.pop(0) if kept else None
-    high_ref, low_ref = refs
+    high_ref, low_ref, stage_ref, sems = refs[:4]
+    taken_ref, taken_sems = refs[4:] if minus else (None, None)
+    size = pieces[0].shape[0]
 
     @pl.when(pl.program_id(0) == 0)
     def _():
-        for index, piece_ref in enumerate(pieces):
-            size = piece_ref.shape[0]
-            span = pl.ds(pl.multiple_of(place_ref[1 + index] * size, size), size)
-            value = piece_ref[...]
+        spans = [pl.ds(pl.multiple_of(place_ref[1 + index] * size, size), size) for index in range(8)]
+        copies = []
+        for index in range(8):
+            group = [pltpu.make_async_copy(pieces[index], stage_ref.at[index], sems.at[index])]
             if minus:
-                value = value - minus_ref[span, :]
+                group.append(pltpu.make_async_copy(
+                    minus_ref.at[spans[index], :], taken_ref.at[index], taken_sems.at[index]))
+            for copy in group:
+                copy.start()
+            copies.append(group)
+        for index, span in enumerate(spans):
+            for copy in copies[index]:
+                copy.wait()
+            value = stage_ref[index]
+            if minus:
+                value = value - taken_ref[index]
             high, low = split(value)
             if kept:
                 factor_ref[span, :] = value
@@ -80,13 +93,14 @@
     tile = rows // 12
     once = dict(pipeline_mode=pl.Buffered(1))
     whole = pl.BlockSpec((width, depth), lambda i, places: (0, 0), **once)
-    piece = pl.BlockSpec((width // 8, depth), lambda i, places: (0, 0), **once)
+    anywhere = pl.BlockSpec(memory_space=pl.ANY)
+    stage = [pltpu.VMEM((8, width // 8, depth), jnp.float32), pltpu.SemaphoreType.DMA((8,))]
     column = pl.BlockSpec((width, tile), lambda i, places: (0, i))
     operands, in_specs = [places, ancestor, *pieces], [
-        pl.BlockSpec((tile, depth), lambda i, places: (places[0] * 6 + i, 0)), *[piece] * 8]
+        pl.BlockSpec((tile, depth), lambda i, places: (places[0] * 6 + i, 0)), *[anywhere] * 8]
     if minus is not None:
         operands.append(minus)
-        in_specs.append(whole)
+        in_specs.append(anywhere)
     if added is not None:
         operands.append(added)
         in_specs.append(column)
@@ -101,13 +115,13 @@
             grid=(6,),
             in_specs=in_specs,
             out_specs=out_specs,
-            scratch_shapes=[pltpu.VMEM((width, depth), jnp.bfloat16)] * 2,
+            scratch_shapes=[pltpu.VMEM((width, depth), jnp.bfloat16)] * 2 + stage * (1 if minus is None else 2),
         ),
         out_shape=out_shape,
         cost_estimate=pl.CostEstimate(
             flops=3 * rows * depth * width, transcendentals=0,
             bytes_accessed=2 * rows * depth + 4 * width * depth + 2 * rows * width),
-        compiler_params=pltpu.CompilerParams(vmem_limit_bytes=40 * 1024 * 1024),
+        compiler_params=pltpu.CompilerParams(vmem_limit_bytes=LIMIT),
     )(*operands)
     return result if kept else result[0]
 
@@ -161,10 +175,11 @@
         own = lax.dynamic_slice_in_dim(mask, column_index * blocks, blocks).astype(jnp.float32)
         return shard.T * jnp.broadcast_to(own[:, None], (blocks, BLOCK)).reshape(1, depth)
 
-    def gathered(piece, side_axis, ring_axis):
+    def gathered(piece, side_axis, ring_axis, side=None):
         below = lax.ppermute(piece, ring_axis, up)
         above = lax.ppermute(piece, ring_axis, down)
-        side = lax.ppermute(piece, side_axis, SWAP)
+        if side is None:
+            side = lax.ppermute(piece, side_axis, SWAP)
         side_below = lax.ppermute(side, ring_axis, up)
         side_above = lax.ppermute(side, ring_axis, down)
         far = lax.ppermute(below, ring_axis, up)
@@ -197,8 +212,9 @@
     raw = lax.ppermute(jnp.concatenate([piece_one, piece_two]), ALL, raw_routes())
     row_pieces = gathered(raw, "xh", "y")
     link_base = lax.optimization_barrier(-product(diag_one, link_two))
-    piece_two, *pieces_one = lax.optimization_barrier((piece_two, *pieces_one))
-    pieces_two = gathered(piece_two, "xl", "z")
+    side_two = lax.ppermute(piece_two, "xl", SWAP)
+    piece_two, side_two, *pieces_one = lax.optimization_barrier((piece_two, side_two, *pieces_one))
+    pieces_two = gathered(piece_two, "xl", "z", side_two)
 
     send_one, factor_one = half_product(ancestor, pieces_one, other_places, kept=True)
     received_one = lax.ppermute(send_one, "core", SWAP)
@@ -221,9 +237,10 @@
     spread = spread.reshape(8, 8, 3, strip // 8, half).transpose(2, 1, 0, 3, 4).reshape(3, width, half)
     other = lax.ppermute(spread, "core", SWAP)
     sums = jnp.where(core == 0, jnp.concatenate([spread, other], 2), jnp.concatenate([other, spread], 2))
-    d_one = diag_one - sums[0].T
+    turned_one, turned_two = lax.optimization_barrier((sums[0].T, sums[2].T))
+    d_one = diag_one - turned_one
     link_inverse = link_base - sums[1] + product(sums[0], link_two, ((0,), (0,)))
-    d_two = diag_two - sums[2].T - product(link_two, link_inverse, ((0,), (0,)))
+    d_two = diag_two - turned_two - product(link_two, link_inverse, ((0,), (0,)))
     return (to_rows(x_one), d_one, to_rows(x_two), link_inverse, d_two)
 
 

time: 389 us -> 374 us (0.961)
  waiting for transfers between devices: 133 us -> 118 us
  local copies, waits for them, and re-layouts: 27.5 us -> 16.2 us
  Pallas kernels: 51 us -> 61.9 us
  starting transfers between devices: 109 us -> 105 us
    unnamed x68 -> x46, local copies, waits for them, and re-layouts: 26.7 us -> 13.2 us
    ppermute x3 -> x2, waiting for transfers between devices: 15.9 us -> 4.57 us  [gathered(): side = lax.ppermute(piece, side_axis, SWAP)]
    pallas_call x4, Pallas kernels: 48 us -> 58.9 us  [half_product(): pl.pallas_call(functools.partial(half_kernel, minus is not None, added is...]
    ppermute x3, waiting for transfers between devices: 10.6 us -> 0.01 us  [gathered(): side_far = lax.ppermute(side_above, ring_axis, down)]
    ppermute x3, waiting for transfers between devices: 23.1 us -> 33.1 us  [gathered(): far = lax.ppermute(below, ring_axis, up)]
    ppermute x3, waiting for transfers between devices: 50.1 us -> 57.7 us  [gathered(): below = lax.ppermute(piece, ring_axis, up)]
    ppermute x3, waiting for transfers between devices: 17.4 us -> 11.3 us  [gathered(): above = lax.ppermute(piece, ring_axis, down)]
    ppermute x3, waiting for transfers between devices: 11.3 us -> 5.23 us  [gathered(): side_above = lax.ppermute(side, ring_axis, down)]
  transfers between devices with their start and end apart: 30 -> 30, of which waited for: 16 -> 12; matrix products, arithmetic and copies ran while one was open for 6% -> 7% of each run, Pallas kernels for 10% -> 13%
where the time goes in v7:
time: 374 us; the launch traced here: 372 us
  waiting for transfers between devices  118 us (32%)
  starting transfers between devices  105 us (28%)
  Pallas kernels  61.9 us (17%)
  blocking collectives  37 us (10%)
  matrix products  20.4 us (5%)
  local copies, waits for them, and re-layouts  16.2 us (4%)
  other arithmetic  12.8 us (3%)
    pallas_call x4, Pallas kernels, half_product(): pl.pallas_call(functools.partial(half_kernel, minus is not None, added is...  58.9 us
    ppermute x3, waiting for transfers between devices, gathered(): below = lax.ppermute(piece, ring_axis, up)  57.7 us
    ppermute x2, starting transfers between devices, gathered(): side = lax.ppermute(piece, side_axis, SWAP)  56.2 us
    ppermute x3, waiting for transfers between devices, gathered(): far = lax.ppermute(below, ring_axis, up)  33.1 us
    all_to_all x1, blocking collectives, per_device(): lax.all_to_all(jnp.broadcast_to(piece[None], (64,) + piece.shape), CHIPS,...  27.9 us
    dot_general x7, matrix products, product(): lax.dot_general(left, right, (contract, ((), ())), precision=lax.Precisio...  20.4 us
    unnamed x46, local copies, waits for them, and re-layouts  13.2 us
    all_to_all x2, starting transfers between devices, scattered(): lax.all_to_all(chip.reshape(8, strip, rows // 2), PLANE, split_axis=0, co...  13.1 us
  transfers between devices with their start and end apart: 30, of which 12 were waited for; matrix products, arithmetic and copies ran while one was open for 7% of the time, Pallas kernels for 13%

profile of v7, /device:TPU:1, one launch (start us, length us, event | category | flops | bytes accessed | tf_op | source)
XLA Modules:
  0.0 372.1 jit_solution(5455916229446184354)
XLA Ops:
  8.6 4.6 %collective-permute-done.1.refs_1_ = f32[64,1536]{1,0:T(8,128)S(1)} collective-permute-done((f32[64,1536]{1,0:T(8,128)S(1)}, f32[64,1536]{1,0:T(8,128)S(1)}, u32[]{:S(2)}, u32[]{:S(2)}) %collective-permute-start.1) | collective-permute-done | bytes 393248 | tf_op jit(solution)/shard_map/ppermute | solution.py:182
  13.1 4.1 %collective-permute-start.5 = (f32[64,1536]{1,0:T(8,128)S(1)}, f32[64,1536]{1,0:T(8,128)}, u32[]{:S(2)}, u32[]{:S(2)}) collective-permute-start(f32[64,1536]{1,0:T(8,128)S(1)} %collective-permute-done.1.refs_1_), channel_id=1, source_target_pairs={{0,48},{16,0},{32,16},{48,32},{1,49},{17,1},{33,17},{49,33},{2,50}... | collective-permute-start | bytes 1179656 | tf_op jit(solution)/shard_map/ppermute | solution.py:184
  19.7 5.2 %collective-permute-done.5.refs_5_ = f32[64,1536]{1,0:T(8,128)} collective-permute-done((f32[64,1536]{1,0:T(8,128)S(1)}, f32[64,1536]{1,0:T(8,128)}, u32[]{:S(2)}, u32[]{:S(2)}) %collective-permute-start.5) | collective-permute-done | bytes 393248 | tf_op jit(solution)/shard_map/ppermute | solution.py:184
  29.5 8.4 %collective-permute-done.6.refs_6_ = f32[64,1536]{1,0:T(8,128)} collective-permute-done((f32[64,1536]{1,0:T(8,128)S(1)}, f32[64,1536]{1,0:T(8,128)}, u32[]{:S(2)}, u32[]{:S(2)}) %collective-permute-start.6) | collective-permute-done | bytes 393248 | tf_op jit(solution)/shard_map/ppermute | solution.py:185
  38.0 14.0 %shard_map.119 = (f32[512,1536]{1,0:T(8,128)}, f32[512,1536]{1,0:T(8,128)}) custom-call(s32[9]{0:T(128)} %stack.94.place_ref, f32[3072,1536]{1,0:T(8,128)} %a_ref.7, f32[64,1536]{1,0:T(8,128)} %copy-done.10, f32[64,1536]{1,0:T(8,128)} %copy-done.18, f32[64,1536]{1,0:T(8,128)} %copy-done.19, f32[64,1536]{1,0:T(8,128)} %copy-done.20, ...), custom_call_target="tpu_custom_call" | custom-call | flops 7247757312 | bytes 15728640 | tf_op jit(solution)/shard_map/pallas_call | solution.py:111
  52.0 3.0 collective-permute-start.8
  59.2 7.6 %collective-permute-done.18.refs_2_ = f32[64,1536]{1,0:T(8,128)S(1)} collective-permute-done((f32[64,1536]{1,0:T(8,128)S(1)}, f32[64,1536]{1,0:T(8,128)S(1)}, u32[]{:S(2)}, u32[]{:S(2)}) %collective-permute-start.18) | collective-permute-done | bytes 393248 | tf_op jit(solution)/shard_map/ppermute | solution.py:179
  69.5 6.3 %convolution_bitcast_fusion.refs_8_ = f32[512,1536]{1,0:T(8,128)} fusion(f32[512,1536]{1,0:T(8,128)} %get-tuple-element.34, f32[512,512]{1,0:T(8,128)S(1)} %copy-done), kind=kOutput, calls=%fused_computation | convolution fusion | flops 2415919104 | bytes 7340032 | tf_op jit(solution)/shard_map/dot_general | solution.py:23
  75.9 7.8 %collective-permute-done.22.refs_6_ = f32[64,1536]{1,0:T(8,128)S(1)} collective-permute-done((f32[64,1536]{1,0:T(8,128)S(1)}, f32[64,1536]{1,0:T(8,128)S(1)}, u32[]{:S(2)}, u32[]{:S(2)}) %collective-permute-start.22) | collective-permute-done | bytes 393248 | tf_op jit(solution)/shard_map/ppermute | solution.py:185
  84.5 15.0 %shard_map.122 = f32[512,1536]{1,0:T(8,128)} custom-call(s32[9]{0:T(128)} %stack.94.place_ref, f32[3072,1536]{1,0:T(8,128)} %a_ref.7, f32[64,1536]{1,0:T(8,128)} %copy-done.4, f32[64,1536]{1,0:T(8,128)} %copy-done.12, f32[64,1536]{1,0:T(8,128)} %copy-done.13, f32[64,1536]{1,0:T(8,128)} %copy-done.15, f32[64,1536]{1,0:T(8,128)} %copy-done.16, ...), custom_call_target="tpu_custom_call" | custom-call | flops 7247757312 | bytes 15728640 | tf_op jit(solution)/shard_map/pallas_call | solution.py:111
  101.3 14.5 %shard_map.120 = f32[512,1536]{1,0:T(8,128)} custom-call(s32[9]{0:T(128)} %stack.92.place_ref, f32[3072,1536]{1,0:T(8,128)} %a_ref.7, f32[64,1536]{1,0:T(8,128)} %copy-done.10, f32[64,1536]{1,0:T(8,128)} %copy-done.18, f32[64,1536]{1,0:T(8,128)} %copy-done.19, f32[64,1536]{1,0:T(8,128)} %copy-done.20, f32[64,1536]{1,0:T(8,128)} %collective-permute-done.4.refs_4_, ...), custom_call_target="tpu_custom_call" | custom-call | flops 7247757312 | bytes 15728640 | tf_op jit(solution)/shard_map/pallas_call | solution.py:111
  115.8 6.5 %all-to-all-start = ((f32[8,64,1536]{2,1,0:T(8,128)}), f32[8,64,1536]{2,1,0:T(8,128)}, u32[]{:S(2)}, u32[]{:S(2)}) async-start(f32[8,64,1536]{2,1,0:T(8,128)} %bitcast.82), calls=%async_computation | async-start | bytes 6291456 | tf_op jit(solution)/shard_map/all_to_all | solution.py:190
  123.1 54.1 %collective-permute-start.11 = (f32[128,1536]{1,0:T(8,128)S(1)}, f32[128,1536]{1,0:T(8,128)S(1)}, u32[]{:S(2)}, u32[]{:S(2)}) collective-permute-start(f32[128,1536]{1,0:T(8,128)S(1)} %collective-permute-done.10.refs_0_), channel_id=1, source_target_pairs={{0,8},{8,0},{1,9},{9,1},{2,10},{10,2},{3,11},{11,3},{4,12},{12,4},... | collective-permute-start | bytes 2359304 | tf_op jit(solution)/shard_map/ppermute | solution.py:182
  177.2 15.4 %shard_map.123 = f32[512,1536]{1,0:T(8,128)} custom-call(s32[9]{0:T(128)} %stack.92.place_ref, f32[3072,1536]{1,0:T(8,128)} %a_ref.7, f32[64,1536]{1,0:T(8,128)} %copy-done.4, f32[64,1536]{1,0:T(8,128)} %copy-done.12, f32[64,1536]{1,0:T(8,128)} %copy-done.13, f32[64,1536]{1,0:T(8,128)} %copy-done.15, f32[64,1536]{1,0:T(8,128)} %copy-done.16, ...), custom_call_target="tpu_custom_call" | custom-call | flops 7247757312 | bytes 15728640 | tf_op jit(solution)/shard_map/pallas_call | solution.py:111
  192.7 6.6 %all-to-all-start.1 = ((f32[8,64,1536]{2,1,0:T(8,128)}), f32[8,64,1536]{2,1,0:T(8,128)}, u32[]{:S(2)}, u32[]{:S(2)}) async-start(f32[8,64,1536]{2,1,0:T(8,128)} %bitcast.81), calls=%async_computation.1 | async-start | bytes 6291456 | tf_op jit(solution)/shard_map/all_to_all | solution.py:190
  204.1 50.1 %collective-permute-done.12.refs_2_ = f32[128,1536]{1,0:T(8,128)S(1)} collective-permute-done((f32[128,1536]{1,0:T(8,128)S(1)}, f32[128,1536]{1,0:T(8,128)S(1)}, u32[]{:S(2)}, u32[]{:S(2)}) %collective-permute-start.12) | collective-permute-done | bytes 786464 | tf_op jit(solution)/shard_map/ppermute | solution.py:179
  256.9 11.3 %collective-permute-done.13.refs_3_ = f32[128,1536]{1,0:T(8,128)} collective-permute-done((f32[128,1536]{1,0:T(8,128)S(1)}, f32[128,1536]{1,0:T(8,128)}, u32[]{:S(2)}, u32[]{:S(2)}) %collective-permute-start.13) | collective-permute-done | bytes 786464 | tf_op jit(solution)/shard_map/ppermute | solution.py:180
  271.1 16.9 %collective-permute-done.16.refs_6_ = f32[128,1536]{1,0:T(8,128)} collective-permute-done((f32[128,1536]{1,0:T(8,128)S(1)}, f32[128,1536]{1,0:T(8,128)}, u32[]{:S(2)}, u32[]{:S(2)}) %collective-permute-start.16) | collective-permute-done | bytes 786464 | tf_op jit(solution)/shard_map/ppermute | solution.py:185
  288.0 3.0 shard_map.121
  296.5 3.6 convolution_bitcast_fusion.4
  303.9 3.4 convolution_bitcast_fusion.2
  309.1 9.1 %all_to_all.20 = f32[8,3,8,256]{3,2,1,0:T(8,128)S(1)} all-to-all(f32[8,3,8,256]{3,2,1,0:T(8,128)S(1)} %copy_bitcast_fusion), channel_id=1, replica_groups=mesh['xl'=2,'z'=4,'xh'=2,'y'=4,'core'=2] {'xl','z'}, dimensions={0} | all-to-all | bytes 393216 | tf_op jit(solution)/shard_map/all_to_all | solution.py:234
  318.3 27.9 %all_to_all.21 = f32[64,3,8,256]{3,2,1,0:T(8,128)S(1)} all-to-all(f32[64,3,8,256]{3,2,1,0:T(8,128)S(1)} %broadcast_in_dim.8), channel_id=1, replica_groups=mesh['xl'=2,'z'=4,'xh'=2,'y'=4,'core'=2] {'xl','z','xh','y'}, dimensions={0} | all-to-all | bytes 3145728 | tf_op jit(solution)/shard_map/all_to_all | solution.py:235
  351.9 3.2 convolution_negate_fusion
  (122 shorter events, 69.3 us)
Async XLA Ops:
  2.6 10.5 %collective-permute-start.1 = (f32[64,1536]{1,0:T(8,128)S(1)}, f32[64,1536]{1,0:T(8,128)S(1)}, u32[]{:S(2)}, u32[]{:S(2)}) collective-permute-start(f32[64,1536]{1,0:T(8,128)S(1)} %multiply_bitcast_fusion.refs_0_), channel_id=1, source_target_pairs={{0,64},{64,0},{1,65},{65,1},{2,66},{66,2},{3,67},{67,3},{4,68},{68... | collective-permute-start | bytes 1179656 | tf_op jit(solution)/shard_map/ppermute | solution.py:182
  4.7 14.9 %collective-permute-start.2 = (f32[64,1536]{1,0:T(8,128)S(1)}, f32[64,1536]{1,0:T(8,128)S(1)}, u32[]{:S(2)}, u32[]{:S(2)}) collective-permute-start(f32[64,1536]{1,0:T(8,128)S(1)} %multiply_bitcast_fusion.refs_0_), channel_id=1, source_target_pairs={{0,16},{16,32},{32,48},{48,0},{1,17},{17,33},{33,49},{49,1},{2,18}... | collective-permute-start | bytes 1179656 | tf_op jit(solution)/shard_map/ppermute | solution.py:179
  6.4 22.0 %collective-permute-start.3 = (f32[64,1536]{1,0:T(8,128)S(1)}, f32[64,1536]{1,0:T(8,128)S(1)}, u32[]{:S(2)}, u32[]{:S(2)}) collective-permute-start(f32[64,1536]{1,0:T(8,128)S(1)} %multiply_bitcast_fusion.refs_0_), channel_id=1, source_target_pairs={{0,48},{16,0},{32,16},{48,32},{1,49},{17,1},{33,17},{49,33},{2,50}... | collective-permute-start | bytes 1179656 | tf_op jit(solution)/shard_map/ppermute | solution.py:180
  13.1 11.8 %collective-permute-start.5 = (f32[64,1536]{1,0:T(8,128)S(1)}, f32[64,1536]{1,0:T(8,128)}, u32[]{:S(2)}, u32[]{:S(2)}) collective-permute-start(f32[64,1536]{1,0:T(8,128)S(1)} %collective-permute-done.1.refs_1_), channel_id=1, source_target_pairs={{0,48},{16,0},{32,16},{48,32},{1,49},{17,1},{33,17},{49,33},{2,50}... | collective-permute-start | bytes 1179656 | tf_op jit(solution)/shard_map/ppermute | solution.py:184
  19.6 18.3 %collective-permute-start.6 = (f32[64,1536]{1,0:T(8,128)S(1)}, f32[64,1536]{1,0:T(8,128)}, u32[]{:S(2)}, u32[]{:S(2)}) collective-permute-start(f32[64,1536]{1,0:T(8,128)S(1)} %collective-permute-done.2.refs_2_), channel_id=1, source_target_pairs={{0,16},{16,32},{32,48},{48,0},{1,17},{17,33},{33,49},{49,1},{2,18}... | collective-permute-start | bytes 1179656 | tf_op jit(solution)/shard_map/ppermute | solution.py:185
  24.9 13.0 %collective-permute-start.7 = (f32[64,1536]{1,0:T(8,128)}, f32[64,1536]{1,0:T(8,128)}, u32[]{:S(2)}, u32[]{:S(2)}) collective-permute-start(f32[64,1536]{1,0:T(8,128)} %collective-permute-done.5.refs_5_), channel_id=1, source_target_pairs={{0,48},{16,0},{32,16},{48,32},{1,49},{17,1},{33,17},{49,33},{2,50}... | collective-permute-start | bytes 1179656 | tf_op jit(solution)/shard_map/ppermute | solution.py:186
  52.0 49.3 %collective-permute-start.8 = (f32[512,1536]{1,0:T(8,128)}, f32[512,1536]{1,0:T(8,128)}, u32[]{:S(2)}, u32[]{:S(2)}) collective-permute-start(f32[512,1536]{1,0:T(8,128)} %get-tuple-element.29), channel_id=1, source_target_pairs={{0,1},{1,0},{2,3},{3,2},{4,5},{5,4},{6,7},{7,6},{8,9},{9,8},{10,11... | collective-permute-start | bytes 9437192 | tf_op jit(solution)/shard_map/ppermute | solution.py:220
  55.0 11.8 %collective-permute-start.18 = (f32[64,1536]{1,0:T(8,128)S(1)}, f32[64,1536]{1,0:T(8,128)S(1)}, u32[]{:S(2)}, u32[]{:S(2)}) collective-permute-start(f32[64,1536]{1,0:T(8,128)S(1)} %multiply_bitcast_fusion.1.refs_0_), channel_id=1, source_target_pairs={{0,16},{16,32},{32,48},{48,0},{1,17},{17,33},{33,49},{49,1},{2,18}... | collective-permute-start | bytes 1179656 | tf_op jit(solution)/shard_map/ppermute | solution.py:179
  55.1 11.8 %collective-permute-start.21 = (f32[64,1536]{1,0:T(8,128)S(1)}, f32[64,1536]{1,0:T(8,128)S(1)}, u32[]{:S(2)}, u32[]{:S(2)}) collective-permute-start(f32[64,1536]{1,0:T(8,128)S(1)} %collective-permute-done.refs_1_), channel_id=1, source_target_pairs={{0,48},{16,0},{32,16},{48,32},{1,49},{17,1},{33,17},{49,33},{2,50}... | collective-permute-start | bytes 1179656 | tf_op jit(solution)/shard_map/ppermute | solution.py:184
  57.7 18.1 %collective-permute-start.19 = (f32[64,1536]{1,0:T(8,128)S(1)}, f32[64,1536]{1,0:T(8,128)S(1)}, u32[]{:S(2)}, u32[]{:S(2)}) collective-permute-start(f32[64,1536]{1,0:T(8,128)S(1)} %multiply_bitcast_fusion.1.refs_0_), channel_id=1, source_target_pairs={{0,48},{16,0},{32,16},{48,32},{1,49},{17,1},{33,17},{49,33},{2,50}... | collective-permute-start | bytes 1179656 | tf_op jit(solution)/shard_map/ppermute | solution.py:180
  57.8 18.1 %collective-permute-start.20 = (f32[64,1536]{1,0:T(8,128)S(1)}, f32[64,1536]{1,0:T(8,128)S(1)}, u32[]{:S(2)}, u32[]{:S(2)}) collective-permute-start(f32[64,1536]{1,0:T(8,128)S(1)} %collective-permute-done.refs_1_), channel_id=1, source_target_pairs={{0,16},{16,32},{32,48},{48,0},{1,17},{17,33},{33,49},{49,1},{2,18}... | collective-permute-start | bytes 1179656 | tf_op jit(solution)/shard_map/ppermute | solution.py:183
  66.8 16.9 %collective-permute-start.22 = (f32[64,1536]{1,0:T(8,128)S(1)}, f32[64,1536]{1,0:T(8,128)S(1)}, u32[]{:S(2)}, u32[]{:S(2)}) collective-permute-start(f32[64,1536]{1,0:T(8,128)S(1)} %collective-permute-done.18.refs_2_), channel_id=1, source_target_pairs={{0,16},{16,32},{32,48},{48,0},{1,17},{17,33},{33,49},{49,1},{2,18}... | collective-permute-start | bytes 1179656 | tf_op jit(solution)/shard_map/ppermute | solution.py:185
  66.9 16.8 %collective-permute-start.23 = (f32[64,1536]{1,0:T(8,128)S(1)}, f32[64,1536]{1,0:T(8,128)}, u32[]{:S(2)}, u32[]{:S(2)}) collective-permute-start(f32[64,1536]{1,0:T(8,128)S(1)} %collective-permute-done.21.refs_5_), channel_id=1, source_target_pairs={{0,48},{16,0},{32,16},{48,32},{1,49},{17,1},{33,17},{49,33},{2,50}... | collective-permute-start | bytes 1179656 | tf_op jit(solution)/shard_map/ppermute | solution.py:186
  99.5 77.8 %collective-permute-start.24 = (f32[512,1536]{1,0:T(8,128)}, f32[512,1536]{1,0:T(8,128)}, u32[]{:S(2)}, u32[]{:S(2)}) collective-permute-start(f32[512,1536]{1,0:T(8,128)} %shard_map.122), channel_id=1, source_target_pairs={{0,1},{1,0},{2,3},{3,2},{4,5},{5,4},{6,7},{7,6},{8,9},{9,8},{10,11... | collective-permute-start | bytes 9437192 | tf_op jit(solution)/shard_map/ppermute | solution.py:225
  115.8 76.8 %all-to-all-start = ((f32[8,64,1536]{2,1,0:T(8,128)}), f32[8,64,1536]{2,1,0:T(8,128)}, u32[]{:S(2)}, u32[]{:S(2)}) async-start(f32[8,64,1536]{2,1,0:T(8,128)} %bitcast.82), calls=%async_computation | async-start | bytes 6291456 | tf_op jit(solution)/shard_map/all_to_all | solution.py:190
  123.1 77.6 %collective-permute-start.11 = (f32[128,1536]{1,0:T(8,128)S(1)}, f32[128,1536]{1,0:T(8,128)S(1)}, u32[]{:S(2)}, u32[]{:S(2)}) collective-permute-start(f32[128,1536]{1,0:T(8,128)S(1)} %collective-permute-done.10.refs_0_), channel_id=1, source_target_pairs={{0,8},{8,0},{1,9},{9,1},{2,10},{10,2},{3,11},{11,3},{4,12},{12,4},... | collective-permute-start | bytes 2359304 | tf_op jit(solution)/shard_map/ppermute | solution.py:182
  192.7 109.1 %all-to-all-start.1 = ((f32[8,64,1536]{2,1,0:T(8,128)}), f32[8,64,1536]{2,1,0:T(8,128)}, u32[]{:S(2)}, u32[]{:S(2)}) async-start(f32[8,64,1536]{2,1,0:T(8,128)} %bitcast.81), calls=%async_computation.1 | async-start | bytes 6291456 | tf_op jit(solution)/shard_map/all_to_all | solution.py:190
  199.3 54.9 %collective-permute-start.12 = (f32[128,1536]{1,0:T(8,128)S(1)}, f32[128,1536]{1,0:T(8,128)S(1)}, u32[]{:S(2)}, u32[]{:S(2)}) collective-permute-start(f32[128,1536]{1,0:T(8,128)S(1)} %collective-permute-done.10.refs_0_), channel_id=1, source_target_pairs={{0,2},{2,4},{4,6},{6,0},{1,3},{3,5},{5,7},{7,1},{8,10},{10,12},{12... | collective-permute-start | bytes 2359304 | tf_op jit(solution)/shard_map/ppermute | solution.py:179
  200.7 53.4 %collective-permute-start.15 = (f32[128,1536]{1,0:T(8,128)S(1)}, f32[128,1536]{1,0:T(8,128)}, u32[]{:S(2)}, u32[]{:S(2)}) collective-permute-start(f32[128,1536]{1,0:T(8,128)S(1)} %collective-permute-done.11.refs_1_), channel_id=1, source_target_pairs={{0,6},{2,0},{4,2},{6,4},{1,7},{3,1},{5,3},{7,5},{8,14},{10,8},{12,... | collective-permute-start | bytes 2359304 | tf_op jit(solution)/shard_map/ppermute | solution.py:184
  202.6 65.6 %collective-permute-start.13 = (f32[128,1536]{1,0:T(8,128)S(1)}, f32[128,1536]{1,0:T(8,128)}, u32[]{:S(2)}, u32[]{:S(2)}) collective-permute-start(f32[128,1536]{1,0:T(8,128)S(1)} %collective-permute-done.10.refs_0_), channel_id=1, source_target_pairs={{0,6},{2,0},{4,2},{6,4},{1,7},{3,1},{5,3},{7,5},{8,14},{10,8},{12,... | collective-permute-start | bytes 2359304 | tf_op jit(solution)/shard_map/ppermute | solution.py:180
  204.0 67.1 %collective-permute-start.14 = (f32[128,1536]{1,0:T(8,128)S(1)}, f32[128,1536]{1,0:T(8,128)}, u32[]{:S(2)}, u32[]{:S(2)}) collective-permute-start(f32[128,1536]{1,0:T(8,128)S(1)} %collective-permute-done.11.refs_1_), channel_id=1, source_target_pairs={{0,2},{2,4},{4,6},{6,0},{1,3},{3,5},{5,7},{7,1},{8,10},{10,12},{12... | collective-permute-start | bytes 2359304 | tf_op jit(solution)/shard_map/ppermute | solution.py:183
  254.2 33.8 %collective-permute-start.16 = (f32[128,1536]{1,0:T(8,128)S(1)}, f32[128,1536]{1,0:T(8,128)}, u32[]{:S(2)}, u32[]{:S(2)}) collective-permute-start(f32[128,1536]{1,0:T(8,128)S(1)} %collective-permute-done.12.refs_2_), channel_id=1, source_target_pairs={{0,2},{2,4},{4,6},{6,0},{1,3},{3,5},{5,7},{7,1},{8,10},{10,12},{12... | collective-permute-start | bytes 2359304 | tf_op jit(solution)/shard_map/ppermute | solution.py:185
  254.2 33.8 %collective-permute-start.17 = (f32[128,1536]{1,0:T(8,128)}, f32[128,1536]{1,0:T(8,128)}, u32[]{:S(2)}, u32[]{:S(2)}) collective-permute-start(f32[128,1536]{1,0:T(8,128)} %collective-permute-done.15.refs_5_), channel_id=1, source_target_pairs={{0,6},{2,0},{4,2},{6,4},{1,7},{3,1},{5,3},{7,5},{8,14},{10,8},{12,... | collective-permute-start | bytes 2359304 | tf_op jit(solution)/shard_map/ppermute | solution.py:186
  346.4 14.4 %collective-permute-start.26 = (f32[3,512,256]{2,1,0:T(8,128)S(1)}, f32[3,512,256]{2,1,0:T(8,128)}, u32[]{:S(2)}, u32[]{:S(2)}) collective-permute-start(f32[3,512,256]{2,1,0:T(8,128)S(1)} %bitcast.84), channel_id=1, source_target_pairs={{0,1},{1,0},{2,3},{3,2},{4,5},{5,4},{6,7},{7,6},{8,9},{9,8},{10,11... | collective-permute-start | bytes 4718600 | tf_op jit(solution)/shard_map/ppermute | solution.py:238
  (27 other events, 313.5 us)

commit v8 on v5

--- a/solution.py
+++ b/solution.py
@@ -9,6 +9,7 @@
 
 
 BLOCK = 128
+LIMIT = 32 * 1024 * 1024
 ROW = ("xl", "z")
 COL = ("xh", "y", "core")
 PLANE = ("xh", "y")
@@ -44,14 +45,19 @@
     return high, (value - high.astype(jnp.float32)).astype(jnp.bfloat16)
 
 
-def half_kernel(minus, added, kept, place_ref, a_ref, *refs):
+def multiply(a_ref, high_ref, low_ref):
+    a_high, a_low = split(a_ref[...])
+    dims = (((1,), (1,)), ((), ()))
+    dot = lambda l, r: lax.dot_general(l, r, dims, preferred_element_type=jnp.float32)
+    return dot(high_ref[...], a_high) + dot(low_ref[...], a_high) + dot(high_ref[...], a_low)
+
+
+def first_kernel(minus, kept, place_ref, a_ref, *refs):
     refs = list(refs)
     pieces = [refs.pop(0) for _ in range(8)]
     minus_ref = refs.pop(0) if minus else None
-    added_ref = refs.pop(0) if added else None
-    out_ref = refs.pop(0)
-    factor_ref = refs.pop(0) if kept else None
-    high_ref, low_ref = refs
+    out_ref, high_ref, low_ref = refs[:3]
+    factor_ref = refs[3] if kept else None
 
     @pl.when(pl.program_id(0) == 0)
     def _():
@@ -67,49 +73,45 @@
             high_ref[span, :] = high
             low_ref[span, :] = low
 
-    a_high, a_low = split(a_ref[...])
-    dims = (((1,), (1,)), ((), ()))
-    dot = lambda l, r: lax.dot_general(l, r, dims, preferred_element_type=jnp.float32)
-    total = dot(high_ref[...], a_high) + dot(low_ref[...], a_high) + dot(high_ref[...], a_low)
-    out_ref[...] = total + added_ref[...] if added else total
-
-
-def half_product(ancestor, pieces, places, minus=None, added=None, kept=False):
+    out_ref[...] = multiply(a_ref, high_ref, low_ref)
+
+
+def second_kernel(place_ref, a_ref, high_ref, low_ref, added_ref, out_ref):
+    del place_ref
+    out_ref[...] = multiply(a_ref, high_ref, low_ref) + added_ref[...]
+
+
+def half_product(ancestor, places, pieces=None, minus=None, kept=False, parts=None, added=None):
     rows, depth = ancestor.shape
-    width = 8 * pieces[0].shape[0]
+    width = 8 * pieces[0].shape[0] if pieces else parts[0].shape[0]
     tile = rows // 12
     once = dict(pipeline_mode=pl.Buffered(1))
     whole = pl.BlockSpec((width, depth), lambda i, places: (0, 0), **once)
     piece = pl.BlockSpec((width // 8, depth), lambda i, places: (0, 0), **once)
     column = pl.BlockSpec((width, tile), lambda i, places: (0, i))
-    operands, in_specs = [places, ancestor, *pieces], [
-        pl.BlockSpec((tile, depth), lambda i, places: (places[0] * 6 + i, 0)), *[piece] * 8]
-    if minus is not None:
-        operands.append(minus)
-        in_specs.append(whole)
-    if added is not None:
-        operands.append(added)
-        in_specs.append(column)
+    in_specs = [pl.BlockSpec((tile, depth), lambda i, places: (places[0] * 6 + i, 0))]
     out_shape, out_specs = [jax.ShapeDtypeStruct((width, rows // 2), jnp.float32)], [column]
-    if kept:
-        out_shape.append(jax.ShapeDtypeStruct((width, depth), jnp.float32))
-        out_specs.append(whole)
-    result = pl.pallas_call(
-        functools.partial(half_kernel, minus is not None, added is not None, kept),
+    if pieces:
+        kernel = functools.partial(first_kernel, minus is not None, kept)
+        operands = [*pieces] + ([] if minus is None else [minus])
+        in_specs += [piece] * 8 + ([] if minus is None else [whole])
+        for kind in [jnp.bfloat16, jnp.bfloat16] + [jnp.float32] * kept:
+            out_shape.append(jax.ShapeDtypeStruct((width, depth), kind))
+            out_specs.append(whole)
+    else:
+        kernel = second_kernel
+        operands = [*parts, added]
+        in_specs += [whole, whole, column]
+    return pl.pallas_call(
+        kernel,
         grid_spec=pltpu.PrefetchScalarGridSpec(
-            num_scalar_prefetch=1,
-            grid=(6,),
-            in_specs=in_specs,
-            out_specs=out_specs,
-            scratch_shapes=[pltpu.VMEM((width, depth), jnp.bfloat16)] * 2,
-        ),
+            num_scalar_prefetch=1, grid=(6,), in_specs=in_specs, out_specs=out_specs),
         out_shape=out_shape,
         cost_estimate=pl.CostEstimate(
             flops=3 * rows * depth * width, transcendentals=0,
             bytes_accessed=2 * rows * depth + 4 * width * depth + 2 * rows * width),
-        compiler_params=pltpu.CompilerParams(vmem_limit_bytes=40 * 1024 * 1024),
-    )(*operands)
-    return result if kept else result[0]
+        compiler_params=pltpu.CompilerParams(vmem_limit_bytes=LIMIT),
+    )(places, ancestor, *operands)
 
 
 def order_kernel(place_ref, *refs):
@@ -200,14 +202,14 @@
     piece_two, *pieces_one = lax.optimization_barrier((piece_two, *pieces_one))
     pieces_two = gathered(piece_two, "xl", "z")
 
-    send_one, factor_one = half_product(ancestor, pieces_one, other_places, kept=True)
+    send_one, *parts_one, factor_one = half_product(ancestor, other_places, pieces_one, kept=True)
     received_one = lax.ppermute(send_one, "core", SWAP)
-    chip_one = half_product(ancestor, pieces_one, own_places, added=received_one)
+    (chip_one,) = half_product(ancestor, own_places, parts=parts_one, added=received_one)
     x_one = scattered(chip_one)
     mixed = product(link_two, factor_one, ((0,), (0,)))
-    send_two = half_product(ancestor, pieces_two, other_places, minus=mixed)
+    send_two, *parts_two = half_product(ancestor, other_places, pieces_two, minus=mixed)
     received_two = lax.ppermute(send_two, "core", SWAP)
-    chip_two = half_product(ancestor, pieces_two, own_places, minus=mixed, added=received_two)
+    (chip_two,) = half_product(ancestor, own_places, parts=parts_two, added=received_two)
     x_two = scattered(chip_two)
 
     rows_one, rows_two = ordered(row_pieces, plane_places)

time: 389 us -> 384 us (0.987)
    unnamed x68 -> x52, local copies, waits for them, and re-layouts: 26.7 us -> 25.5 us
where the time goes in v8:
time: 384 us; the launch traced here: 383 us
  waiting for transfers between devices  132 us (34%)
  starting transfers between devices  108 us (28%)
  Pallas kernels  49.8 us (13%)
  blocking collectives  37.1 us (10%)
  local copies, waits for them, and re-layouts  26.3 us (7%)
  matrix products  16.9 us (4%)
  other arithmetic  11.4 us (3%)
    ppermute x3, starting transfers between devices, gathered(): side = lax.ppermute(piece, side_axis, SWAP)  57.5 us
    ppermute x3, waiting for transfers between devices, gathered(): below = lax.ppermute(piece, ring_axis, up)  50.1 us
    pallas_call x4, Pallas kernels, half_product(): pl.pallas_call(kernel, grid_spec=pltpu.PrefetchScalarGridSpec(num_scalar_...  46.8 us
    all_to_all x1, blocking collectives, per_device(): lax.all_to_all(jnp.broadcast_to(piece[None], (64,) + piece.shape), CHIPS,...  27.9 us
    unnamed x52, local copies, waits for them, and re-layouts  25.5 us
    ppermute x3, waiting for transfers between devices, gathered(): far = lax.ppermute(below, ring_axis, up)  22.4 us
    dot_general x7, matrix products, product(): lax.dot_general(left, right, (contract, ((), ())), precision=lax.Precisio...  16.9 us
    ppermute x3, waiting for transfers between devices, gathered(): above = lax.ppermute(piece, ring_axis, down)  16.6 us
  transfers between devices with their start and end apart: 30, of which 16 were waited for; matrix products, arithmetic and copies ran while one was open for 6% of the time, Pallas kernels for 10%

profile of v8, /device:TPU:1, one launch (start us, length us, event | category | flops | bytes accessed | tf_op | source)
XLA Modules:
  0.0 382.8 jit_solution(16819324905767379415)
XLA Ops:
  6.4 6.8 %collective-permute-done.refs_1_ = f32[64,1536]{1,0:T(8,128)S(1)} collective-permute-done((f32[64,1536]{1,0:T(8,128)S(1)}, f32[64,1536]{1,0:T(8,128)S(1)}, u32[]{:S(2)}, u32[]{:S(2)}) %collective-permute-start) | collective-permute-done | bytes 393248 | tf_op jit(solution)/shard_map/ppermute | solution.py:169
  13.1 4.1 %collective-permute-start.4 = (f32[64,1536]{1,0:T(8,128)S(1)}, f32[64,1536]{1,0:T(8,128)S(1)}, u32[]{:S(2)}, u32[]{:S(2)}) collective-permute-start(f32[64,1536]{1,0:T(8,128)S(1)} %collective-permute-done.refs_1_), channel_id=1, source_target_pairs={{0,48},{16,0},{32,16},{48,32},{1,49},{17,1},{33,17},{49,33},{2,50}... | collective-permute-start | bytes 1179656 | tf_op jit(solution)/shard_map/ppermute | solution.py:171
  19.0 5.2 %collective-permute-done.4.refs_5_ = f32[64,1536]{1,0:T(8,128)S(1)} collective-permute-done((f32[64,1536]{1,0:T(8,128)S(1)}, f32[64,1536]{1,0:T(8,128)S(1)}, u32[]{:S(2)}, u32[]{:S(2)}) %collective-permute-start.4) | collective-permute-done | bytes 393248 | tf_op jit(solution)/shard_map/ppermute | solution.py:171
  24.2 3.4 collective-permute-start.6
  35.8 5.3 %collective-permute-done.6.refs_7_ = f32[64,1536]{1,0:T(8,128)S(1)} collective-permute-done((f32[64,1536]{1,0:T(8,128)S(1)}, f32[64,1536]{1,0:T(8,128)S(1)}, u32[]{:S(2)}, u32[]{:S(2)}) %collective-permute-start.6) | collective-permute-done | bytes 393248 | tf_op jit(solution)/shard_map/ppermute | solution.py:173
  45.1 12.5 %shard_map.119 = (f32[512,1536]{1,0:T(8,128)}, bf16[512,1536]{1,0:T(8,128)(2,1)S(1)}, bf16[512,1536]{1,0:T(8,128)(2,1)S(1)}, f32[512,1536]{1,0:T(8,128)S(1)}) custom-call(s32[9]{0:T(128)S(1)} %stack.94.place_ref, f32[3072,1536]{1,0:T(8,128)} %a_ref.7, f32[64,1536]{1,0:T(8,128)S(1)} %multiply_bitcast_fusion.refs_0_, f32[64,1536]{1,0:T(8,128)S(1)} %copy-done.13, ...), custom_call_target="tpu_custom_call" | custom-call | flops 7247757312 | bytes 15728640 | tf_op jit(solution)/shard_map/pallas_call | solution.py:105
  61.4 9.2 %collective-permute-done.17.refs_1_ = f32[64,1536]{1,0:T(8,128)S(1)} collective-permute-done((f32[64,1536]{1,0:T(8,128)S(1)}, f32[64,1536]{1,0:T(8,128)S(1)}, u32[]{:S(2)}, u32[]{:S(2)}) %collective-permute-start.17) | collective-permute-done | bytes 393248 | tf_op jit(solution)/shard_map/ppermute | solution.py:169
  70.6 3.4 collective-permute-start.21
  75.5 6.1 %collective-permute-done.21.refs_5_ = f32[64,1536]{1,0:T(8,128)S(1)} collective-permute-done((f32[64,1536]{1,0:T(8,128)S(1)}, f32[64,1536]{1,0:T(8,128)S(1)}, u32[]{:S(2)}, u32[]{:S(2)}) %collective-permute-start.21) | collective-permute-done | bytes 393248 | tf_op jit(solution)/shard_map/ppermute | solution.py:171
  81.7 3.4 collective-permute-start.23
  93.2 5.3 %collective-permute-done.23.refs_7_ = f32[64,1536]{1,0:T(8,128)S(1)} collective-permute-done((f32[64,1536]{1,0:T(8,128)S(1)}, f32[64,1536]{1,0:T(8,128)S(1)}, u32[]{:S(2)}, u32[]{:S(2)}) %collective-permute-start.23) | collective-permute-done | bytes 393248 | tf_op jit(solution)/shard_map/ppermute | solution.py:173
  98.5 12.4 %shard_map.122 = (f32[512,1536]{1,0:T(8,128)}, bf16[512,1536]{1,0:T(8,128)(2,1)S(1)}, bf16[512,1536]{1,0:T(8,128)(2,1)S(1)}) custom-call(s32[9]{0:T(128)S(1)} %stack.94.place_ref, f32[3072,1536]{1,0:T(8,128)} %a_ref.7, f32[64,1536]{1,0:T(8,128)S(1)} %multiply_bitcast_fusion.1.refs_0_, f32[64,1536]{1,0:T(8,128)S(1)} %collective-permute-done.17.refs_1_, ...), custom_call_target="tpu_custom_call" | custom-call | flops 7247757312 | bytes 15728640 | tf_op jit(solution)/shard_map/pallas_call | solution.py:105
  116.4 11.0 %shard_map.120 = f32[512,1536]{1,0:T(8,128)S(1)} custom-call(s32[9]{0:T(128)S(1)} %stack.92.place_ref, f32[3072,1536]{1,0:T(8,128)} %a_ref.7, bf16[512,1536]{1,0:T(8,128)(2,1)S(1)} %get-tuple-element.31.high_ref, bf16[512,1536]{1,0:T(8,128)(2,1)S(1)} %copy-done.7, f32[512,1536]{1,0:T(8,128)} %collective-permute-done.7.added_ref), custom_call_target="tpu_custom_call" | custom-call | flops 7247757312 | bytes 15728640 | tf_op jit(solution)/shard_map/pallas_call | solution.py:105
  129.1 6.8 %all-to-all-start = ((f32[8,64,1536]{2,1,0:T(8,128)}), f32[8,64,1536]{2,1,0:T(8,128)}, u32[]{:S(2)}, u32[]{:S(2)}) async-start(f32[8,64,1536]{2,1,0:T(8,128)} %bitcast.84), calls=%async_computation | async-start | bytes 6291456 | tf_op jit(solution)/shard_map/all_to_all | solution.py:177
  136.7 54.1 %collective-permute-start.10 = (f32[128,1536]{1,0:T(8,128)S(1)}, f32[128,1536]{1,0:T(8,128)}, u32[]{:S(2)}, u32[]{:S(2)}) collective-permute-start(f32[128,1536]{1,0:T(8,128)S(1)} %collective-permute-done.9.refs_0_), channel_id=1, source_target_pairs={{0,8},{8,0},{1,9},{9,1},{2,10},{10,2},{3,11},{11,3},{4,12},{12,4},... | collective-permute-start | bytes 2359304 | tf_op jit(solution)/shard_map/ppermute | solution.py:169
  192.2 11.0 %shard_map.123 = f32[512,1536]{1,0:T(8,128)S(1)} custom-call(s32[9]{0:T(128)S(1)} %stack.92.place_ref, f32[3072,1536]{1,0:T(8,128)} %a_ref.7, bf16[512,1536]{1,0:T(8,128)(2,1)S(1)} %copy-done.9, bf16[512,1536]{1,0:T(8,128)(2,1)S(1)} %copy-done.11, f32[512,1536]{1,0:T(8,128)} %collective-permute-done.24.added_ref), custom_call_target="tpu_custom_call" | custom-call | flops 7247757312 | bytes 15728640 | tf_op jit(solution)/shard_map/pallas_call | solution.py:105
  204.9 8.2 %all-to-all-start.1 = ((f32[8,64,1536]{2,1,0:T(8,128)}), f32[8,64,1536]{2,1,0:T(8,128)}, u32[]{:S(2)}, u32[]{:S(2)}) async-start(f32[8,64,1536]{2,1,0:T(8,128)} %bitcast.83), calls=%async_computation.1 | async-start | bytes 6291456 | tf_op jit(solution)/shard_map/all_to_all | solution.py:177
  217.9 50.1 %collective-permute-done.11.refs_2_ = f32[128,1536]{1,0:T(8,128)S(1)} collective-permute-done((f32[128,1536]{1,0:T(8,128)S(1)}, f32[128,1536]{1,0:T(8,128)S(1)}, u32[]{:S(2)}, u32[]{:S(2)}) %collective-permute-start.11) | collective-permute-done | bytes 786464 | tf_op jit(solution)/shard_map/ppermute | solution.py:167
  270.7 11.1 %collective-permute-done.12.refs_3_ = f32[128,1536]{1,0:T(8,128)} collective-permute-done((f32[128,1536]{1,0:T(8,128)S(1)}, f32[128,1536]{1,0:T(8,128)}, u32[]{:S(2)}, u32[]{:S(2)}) %collective-permute-start.12) | collective-permute-done | bytes 786464 | tf_op jit(solution)/shard_map/ppermute | solution.py:168
  284.9 16.9 %collective-permute-done.15.refs_6_ = f32[128,1536]{1,0:T(8,128)} collective-permute-done((f32[128,1536]{1,0:T(8,128)S(1)}, f32[128,1536]{1,0:T(8,128)}, u32[]{:S(2)}, u32[]{:S(2)}) %collective-permute-start.15) | collective-permute-done | bytes 786464 | tf_op jit(solution)/shard_map/ppermute | solution.py:172
  310.3 3.6 convolution_bitcast_fusion.4
  317.7 3.4 convolution_bitcast_fusion.2
  322.8 9.2 %all_to_all.20 = f32[8,3,8,256]{3,2,1,0:T(8,128)S(1)} all-to-all(f32[8,3,8,256]{3,2,1,0:T(8,128)S(1)} %copy_bitcast_fusion), channel_id=1, replica_groups=mesh['xl'=2,'z'=4,'xh'=2,'y'=4,'core'=2] {'xl','z'}, dimensions={0} | all-to-all | bytes 393216 | tf_op jit(solution)/shard_map/all_to_all | solution.py:220
  332.2 27.9 %all_to_all.21 = f32[64,3,8,256]{3,2,1,0:T(8,128)S(1)} all-to-all(f32[64,3,8,256]{3,2,1,0:T(8,128)S(1)} %broadcast_in_dim.8), channel_id=1, replica_groups=mesh['xl'=2,'z'=4,'xh'=2,'y'=4,'core'=2] {'xl','z','xh','y'}, dimensions={0} | all-to-all | bytes 3145728 | tf_op jit(solution)/shard_map/all_to_all | solution.py:221
  (126 shorter events, 91.5 us)
Async XLA Ops:
  4.7 14.2 %collective-permute-start.1 = (f32[64,1536]{1,0:T(8,128)S(1)}, f32[64,1536]{1,0:T(8,128)S(1)}, u32[]{:S(2)}, u32[]{:S(2)}) collective-permute-start(f32[64,1536]{1,0:T(8,128)S(1)} %multiply_bitcast_fusion.refs_0_), channel_id=1, source_target_pairs={{0,16},{16,32},{32,48},{48,0},{1,17},{17,33},{33,49},{49,1},{2,18}... | collective-permute-start | bytes 1179656 | tf_op jit(solution)/shard_map/ppermute | solution.py:167
  13.1 11.1 %collective-permute-start.4 = (f32[64,1536]{1,0:T(8,128)S(1)}, f32[64,1536]{1,0:T(8,128)S(1)}, u32[]{:S(2)}, u32[]{:S(2)}) collective-permute-start(f32[64,1536]{1,0:T(8,128)S(1)} %collective-permute-done.refs_1_), channel_id=1, source_target_pairs={{0,48},{16,0},{32,16},{48,32},{1,49},{17,1},{33,17},{49,33},{2,50}... | collective-permute-start | bytes 1179656 | tf_op jit(solution)/shard_map/ppermute | solution.py:171
  17.3 15.4 %collective-permute-start.2 = (f32[64,1536]{1,0:T(8,128)S(1)}, f32[64,1536]{1,0:T(8,128)S(1)}, u32[]{:S(2)}, u32[]{:S(2)}) collective-permute-start(f32[64,1536]{1,0:T(8,128)S(1)} %multiply_bitcast_fusion.refs_0_), channel_id=1, source_target_pairs={{0,48},{16,0},{32,16},{48,32},{1,49},{17,1},{33,17},{49,33},{2,50}... | collective-permute-start | bytes 1179656 | tf_op jit(solution)/shard_map/ppermute | solution.py:168
  17.6 15.8 %collective-permute-start.3 = (f32[64,1536]{1,0:T(8,128)S(1)}, f32[64,1536]{1,0:T(8,128)S(1)}, u32[]{:S(2)}, u32[]{:S(2)}) collective-permute-start(f32[64,1536]{1,0:T(8,128)S(1)} %collective-permute-done.refs_1_), channel_id=1, source_target_pairs={{0,16},{16,32},{32,48},{48,0},{1,17},{17,33},{33,49},{49,1},{2,18}... | collective-permute-start | bytes 1179656 | tf_op jit(solution)/shard_map/ppermute | solution.py:170
  18.9 16.9 %collective-permute-start.5 = (f32[64,1536]{1,0:T(8,128)S(1)}, f32[64,1536]{1,0:T(8,128)S(1)}, u32[]{:S(2)}, u32[]{:S(2)}) collective-permute-start(f32[64,1536]{1,0:T(8,128)S(1)} %collective-permute-done.1.refs_2_), channel_id=1, source_target_pairs={{0,16},{16,32},{32,48},{48,0},{1,17},{17,33},{33,49},{49,1},{2,18}... | collective-permute-start | bytes 1179656 | tf_op jit(solution)/shard_map/ppermute | solution.py:172
  24.2 16.9 %collective-permute-start.6 = (f32[64,1536]{1,0:T(8,128)S(1)}, f32[64,1536]{1,0:T(8,128)S(1)}, u32[]{:S(2)}, u32[]{:S(2)}) collective-permute-start(f32[64,1536]{1,0:T(8,128)S(1)} %collective-permute-done.4.refs_5_), channel_id=1, source_target_pairs={{0,48},{16,0},{32,16},{48,32},{1,49},{17,1},{33,17},{49,33},{2,50}... | collective-permute-start | bytes 1179656 | tf_op jit(solution)/shard_map/ppermute | solution.py:173
  57.6 57.4 %collective-permute-start.7 = (f32[512,1536]{1,0:T(8,128)}, f32[512,1536]{1,0:T(8,128)}, u32[]{:S(2)}, u32[]{:S(2)}) collective-permute-start(f32[512,1536]{1,0:T(8,128)} %get-tuple-element.33), channel_id=1, source_target_pairs={{0,1},{1,0},{2,3},{3,2},{4,5},{5,4},{6,7},{7,6},{8,9},{9,8},{10,11... | collective-permute-start | bytes 9437192 | tf_op jit(solution)/shard_map/ppermute | solution.py:206
  61.2 14.3 %collective-permute-start.18 = (f32[64,1536]{1,0:T(8,128)S(1)}, f32[64,1536]{1,0:T(8,128)S(1)}, u32[]{:S(2)}, u32[]{:S(2)}) collective-permute-start(f32[64,1536]{1,0:T(8,128)S(1)} %multiply_bitcast_fusion.1.refs_0_), channel_id=1, source_target_pairs={{0,16},{16,32},{32,48},{48,0},{1,17},{17,33},{33,49},{49,1},{2,18}... | collective-permute-start | bytes 1179656 | tf_op jit(solution)/shard_map/ppermute | solution.py:167
  70.6 11.0 %collective-permute-start.21 = (f32[64,1536]{1,0:T(8,128)S(1)}, f32[64,1536]{1,0:T(8,128)S(1)}, u32[]{:S(2)}, u32[]{:S(2)}) collective-permute-start(f32[64,1536]{1,0:T(8,128)S(1)} %collective-permute-done.17.refs_1_), channel_id=1, source_target_pairs={{0,48},{16,0},{32,16},{48,32},{1,49},{17,1},{33,17},{49,33},{2,50}... | collective-permute-start | bytes 1179656 | tf_op jit(solution)/shard_map/ppermute | solution.py:171
  74.0 16.0 %collective-permute-start.19 = (f32[64,1536]{1,0:T(8,128)S(1)}, f32[64,1536]{1,0:T(8,128)S(1)}, u32[]{:S(2)}, u32[]{:S(2)}) collective-permute-start(f32[64,1536]{1,0:T(8,128)S(1)} %multiply_bitcast_fusion.1.refs_0_), channel_id=1, source_target_pairs={{0,48},{16,0},{32,16},{48,32},{1,49},{17,1},{33,17},{49,33},{2,50}... | collective-permute-start | bytes 1179656 | tf_op jit(solution)/shard_map/ppermute | solution.py:168
  74.1 16.0 %collective-permute-start.20 = (f32[64,1536]{1,0:T(8,128)S(1)}, f32[64,1536]{1,0:T(8,128)S(1)}, u32[]{:S(2)}, u32[]{:S(2)}) collective-permute-start(f32[64,1536]{1,0:T(8,128)S(1)} %collective-permute-done.17.refs_1_), channel_id=1, source_target_pairs={{0,16},{16,32},{32,48},{48,0},{1,17},{17,33},{33,49},{49,1},{2,18}... | collective-permute-start | bytes 1179656 | tf_op jit(solution)/shard_map/ppermute | solution.py:170
  75.5 17.7 %collective-permute-start.22 = (f32[64,1536]{1,0:T(8,128)S(1)}, f32[64,1536]{1,0:T(8,128)S(1)}, u32[]{:S(2)}, u32[]{:S(2)}) collective-permute-start(f32[64,1536]{1,0:T(8,128)S(1)} %collective-permute-done.18.refs_2_), channel_id=1, source_target_pairs={{0,16},{16,32},{32,48},{48,0},{1,17},{17,33},{33,49},{49,1},{2,18}... | collective-permute-start | bytes 1179656 | tf_op jit(solution)/shard_map/ppermute | solution.py:172
  81.7 16.9 %collective-permute-start.23 = (f32[64,1536]{1,0:T(8,128)S(1)}, f32[64,1536]{1,0:T(8,128)S(1)}, u32[]{:S(2)}, u32[]{:S(2)}) collective-permute-start(f32[64,1536]{1,0:T(8,128)S(1)} %collective-permute-done.21.refs_5_), channel_id=1, source_target_pairs={{0,48},{16,0},{32,16},{48,32},{1,49},{17,1},{33,17},{49,33},{2,50}... | collective-permute-start | bytes 1179656 | tf_op jit(solution)/shard_map/ppermute | solution.py:173
  113.2 77.7 %collective-permute-start.24 = (f32[512,1536]{1,0:T(8,128)}, f32[512,1536]{1,0:T(8,128)}, u32[]{:S(2)}, u32[]{:S(2)}) collective-permute-start(f32[512,1536]{1,0:T(8,128)} %get-tuple-element.40), channel_id=1, source_target_pairs={{0,1},{1,0},{2,3},{3,2},{4,5},{5,4},{6,7},{7,6},{8,9},{9,8},{10,11... | collective-permute-start | bytes 9437192 | tf_op jit(solution)/shard_map/ppermute | solution.py:211
  129.1 75.8 %all-to-all-start = ((f32[8,64,1536]{2,1,0:T(8,128)}), f32[8,64,1536]{2,1,0:T(8,128)}, u32[]{:S(2)}, u32[]{:S(2)}) async-start(f32[8,64,1536]{2,1,0:T(8,128)} %bitcast.84), calls=%async_computation | async-start | bytes 6291456 | tf_op jit(solution)/shard_map/all_to_all | solution.py:177
  136.7 77.9 %collective-permute-start.10 = (f32[128,1536]{1,0:T(8,128)S(1)}, f32[128,1536]{1,0:T(8,128)}, u32[]{:S(2)}, u32[]{:S(2)}) collective-permute-start(f32[128,1536]{1,0:T(8,128)S(1)} %collective-permute-done.9.refs_0_), channel_id=1, source_target_pairs={{0,8},{8,0},{1,9},{9,1},{2,10},{10,2},{3,11},{11,3},{4,12},{12,4},... | collective-permute-start | bytes 2359304 | tf_op jit(solution)/shard_map/ppermute | solution.py:169
  204.9 110.7 %all-to-all-start.1 = ((f32[8,64,1536]{2,1,0:T(8,128)}), f32[8,64,1536]{2,1,0:T(8,128)}, u32[]{:S(2)}, u32[]{:S(2)}) async-start(f32[8,64,1536]{2,1,0:T(8,128)} %bitcast.83), calls=%async_computation.1 | async-start | bytes 6291456 | tf_op jit(solution)/shard_map/all_to_all | solution.py:177
  213.1 54.9 %collective-permute-start.11 = (f32[128,1536]{1,0:T(8,128)S(1)}, f32[128,1536]{1,0:T(8,128)S(1)}, u32[]{:S(2)}, u32[]{:S(2)}) collective-permute-start(f32[128,1536]{1,0:T(8,128)S(1)} %collective-permute-done.9.refs_0_), channel_id=1, source_target_pairs={{0,2},{2,4},{4,6},{6,0},{1,3},{3,5},{5,7},{7,1},{8,10},{10,12},{12... | collective-permute-start | bytes 2359304 | tf_op jit(solution)/shard_map/ppermute | solution.py:167
  214.5 53.4 %collective-permute-start.14 = (f32[128,1536]{1,0:T(8,128)}, f32[128,1536]{1,0:T(8,128)S(1)}, u32[]{:S(2)}, u32[]{:S(2)}) collective-permute-start(f32[128,1536]{1,0:T(8,128)} %collective-permute-done.10.refs_1_), channel_id=1, source_target_pairs={{0,6},{2,0},{4,2},{6,4},{1,7},{3,1},{5,3},{7,5},{8,14},{10,8},{12,... | collective-permute-start | bytes 2359304 | tf_op jit(solution)/shard_map/ppermute | solution.py:171
  216.4 65.4 %collective-permute-start.12 = (f32[128,1536]{1,0:T(8,128)S(1)}, f32[128,1536]{1,0:T(8,128)}, u32[]{:S(2)}, u32[]{:S(2)}) collective-permute-start(f32[128,1536]{1,0:T(8,128)S(1)} %collective-permute-done.9.refs_0_), channel_id=1, source_target_pairs={{0,6},{2,0},{4,2},{6,4},{1,7},{3,1},{5,3},{7,5},{8,14},{10,8},{12,... | collective-permute-start | bytes 2359304 | tf_op jit(solution)/shard_map/ppermute | solution.py:168
  217.8 67.1 %collective-permute-start.13 = (f32[128,1536]{1,0:T(8,128)}, f32[128,1536]{1,0:T(8,128)}, u32[]{:S(2)}, u32[]{:S(2)}) collective-permute-start(f32[128,1536]{1,0:T(8,128)} %collective-permute-done.10.refs_1_), channel_id=1, source_target_pairs={{0,2},{2,4},{4,6},{6,0},{1,3},{3,5},{5,7},{7,1},{8,10},{10,12},{12... | collective-permute-start | bytes 2359304 | tf_op jit(solution)/shard_map/ppermute | solution.py:170
  267.9 33.8 %collective-permute-start.15 = (f32[128,1536]{1,0:T(8,128)S(1)}, f32[128,1536]{1,0:T(8,128)}, u32[]{:S(2)}, u32[]{:S(2)}) collective-permute-start(f32[128,1536]{1,0:T(8,128)S(1)} %collective-permute-done.11.refs_2_), channel_id=1, source_target_pairs={{0,2},{2,4},{4,6},{6,0},{1,3},{3,5},{5,7},{7,1},{8,10},{10,12},{12... | collective-permute-start | bytes 2359304 | tf_op jit(solution)/shard_map/ppermute | solution.py:172
  268.0 33.8 %collective-permute-start.16 = (f32[128,1536]{1,0:T(8,128)S(1)}, f32[128,1536]{1,0:T(8,128)}, u32[]{:S(2)}, u32[]{:S(2)}) collective-permute-start(f32[128,1536]{1,0:T(8,128)S(1)} %collective-permute-done.14.refs_5_), channel_id=1, source_target_pairs={{0,6},{2,0},{4,2},{6,4},{1,7},{3,1},{5,3},{7,5},{8,14},{10,8},{12,... | collective-permute-start | bytes 2359304 | tf_op jit(solution)/shard_map/ppermute | solution.py:173
  360.3 14.6 %collective-permute-start.26 = (f32[3,512,256]{2,1,0:T(8,128)S(1)}, f32[3,512,256]{2,1,0:T(8,128)}, u32[]{:S(2)}, u32[]{:S(2)}) collective-permute-start(f32[3,512,256]{2,1,0:T(8,128)S(1)} %bitcast.86), channel_id=1, source_target_pairs={{0,1},{1,0},{2,3},{3,2},{4,5},{5,4},{6,7},{7,6},{8,9},{9,8},{10,11... | collective-permute-start | bytes 4718600 | tf_op jit(solution)/shard_map/ppermute | solution.py:224
  (30 other events, 270.5 us)

commit v9 on v8

--- a/solution.py
+++ b/solution.py
@@ -137,6 +137,19 @@
     )(places, *pieces)
 
 
+def turn_kernel(one_ref, two_ref, one_out, two_out):
+    one_out[...] = one_ref[...].T
+    two_out[...] = two_ref[...].T
+
+
+def turned(one, two):
+    return pl.pallas_call(
+        turn_kernel,
+        out_shape=[jax.ShapeDtypeStruct(value.shape[::-1], value.dtype) for value in (one, two)],
+        cost_estimate=pl.CostEstimate(flops=0, transcendentals=0, bytes_accessed=16 * one.size),
+    )(one, two)
+
+
 def per_device(ancestor, lhat_one, lhat_two, link_two, diag_one, diag_two, mask_one, mask_two):
     column_index = lax.axis_index(COL)
     core = lax.axis_index("core")
@@ -163,14 +176,20 @@
         own = lax.dynamic_slice_in_dim(mask, column_index * blocks, blocks).astype(jnp.float32)
         return shard.T * jnp.broadcast_to(own[:, None], (blocks, BLOCK)).reshape(1, depth)
 
-    def gathered(piece, side_axis, ring_axis):
+    def gathered(piece, side_axis, ring_axis, far_aside=False):
         below = lax.ppermute(piece, ring_axis, up)
         above = lax.ppermute(piece, ring_axis, down)
         side = lax.ppermute(piece, side_axis, SWAP)
         side_below = lax.ppermute(side, ring_axis, up)
         side_above = lax.ppermute(side, ring_axis, down)
-        far = lax.ppermute(below, ring_axis, up)
-        side_far = lax.ppermute(side_above, ring_axis, down)
+        if far_aside:
+            middle = piece.shape[0] // 2
+            far = jnp.concatenate([lax.ppermute(below[:middle], ring_axis, up),
+                                   lax.ppermute(above[middle:], ring_axis, down)])
+            side_far = lax.ppermute(far, side_axis, SWAP)
+        else:
+            far = lax.ppermute(below, ring_axis, up)
+            side_far = lax.ppermute(side_above, ring_axis, down)
         return [piece, side, below, above, side_below, side_above, far, side_far]
 
     def scattered(chip):
@@ -197,7 +216,7 @@
     piece_two = masked(lhat_two, mask_two)
     pieces_one = gathered(piece_one, "xl", "z")
     raw = lax.ppermute(jnp.concatenate([piece_one, piece_two]), ALL, raw_routes())
-    row_pieces = gathered(raw, "xh", "y")
+    row_pieces = gathered(raw, "xh", "y", far_aside=True)
     link_base = lax.optimization_barrier(-product(diag_one, link_two))
     piece_two, *pieces_one = lax.optimization_barrier((piece_two, *pieces_one))
     pieces_two = gathered(piece_two, "xl", "z")
@@ -223,9 +242,10 @@
     spread = spread.reshape(8, 8, 3, strip // 8, half).transpose(2, 1, 0, 3, 4).reshape(3, width, half)
     other = lax.ppermute(spread, "core", SWAP)
     sums = jnp.where(core == 0, jnp.concatenate([spread, other], 2), jnp.concatenate([other, spread], 2))
-    d_one = diag_one - sums[0].T
+    one_base, two_base = turned(diag_one, diag_two)
+    d_one = (one_base - sums[0]).T
     link_inverse = link_base - sums[1] + product(sums[0], link_two, ((0,), (0,)))
-    d_two = diag_two - sums[2].T - product(link_two, link_inverse, ((0,), (0,)))
+    d_two = (two_base - sums[2] - product(link_inverse, link_two, ((0,), (0,)))).T
     return (to_rows(x_one), d_one, to_rows(x_two), link_inverse, d_two)
 
 

time: 384 us -> 380 us (0.990)
  waiting for transfers between devices: 132 us -> 117 us
  starting transfers between devices: 108 us -> 120 us
  local copies, waits for them, and re-layouts: 26.3 us -> 21.3 us
    ppermute x3, starting transfers between devices: 57.5 us -> 6.01 us  [gathered(): side = lax.ppermute(piece, side_axis, SWAP)]
    ppermute x3, waiting for transfers between devices: 50.1 us -> 0.01 us  [gathered(): below = lax.ppermute(piece, ring_axis, up)]
    ppermute x3, starting transfers between devices: 3.35 us -> 52.2 us  [gathered(): below = lax.ppermute(piece, ring_axis, up)]
    ppermute x3, waiting for transfers between devices: 16.6 us -> 51.9 us  [gathered(): above = lax.ppermute(piece, ring_axis, down)]
    ppermute x3 -> x2, waiting for transfers between devices: 22.4 us -> 5.53 us  [gathered(): far = lax.ppermute(below, ring_axis, up)]
    ppermute x0 -> x3, waiting for transfers between devices: none -> 8.87 us  [the longest x1 4.58 us: gathered(): lax.ppermute(above[middle:], ring_axis, down)]
    ppermute x0 -> x3, starting transfers between devices: none -> 7.44 us  [the longest x1 5.84 us: gathered(): side_far = lax.ppermute(far, side_axis, SWAP)]
    ppermute x3, waiting for transfers between devices: 11.3 us -> 17 us  [gathered(): side_above = lax.ppermute(side, ring_axis, down)]
  transfers between devices with their start and end apart: 30 -> 31, of which waited for: 16 -> 17; matrix products, arithmetic and copies ran while one was open for 6% -> 4% of each run, Pallas kernels for 10% -> 11%
where the time goes in v9:
time: 380 us; the launch traced here: 379 us
  starting transfers between devices  120 us (32%)
  waiting for transfers between devices  117 us (31%)
  Pallas kernels  53.1 us (14%)
  blocking collectives  38.1 us (10%)
  local copies, waits for them, and re-layouts  21.3 us (6%)
  matrix products  16.8 us (4%)
  other arithmetic  11.4 us (3%)
    ppermute x3, starting transfers between devices, gathered(): below = lax.ppermute(piece, ring_axis, up)  52.2 us
    ppermute x3, waiting for transfers between devices, gathered(): above = lax.ppermute(piece, ring_axis, down)  51.9 us
    pallas_call x4, Pallas kernels, half_product(): pl.pallas_call(kernel, grid_spec=pltpu.PrefetchScalarGridSpec(num_scalar_...  46.8 us
    all_to_all x1, blocking collectives, per_device(): lax.all_to_all(jnp.broadcast_to(piece[None], (64,) + piece.shape), CHIPS,...  29.5 us
    unnamed x51, local copies, waits for them, and re-layouts  20.5 us
    all_to_all x2, starting transfers between devices, scattered(): lax.all_to_all(chip.reshape(8, strip, rows // 2), PLANE, split_axis=0, co...  19 us
    ppermute x3, waiting for transfers between devices, gathered(): side_above = lax.ppermute(side, ring_axis, down)  17 us
    dot_general x7, matrix products, product(): lax.dot_general(left, right, (contract, ((), ())), precision=lax.Precisio...  16.8 us
  transfers between devices with their start and end apart: 31, of which 17 were waited for; matrix products, arithmetic and copies ran while one was open for 4% of the time, Pallas kernels for 11%

profile of v9, /device:TPU:1, one launch (start us, length us, event | category | flops | bytes accessed | tf_op | source)
XLA Modules:
  0.0 379.0 jit_solution(16963894855753880002)
XLA Ops:
  6.4 6.8 %collective-permute-done.refs_1_ = f32[64,1536]{1,0:T(8,128)S(1)} collective-permute-done((f32[64,1536]{1,0:T(8,128)S(1)}, f32[64,1536]{1,0:T(8,128)S(1)}, u32[]{:S(2)}, u32[]{:S(2)}) %collective-permute-start) | collective-permute-done | bytes 393248 | tf_op jit(solution)/shard_map/ppermute | solution.py:182
  13.1 4.1 %collective-permute-start.4 = (f32[64,1536]{1,0:T(8,128)S(1)}, f32[64,1536]{1,0:T(8,128)S(1)}, u32[]{:S(2)}, u32[]{:S(2)}) collective-permute-start(f32[64,1536]{1,0:T(8,128)S(1)} %collective-permute-done.refs_1_), channel_id=1, source_target_pairs={{0,48},{16,0},{32,16},{48,32},{1,49},{17,1},{33,17},{49,33},{2,50}... | collective-permute-start | bytes 1179656 | tf_op jit(solution)/shard_map/ppermute | solution.py:184
  19.0 5.2 %collective-permute-done.4.refs_5_ = f32[64,1536]{1,0:T(8,128)S(1)} collective-permute-done((f32[64,1536]{1,0:T(8,128)S(1)}, f32[64,1536]{1,0:T(8,128)S(1)}, u32[]{:S(2)}, u32[]{:S(2)}) %collective-permute-start.4) | collective-permute-done | bytes 393248 | tf_op jit(solution)/shard_map/ppermute | solution.py:184
  35.8 5.3 %collective-permute-done.6.refs_7_ = f32[64,1536]{1,0:T(8,128)S(1)} collective-permute-done((f32[64,1536]{1,0:T(8,128)S(1)}, f32[64,1536]{1,0:T(8,128)S(1)}, u32[]{:S(2)}, u32[]{:S(2)}) %collective-permute-start.6) | collective-permute-done | bytes 393248 | tf_op jit(solution)/shard_map/ppermute | solution.py:192
  45.1 12.5 %shard_map.119 = (f32[512,1536]{1,0:T(8,128)}, bf16[512,1536]{1,0:T(8,128)(2,1)S(1)}, bf16[512,1536]{1,0:T(8,128)(2,1)S(1)}, f32[512,1536]{1,0:T(8,128)S(1)}) custom-call(s32[9]{0:T(128)S(1)} %stack.94.place_ref, f32[3072,1536]{1,0:T(8,128)} %a_ref.7, f32[64,1536]{1,0:T(8,128)S(1)} %multiply_bitcast_fusion.refs_0_, f32[64,1536]{1,0:T(8,128)S(1)} %copy-done.13, ...), custom_call_target="tpu_custom_call" | custom-call | flops 7247757312 | bytes 15728640 | tf_op jit(solution)/shard_map/pallas_call | solution.py:105
  61.4 9.2 %collective-permute-done.18.refs_1_ = f32[64,1536]{1,0:T(8,128)S(1)} collective-permute-done((f32[64,1536]{1,0:T(8,128)S(1)}, f32[64,1536]{1,0:T(8,128)S(1)}, u32[]{:S(2)}, u32[]{:S(2)}) %collective-permute-start.18) | collective-permute-done | bytes 393248 | tf_op jit(solution)/shard_map/ppermute | solution.py:182
  75.5 6.1 %collective-permute-done.22.refs_5_ = f32[64,1536]{1,0:T(8,128)S(1)} collective-permute-done((f32[64,1536]{1,0:T(8,128)S(1)}, f32[64,1536]{1,0:T(8,128)S(1)}, u32[]{:S(2)}, u32[]{:S(2)}) %collective-permute-start.22) | collective-permute-done | bytes 393248 | tf_op jit(solution)/shard_map/ppermute | solution.py:184
  93.2 5.3 %collective-permute-done.24.refs_7_ = f32[64,1536]{1,0:T(8,128)S(1)} collective-permute-done((f32[64,1536]{1,0:T(8,128)S(1)}, f32[64,1536]{1,0:T(8,128)S(1)}, u32[]{:S(2)}, u32[]{:S(2)}) %collective-permute-start.24) | collective-permute-done | bytes 393248 | tf_op jit(solution)/shard_map/ppermute | solution.py:192
  98.5 12.4 %shard_map.123 = (f32[512,1536]{1,0:T(8,128)}, bf16[512,1536]{1,0:T(8,128)(2,1)S(1)}, bf16[512,1536]{1,0:T(8,128)(2,1)S(1)}) custom-call(s32[9]{0:T(128)S(1)} %stack.94.place_ref, f32[3072,1536]{1,0:T(8,128)} %a_ref.7, f32[64,1536]{1,0:T(8,128)S(1)} %multiply_bitcast_fusion.1.refs_0_, f32[64,1536]{1,0:T(8,128)S(1)} %collective-permute-done.18.refs_1_, ...), custom_call_target="tpu_custom_call" | custom-call | flops 7247757312 | bytes 15728640 | tf_op jit(solution)/shard_map/pallas_call | solution.py:105
  116.4 11.0 %shard_map.120 = f32[512,1536]{1,0:T(8,128)S(1)} custom-call(s32[9]{0:T(128)S(1)} %stack.92.place_ref, f32[3072,1536]{1,0:T(8,128)} %a_ref.7, bf16[512,1536]{1,0:T(8,128)(2,1)S(1)} %get-tuple-element.33.high_ref, bf16[512,1536]{1,0:T(8,128)(2,1)S(1)} %copy-done.7, f32[512,1536]{1,0:T(8,128)} %collective-permute-done.7.added_ref), custom_call_target="tpu_custom_call" | custom-call | flops 7247757312 | bytes 15728640 | tf_op jit(solution)/shard_map/pallas_call | solution.py:105
  129.1 6.8 %all-to-all-start = ((f32[8,64,1536]{2,1,0:T(8,128)}), f32[8,64,1536]{2,1,0:T(8,128)}, u32[]{:S(2)}, u32[]{:S(2)}) async-start(f32[8,64,1536]{2,1,0:T(8,128)} %bitcast.85), calls=%async_computation | async-start | bytes 6291456 | tf_op jit(solution)/shard_map/all_to_all | solution.py:196
  137.5 50.3 %collective-permute-start.11 = (f32[128,1536]{1,0:T(8,128)}, f32[128,1536]{1,0:T(8,128)S(1)}, u32[]{:S(2)}, u32[]{:S(2)}) collective-permute-start(f32[128,1536]{1,0:T(8,128)} %collective-permute-done.9.refs_0_), channel_id=1, source_target_pairs={{0,2},{2,4},{4,6},{6,0},{1,3},{3,5},{5,7},{7,1},{8,10},{10,12},{12... | collective-permute-start | bytes 2359304 | tf_op jit(solution)/shard_map/ppermute | solution.py:180
  189.3 11.0 %shard_map.124 = f32[512,1536]{1,0:T(8,128)S(1)} custom-call(s32[9]{0:T(128)S(1)} %stack.92.place_ref, f32[3072,1536]{1,0:T(8,128)} %a_ref.7, bf16[512,1536]{1,0:T(8,128)(2,1)S(1)} %copy-done.9, bf16[512,1536]{1,0:T(8,128)(2,1)S(1)} %copy-done.11, f32[512,1536]{1,0:T(8,128)} %collective-permute-done.25.added_ref), custom_call_target="tpu_custom_call" | custom-call | flops 7247757312 | bytes 15728640 | tf_op jit(solution)/shard_map/pallas_call | solution.py:105
  201.9 12.2 %all-to-all-start.1 = ((f32[8,64,1536]{2,1,0:T(8,128)}), f32[8,64,1536]{2,1,0:T(8,128)}, u32[]{:S(2)}, u32[]{:S(2)}) async-start(f32[8,64,1536]{2,1,0:T(8,128)} %bitcast.84), calls=%async_computation.1 | async-start | bytes 6291456 | tf_op jit(solution)/shard_map/all_to_all | solution.py:196
  219.6 46.4 %collective-permute-done.12.refs_3_ = f32[128,1536]{1,0:T(8,128)S(1)} collective-permute-done((f32[128,1536]{1,0:T(8,128)}, f32[128,1536]{1,0:T(8,128)S(1)}, u32[]{:S(2)}, u32[]{:S(2)}) %collective-permute-start.12) | collective-permute-done | bytes 786464 | tf_op jit(solution)/shard_map/ppermute | solution.py:181
  270.3 4.6 %collective-permute-done.16 = f32[64,1536]{1,0:T(8,128)S(1)} collective-permute-done((f32[64,1536]{1,0:T(8,128)S(1)}, f32[64,1536]{1,0:T(8,128)S(1)}, u32[]{:S(2)}, u32[]{:S(2)}) %collective-permute-start.16) | collective-permute-done | bytes 393248 | tf_op jit(solution)/shard_map/ppermute | solution.py:188
  274.9 5.8 %collective-permute-start.17 = (f32[128,1536]{1,0:T(8,128)S(1)}, f32[128,1536]{1,0:T(8,128)}, u32[]{:S(2)}, u32[]{:S(2)}) collective-permute-start(f32[128,1536]{1,0:T(8,128)S(1)} %constant_dynamic-update-slice_fusion.refs_6_), channel_id=1, source_target_pairs={{0,8},{8,0},{1,9},{9,1},{2,10},{10,2},{3,11},{11,3},{4,12},{12,4},... | collective-permute-start | bytes 2359304 | tf_op jit(solution)/shard_map/ppermute | solution.py:189
  280.8 5.3 %collective-permute-done.13.refs_4_ = f32[128,1536]{1,0:T(8,128)} collective-permute-done((f32[128,1536]{1,0:T(8,128)}, f32[128,1536]{1,0:T(8,128)}, u32[]{:S(2)}, u32[]{:S(2)}) %collective-permute-start.13) | collective-permute-done | bytes 786464 | tf_op jit(solution)/shard_map/ppermute | solution.py:183
  286.1 5.6 %collective-permute-done.14.refs_5_ = f32[128,1536]{1,0:T(8,128)} collective-permute-done((f32[128,1536]{1,0:T(8,128)}, f32[128,1536]{1,0:T(8,128)}, u32[]{:S(2)}, u32[]{:S(2)}) %collective-permute-start.14) | collective-permute-done | bytes 786464 | tf_op jit(solution)/shard_map/ppermute | solution.py:184
  291.7 4.3 %collective-permute-done.17.refs_7_ = f32[128,1536]{1,0:T(8,128)} collective-permute-done((f32[128,1536]{1,0:T(8,128)S(1)}, f32[128,1536]{1,0:T(8,128)}, u32[]{:S(2)}, u32[]{:S(2)}) %collective-permute-start.17) | collective-permute-done | bytes 786464 | tf_op jit(solution)/shard_map/ppermute | solution.py:189
  304.5 3.6 convolution_bitcast_fusion.3
  311.9 3.4 convolution_bitcast_fusion.1
  319.9 8.7 %all_to_all.20 = f32[8,3,8,256]{3,2,1,0:T(8,128)S(1)} all-to-all(f32[8,3,8,256]{3,2,1,0:T(8,128)S(1)} %copy_bitcast_fusion), channel_id=1, replica_groups=mesh['xl'=2,'z'=4,'xh'=2,'y'=4,'core'=2] {'xl','z'}, dimensions={0} | all-to-all | bytes 393216 | tf_op jit(solution)/shard_map/all_to_all | solution.py:239
  328.7 29.5 %all_to_all.21 = f32[64,3,8,256]{3,2,1,0:T(8,128)S(1)} all-to-all(f32[64,3,8,256]{3,2,1,0:T(8,128)S(1)} %broadcast_in_dim.8), channel_id=1, replica_groups=mesh['xl'=2,'z'=4,'xh'=2,'y'=4,'core'=2] {'xl','z','xh','y'}, dimensions={0} | all-to-all | bytes 3145728 | tf_op jit(solution)/shard_map/all_to_all | solution.py:240
  (131 shorter events, 102.8 us)
Async XLA Ops:
  4.7 14.2 %collective-permute-start.1 = (f32[64,1536]{1,0:T(8,128)S(1)}, f32[64,1536]{1,0:T(8,128)S(1)}, u32[]{:S(2)}, u32[]{:S(2)}) collective-permute-start(f32[64,1536]{1,0:T(8,128)S(1)} %multiply_bitcast_fusion.refs_0_), channel_id=1, source_target_pairs={{0,16},{16,32},{32,48},{48,0},{1,17},{17,33},{33,49},{49,1},{2,18}... | collective-permute-start | bytes 1179656 | tf_op jit(solution)/shard_map/ppermute | solution.py:180
  13.1 11.1 %collective-permute-start.4 = (f32[64,1536]{1,0:T(8,128)S(1)}, f32[64,1536]{1,0:T(8,128)S(1)}, u32[]{:S(2)}, u32[]{:S(2)}) collective-permute-start(f32[64,1536]{1,0:T(8,128)S(1)} %collective-permute-done.refs_1_), channel_id=1, source_target_pairs={{0,48},{16,0},{32,16},{48,32},{1,49},{17,1},{33,17},{49,33},{2,50}... | collective-permute-start | bytes 1179656 | tf_op jit(solution)/shard_map/ppermute | solution.py:184
  17.3 15.4 %collective-permute-start.2 = (f32[64,1536]{1,0:T(8,128)S(1)}, f32[64,1536]{1,0:T(8,128)S(1)}, u32[]{:S(2)}, u32[]{:S(2)}) collective-permute-start(f32[64,1536]{1,0:T(8,128)S(1)} %multiply_bitcast_fusion.refs_0_), channel_id=1, source_target_pairs={{0,48},{16,0},{32,16},{48,32},{1,49},{17,1},{33,17},{49,33},{2,50}... | collective-permute-start | bytes 1179656 | tf_op jit(solution)/shard_map/ppermute | solution.py:181
  17.6 15.8 %collective-permute-start.3 = (f32[64,1536]{1,0:T(8,128)S(1)}, f32[64,1536]{1,0:T(8,128)S(1)}, u32[]{:S(2)}, u32[]{:S(2)}) collective-permute-start(f32[64,1536]{1,0:T(8,128)S(1)} %collective-permute-done.refs_1_), channel_id=1, source_target_pairs={{0,16},{16,32},{32,48},{48,0},{1,17},{17,33},{33,49},{49,1},{2,18}... | collective-permute-start | bytes 1179656 | tf_op jit(solution)/shard_map/ppermute | solution.py:183
  18.9 16.9 %collective-permute-start.5 = (f32[64,1536]{1,0:T(8,128)S(1)}, f32[64,1536]{1,0:T(8,128)S(1)}, u32[]{:S(2)}, u32[]{:S(2)}) collective-permute-start(f32[64,1536]{1,0:T(8,128)S(1)} %collective-permute-done.1.refs_2_), channel_id=1, source_target_pairs={{0,16},{16,32},{32,48},{48,0},{1,17},{17,33},{33,49},{49,1},{2,18}... | collective-permute-start | bytes 1179656 | tf_op jit(solution)/shard_map/ppermute | solution.py:191
  24.2 16.9 %collective-permute-start.6 = (f32[64,1536]{1,0:T(8,128)S(1)}, f32[64,1536]{1,0:T(8,128)S(1)}, u32[]{:S(2)}, u32[]{:S(2)}) collective-permute-start(f32[64,1536]{1,0:T(8,128)S(1)} %collective-permute-done.4.refs_5_), channel_id=1, source_target_pairs={{0,48},{16,0},{32,16},{48,32},{1,49},{17,1},{33,17},{49,33},{2,50}... | collective-permute-start | bytes 1179656 | tf_op jit(solution)/shard_map/ppermute | solution.py:192
  57.6 57.4 %collective-permute-start.7 = (f32[512,1536]{1,0:T(8,128)}, f32[512,1536]{1,0:T(8,128)}, u32[]{:S(2)}, u32[]{:S(2)}) collective-permute-start(f32[512,1536]{1,0:T(8,128)} %get-tuple-element.35), channel_id=1, source_target_pairs={{0,1},{1,0},{2,3},{3,2},{4,5},{5,4},{6,7},{7,6},{8,9},{9,8},{10,11... | collective-permute-start | bytes 9437192 | tf_op jit(solution)/shard_map/ppermute | solution.py:225
  61.2 14.3 %collective-permute-start.19 = (f32[64,1536]{1,0:T(8,128)S(1)}, f32[64,1536]{1,0:T(8,128)S(1)}, u32[]{:S(2)}, u32[]{:S(2)}) collective-permute-start(f32[64,1536]{1,0:T(8,128)S(1)} %multiply_bitcast_fusion.1.refs_0_), channel_id=1, source_target_pairs={{0,16},{16,32},{32,48},{48,0},{1,17},{17,33},{33,49},{49,1},{2,18}... | collective-permute-start | bytes 1179656 | tf_op jit(solution)/shard_map/ppermute | solution.py:180
  70.6 11.0 %collective-permute-start.22 = (f32[64,1536]{1,0:T(8,128)S(1)}, f32[64,1536]{1,0:T(8,128)S(1)}, u32[]{:S(2)}, u32[]{:S(2)}) collective-permute-start(f32[64,1536]{1,0:T(8,128)S(1)} %collective-permute-done.18.refs_1_), channel_id=1, source_target_pairs={{0,48},{16,0},{32,16},{48,32},{1,49},{17,1},{33,17},{49,33},{2,50}... | collective-permute-start | bytes 1179656 | tf_op jit(solution)/shard_map/ppermute | solution.py:184
  74.0 16.0 %collective-permute-start.20 = (f32[64,1536]{1,0:T(8,128)S(1)}, f32[64,1536]{1,0:T(8,128)S(1)}, u32[]{:S(2)}, u32[]{:S(2)}) collective-permute-start(f32[64,1536]{1,0:T(8,128)S(1)} %multiply_bitcast_fusion.1.refs_0_), channel_id=1, source_target_pairs={{0,48},{16,0},{32,16},{48,32},{1,49},{17,1},{33,17},{49,33},{2,50}... | collective-permute-start | bytes 1179656 | tf_op jit(solution)/shard_map/ppermute | solution.py:181
  74.1 16.0 %collective-permute-start.21 = (f32[64,1536]{1,0:T(8,128)S(1)}, f32[64,1536]{1,0:T(8,128)S(1)}, u32[]{:S(2)}, u32[]{:S(2)}) collective-permute-start(f32[64,1536]{1,0:T(8,128)S(1)} %collective-permute-done.18.refs_1_), channel_id=1, source_target_pairs={{0,16},{16,32},{32,48},{48,0},{1,17},{17,33},{33,49},{49,1},{2,18}... | collective-permute-start | bytes 1179656 | tf_op jit(solution)/shard_map/ppermute | solution.py:183
  75.5 17.7 %collective-permute-start.23 = (f32[64,1536]{1,0:T(8,128)S(1)}, f32[64,1536]{1,0:T(8,128)S(1)}, u32[]{:S(2)}, u32[]{:S(2)}) collective-permute-start(f32[64,1536]{1,0:T(8,128)S(1)} %collective-permute-done.19.refs_2_), channel_id=1, source_target_pairs={{0,16},{16,32},{32,48},{48,0},{1,17},{17,33},{33,49},{49,1},{2,18}... | collective-permute-start | bytes 1179656 | tf_op jit(solution)/shard_map/ppermute | solution.py:191
  81.6 16.9 %collective-permute-start.24 = (f32[64,1536]{1,0:T(8,128)S(1)}, f32[64,1536]{1,0:T(8,128)S(1)}, u32[]{:S(2)}, u32[]{:S(2)}) collective-permute-start(f32[64,1536]{1,0:T(8,128)S(1)} %collective-permute-done.22.refs_5_), channel_id=1, source_target_pairs={{0,48},{16,0},{32,16},{48,32},{1,49},{17,1},{33,17},{49,33},{2,50}... | collective-permute-start | bytes 1179656 | tf_op jit(solution)/shard_map/ppermute | solution.py:192
  113.2 74.7 %collective-permute-start.25 = (f32[512,1536]{1,0:T(8,128)}, f32[512,1536]{1,0:T(8,128)}, u32[]{:S(2)}, u32[]{:S(2)}) collective-permute-start(f32[512,1536]{1,0:T(8,128)} %get-tuple-element.43), channel_id=1, source_target_pairs={{0,1},{1,0},{2,3},{3,2},{4,5},{5,4},{6,7},{7,6},{8,9},{9,8},{10,11... | collective-permute-start | bytes 9437192 | tf_op jit(solution)/shard_map/ppermute | solution.py:230
  129.1 72.8 %all-to-all-start = ((f32[8,64,1536]{2,1,0:T(8,128)}), f32[8,64,1536]{2,1,0:T(8,128)}, u32[]{:S(2)}, u32[]{:S(2)}) async-start(f32[8,64,1536]{2,1,0:T(8,128)} %bitcast.85), calls=%async_computation | async-start | bytes 6291456 | tf_op jit(solution)/shard_map/all_to_all | solution.py:196
  137.5 82.0 %collective-permute-start.11 = (f32[128,1536]{1,0:T(8,128)}, f32[128,1536]{1,0:T(8,128)S(1)}, u32[]{:S(2)}, u32[]{:S(2)}) collective-permute-start(f32[128,1536]{1,0:T(8,128)} %collective-permute-done.9.refs_0_), channel_id=1, source_target_pairs={{0,2},{2,4},{4,6},{6,0},{1,3},{3,5},{5,7},{7,1},{8,10},{10,12},{12... | collective-permute-start | bytes 2359304 | tf_op jit(solution)/shard_map/ppermute | solution.py:180
  201.9 107.9 %all-to-all-start.1 = ((f32[8,64,1536]{2,1,0:T(8,128)}), f32[8,64,1536]{2,1,0:T(8,128)}, u32[]{:S(2)}, u32[]{:S(2)}) async-start(f32[8,64,1536]{2,1,0:T(8,128)} %bitcast.84), calls=%async_computation.1 | async-start | bytes 6291456 | tf_op jit(solution)/shard_map/all_to_all | solution.py:196
  214.1 51.9 %collective-permute-start.12 = (f32[128,1536]{1,0:T(8,128)}, f32[128,1536]{1,0:T(8,128)S(1)}, u32[]{:S(2)}, u32[]{:S(2)}) collective-permute-start(f32[128,1536]{1,0:T(8,128)} %collective-permute-done.9.refs_0_), channel_id=1, source_target_pairs={{0,6},{2,0},{4,2},{6,4},{1,7},{3,1},{5,3},{7,5},{8,14},{10,8},{12,... | collective-permute-start | bytes 2359304 | tf_op jit(solution)/shard_map/ppermute | solution.py:181
  216.8 50.8 %collective-permute-start.10 = (f32[128,1536]{1,0:T(8,128)}, f32[128,1536]{1,0:T(8,128)}, u32[]{:S(2)}, u32[]{:S(2)}) collective-permute-start(f32[128,1536]{1,0:T(8,128)} %collective-permute-done.9.refs_0_), channel_id=1, source_target_pairs={{0,8},{8,0},{1,9},{9,1},{2,10},{10,2},{3,11},{11,3},{4,12},{12,4},... | collective-permute-start | bytes 2359304 | tf_op jit(solution)/shard_map/ppermute | solution.py:182
  219.5 50.7 %collective-permute-start.15 = (f32[64,1536]{1,0:T(8,128)S(1)}, f32[64,1536]{1,0:T(8,128)S(1)}, u32[]{:S(2)}, u32[]{:S(2)}) collective-permute-start(f32[64,1536]{1,0:T(8,128)S(1)} %slice.21), channel_id=1, source_target_pairs={{0,2},{2,4},{4,6},{6,0},{1,3},{3,5},{5,7},{7,1},{8,10},{10,12},{12... | collective-permute-start | bytes 1179656 | tf_op jit(solution)/shard_map/ppermute | solution.py:187
  267.6 18.5 %collective-permute-start.13 = (f32[128,1536]{1,0:T(8,128)}, f32[128,1536]{1,0:T(8,128)}, u32[]{:S(2)}, u32[]{:S(2)}) collective-permute-start(f32[128,1536]{1,0:T(8,128)} %collective-permute-done.10.refs_1_), channel_id=1, source_target_pairs={{0,2},{2,4},{4,6},{6,0},{1,3},{3,5},{5,7},{7,1},{8,10},{10,12},{12... | collective-permute-start | bytes 2359304 | tf_op jit(solution)/shard_map/ppermute | solution.py:183
  268.7 23.0 %collective-permute-start.14 = (f32[128,1536]{1,0:T(8,128)}, f32[128,1536]{1,0:T(8,128)}, u32[]{:S(2)}, u32[]{:S(2)}) collective-permute-start(f32[128,1536]{1,0:T(8,128)} %collective-permute-done.10.refs_1_), channel_id=1, source_target_pairs={{0,6},{2,0},{4,2},{6,4},{1,7},{3,1},{5,3},{7,5},{8,14},{10,8},{12,... | collective-permute-start | bytes 2359304 | tf_op jit(solution)/shard_map/ppermute | solution.py:184
  274.9 21.1 %collective-permute-start.17 = (f32[128,1536]{1,0:T(8,128)S(1)}, f32[128,1536]{1,0:T(8,128)}, u32[]{:S(2)}, u32[]{:S(2)}) collective-permute-start(f32[128,1536]{1,0:T(8,128)S(1)} %constant_dynamic-update-slice_fusion.refs_6_), channel_id=1, source_target_pairs={{0,8},{8,0},{1,9},{9,1},{2,10},{10,2},{3,11},{11,3},{4,12},{12,4},... | collective-permute-start | bytes 2359304 | tf_op jit(solution)/shard_map/ppermute | solution.py:189
  358.4 12.8 %collective-permute-start.27 = (f32[3,512,256]{2,1,0:T(8,128)S(1)}, f32[3,512,256]{2,1,0:T(8,128)}, u32[]{:S(2)}, u32[]{:S(2)}) collective-permute-start(f32[3,512,256]{2,1,0:T(8,128)S(1)} %bitcast.87), channel_id=1, source_target_pairs={{0,1},{1,0},{2,3},{3,2},{4,5},{5,4},{6,7},{7,6},{8,9},{9,8},{10,11... | collective-permute-start | bytes 4718600 | tf_op jit(solution)/shard_map/ppermute | solution.py:243
  (31 other events, 280.5 us)

commit v10 on v9

--- a/solution.py
+++ b/solution.py
@@ -176,20 +176,14 @@
         own = lax.dynamic_slice_in_dim(mask, column_index * blocks, blocks).astype(jnp.float32)
         return shard.T * jnp.broadcast_to(own[:, None], (blocks, BLOCK)).reshape(1, depth)
 
-    def gathered(piece, side_axis, ring_axis, far_aside=False):
+    def gathered(piece, side_axis, ring_axis):
         below = lax.ppermute(piece, ring_axis, up)
         above = lax.ppermute(piece, ring_axis, down)
         side = lax.ppermute(piece, side_axis, SWAP)
         side_below = lax.ppermute(side, ring_axis, up)
         side_above = lax.ppermute(side, ring_axis, down)
-        if far_aside:
-            middle = piece.shape[0] // 2
-            far = jnp.concatenate([lax.ppermute(below[:middle], ring_axis, up),
-                                   lax.ppermute(above[middle:], ring_axis, down)])
-            side_far = lax.ppermute(far, side_axis, SWAP)
-        else:
-            far = lax.ppermute(below, ring_axis, up)
-            side_far = lax.ppermute(side_above, ring_axis, down)
+        far = lax.ppermute(below, ring_axis, up)
+        side_far = lax.ppermute(side_above, ring_axis, down)
         return [piece, side, below, above, side_below, side_above, far, side_far]
 
     def scattered(chip):
@@ -216,7 +210,7 @@
     piece_two = masked(lhat_two, mask_two)
     pieces_one = gathered(piece_one, "xl", "z")
     raw = lax.ppermute(jnp.concatenate([piece_one, piece_two]), ALL, raw_routes())
-    row_pieces = gathered(raw, "xh", "y", far_aside=True)
+    row_pieces = gathered(raw, "xh", "y")
     link_base = lax.optimization_barrier(-product(diag_one, link_two))
     piece_two, *pieces_one = lax.optimization_barrier((piece_two, *pieces_one))
     pieces_two = gathered(piece_two, "xl", "z")

time: 380 us -> 382 us (level)
  waiting for transfers between devices: 117 us -> 132 us
  starting transfers between devices: 120 us -> 108 us
    ppermute x3, starting transfers between devices: 6.01 us -> 57.5 us  [gathered(): side = lax.ppermute(piece, side_axis, SWAP)]
    ppermute x3, waiting for transfers between devices: 0.01 us -> 50.1 us  [gathered(): below = lax.ppermute(piece, ring_axis, up)]
    ppermute x3, starting transfers between devices: 52.2 us -> 3.35 us  [gathered(): below = lax.ppermute(piece, ring_axis, up)]
    ppermute x3, waiting for transfers between devices: 51.9 us -> 16.6 us  [gathered(): above = lax.ppermute(piece, ring_axis, down)]
    ppermute x2 -> x3, waiting for transfers between devices: 5.53 us -> 22.4 us  [gathered(): far = lax.ppermute(below, ring_axis, up)]
    ppermute x3 -> x0, waiting for transfers between devices: 8.87 us -> none  [the longest x1 4.58 us: gathered(): lax.ppermute(above[middle:], ring_axis, down)]
    ppermute x3 -> x0, starting transfers between devices: 7.44 us -> none  [the longest x1 5.84 us: gathered(): side_far = lax.ppermute(far, side_axis, SWAP)]
    ppermute x3, waiting for transfers between devices: 17 us -> 11.3 us  [gathered(): side_above = lax.ppermute(side, ring_axis, down)]
  transfers between devices with their start and end apart: 31 -> 30, of which waited for: 17 -> 16; matrix products, arithmetic and copies ran while one was open for 4% -> 4% of each run, Pallas kernels for 11% -> 11%
where the time goes in v10:
time: 382 us; the launch traced here: 381 us
  waiting for transfers between devices  132 us (35%)
  starting transfers between devices  108 us (28%)
  Pallas kernels  53.1 us (14%)
  blocking collectives  37.1 us (10%)
  local copies, waits for them, and re-layouts  21.3 us (6%)
  matrix products  16.9 us (4%)
  other arithmetic  11.4 us (3%)
    ppermute x3, starting transfers between devices, gathered(): side = lax.ppermute(piece, side_axis, SWAP)  57.5 us
    ppermute x3, waiting for transfers between devices, gathered(): below = lax.ppermute(piece, ring_axis, up)  50.1 us
    pallas_call x4, Pallas kernels, half_product(): pl.pallas_call(kernel, grid_spec=pltpu.PrefetchScalarGridSpec(num_scalar_...  46.9 us
    all_to_all x1, blocking collectives, per_device(): lax.all_to_all(jnp.broadcast_to(piece[None], (64,) + piece.shape), CHIPS,...  27.9 us
    ppermute x3, waiting for transfers between devices, gathered(): far = lax.ppermute(below, ring_axis, up)  22.4 us
    unnamed x50, local copies, waits for them, and re-layouts  20.5 us
    dot_general x7, matrix products, product(): lax.dot_general(left, right, (contract, ((), ())), precision=lax.Precisio...  16.9 us
    ppermute x3, waiting for transfers between devices, gathered(): above = lax.ppermute(piece, ring_axis, down)  16.6 us
  transfers between devices with their start and end apart: 30, of which 16 were waited for; matrix products, arithmetic and copies ran while one was open for 4% of the time, Pallas kernels for 11%

profile of v10, /device:TPU:1, one launch (start us, length us, event | category | flops | bytes accessed | tf_op | source)
XLA Modules:
  0.0 381.1 jit_solution(8242433246505874398)
XLA Ops:
  6.4 6.8 %collective-permute-done.refs_1_ = f32[64,1536]{1,0:T(8,128)S(1)} collective-permute-done((f32[64,1536]{1,0:T(8,128)S(1)}, f32[64,1536]{1,0:T(8,128)S(1)}, u32[]{:S(2)}, u32[]{:S(2)}) %collective-permute-start) | collective-permute-done | bytes 393248 | tf_op jit(solution)/shard_map/ppermute | solution.py:182
  13.1 4.1 %collective-permute-start.4 = (f32[64,1536]{1,0:T(8,128)S(1)}, f32[64,1536]{1,0:T(8,128)S(1)}, u32[]{:S(2)}, u32[]{:S(2)}) collective-permute-start(f32[64,1536]{1,0:T(8,128)S(1)} %collective-permute-done.refs_1_), channel_id=1, source_target_pairs={{0,48},{16,0},{32,16},{48,32},{1,49},{17,1},{33,17},{49,33},{2,50}... | collective-permute-start | bytes 1179656 | tf_op jit(solution)/shard_map/ppermute | solution.py:184
  19.0 5.2 %collective-permute-done.4.refs_5_ = f32[64,1536]{1,0:T(8,128)S(1)} collective-permute-done((f32[64,1536]{1,0:T(8,128)S(1)}, f32[64,1536]{1,0:T(8,128)S(1)}, u32[]{:S(2)}, u32[]{:S(2)}) %collective-permute-start.4) | collective-permute-done | bytes 393248 | tf_op jit(solution)/shard_map/ppermute | solution.py:184
  24.2 3.4 collective-permute-start.6
  35.8 5.3 %collective-permute-done.6.refs_7_ = f32[64,1536]{1,0:T(8,128)S(1)} collective-permute-done((f32[64,1536]{1,0:T(8,128)S(1)}, f32[64,1536]{1,0:T(8,128)S(1)}, u32[]{:S(2)}, u32[]{:S(2)}) %collective-permute-start.6) | collective-permute-done | bytes 393248 | tf_op jit(solution)/shard_map/ppermute | solution.py:186
  45.1 12.6 %shard_map.119 = (f32[512,1536]{1,0:T(8,128)}, bf16[512,1536]{1,0:T(8,128)(2,1)S(1)}, bf16[512,1536]{1,0:T(8,128)(2,1)S(1)}, f32[512,1536]{1,0:T(8,128)S(1)}) custom-call(s32[9]{0:T(128)S(1)} %stack.94.place_ref, f32[3072,1536]{1,0:T(8,128)} %a_ref.7, f32[64,1536]{1,0:T(8,128)S(1)} %multiply_bitcast_fusion.refs_0_, f32[64,1536]{1,0:T(8,128)S(1)} %copy-done.13, ...), custom_call_target="tpu_custom_call" | custom-call | flops 7247757312 | bytes 15728640 | tf_op jit(solution)/shard_map/pallas_call | solution.py:105
  61.5 9.2 %collective-permute-done.17.refs_1_ = f32[64,1536]{1,0:T(8,128)S(1)} collective-permute-done((f32[64,1536]{1,0:T(8,128)S(1)}, f32[64,1536]{1,0:T(8,128)S(1)}, u32[]{:S(2)}, u32[]{:S(2)}) %collective-permute-start.17) | collective-permute-done | bytes 393248 | tf_op jit(solution)/shard_map/ppermute | solution.py:182
  70.7 3.4 collective-permute-start.21
  75.6 6.1 %collective-permute-done.21.refs_5_ = f32[64,1536]{1,0:T(8,128)S(1)} collective-permute-done((f32[64,1536]{1,0:T(8,128)S(1)}, f32[64,1536]{1,0:T(8,128)S(1)}, u32[]{:S(2)}, u32[]{:S(2)}) %collective-permute-start.21) | collective-permute-done | bytes 393248 | tf_op jit(solution)/shard_map/ppermute | solution.py:184
  81.7 3.4 collective-permute-start.23
  93.3 5.3 %collective-permute-done.23.refs_7_ = f32[64,1536]{1,0:T(8,128)S(1)} collective-permute-done((f32[64,1536]{1,0:T(8,128)S(1)}, f32[64,1536]{1,0:T(8,128)S(1)}, u32[]{:S(2)}, u32[]{:S(2)}) %collective-permute-start.23) | collective-permute-done | bytes 393248 | tf_op jit(solution)/shard_map/ppermute | solution.py:186
  98.6 12.4 %shard_map.123 = (f32[512,1536]{1,0:T(8,128)}, bf16[512,1536]{1,0:T(8,128)(2,1)S(1)}, bf16[512,1536]{1,0:T(8,128)(2,1)S(1)}) custom-call(s32[9]{0:T(128)S(1)} %stack.94.place_ref, f32[3072,1536]{1,0:T(8,128)} %a_ref.7, f32[64,1536]{1,0:T(8,128)S(1)} %multiply_bitcast_fusion.1.refs_0_, f32[64,1536]{1,0:T(8,128)S(1)} %collective-permute-done.17.refs_1_, ...), custom_call_target="tpu_custom_call" | custom-call | flops 7247757312 | bytes 15728640 | tf_op jit(solution)/shard_map/pallas_call | solution.py:105
  116.5 11.0 %shard_map.120 = f32[512,1536]{1,0:T(8,128)S(1)} custom-call(s32[9]{0:T(128)S(1)} %stack.92.place_ref, f32[3072,1536]{1,0:T(8,128)} %a_ref.7, bf16[512,1536]{1,0:T(8,128)(2,1)S(1)} %get-tuple-element.33.high_ref, bf16[512,1536]{1,0:T(8,128)(2,1)S(1)} %copy-done.7, f32[512,1536]{1,0:T(8,128)} %collective-permute-done.7.added_ref), custom_call_target="tpu_custom_call" | custom-call | flops 7247757312 | bytes 15728640 | tf_op jit(solution)/shard_map/pallas_call | solution.py:105
  129.2 6.8 %all-to-all-start = ((f32[8,64,1536]{2,1,0:T(8,128)}), f32[8,64,1536]{2,1,0:T(8,128)}, u32[]{:S(2)}, u32[]{:S(2)}) async-start(f32[8,64,1536]{2,1,0:T(8,128)} %bitcast.85), calls=%async_computation | async-start | bytes 6291456 | tf_op jit(solution)/shard_map/all_to_all | solution.py:190
  136.8 54.1 %collective-permute-start.10 = (f32[128,1536]{1,0:T(8,128)S(1)}, f32[128,1536]{1,0:T(8,128)}, u32[]{:S(2)}, u32[]{:S(2)}) collective-permute-start(f32[128,1536]{1,0:T(8,128)S(1)} %collective-permute-done.9.refs_0_), channel_id=1, source_target_pairs={{0,8},{8,0},{1,9},{9,1},{2,10},{10,2},{3,11},{11,3},{4,12},{12,4},... | collective-permute-start | bytes 2359304 | tf_op jit(solution)/shard_map/ppermute | solution.py:182
  192.3 11.0 %shard_map.124 = f32[512,1536]{1,0:T(8,128)S(1)} custom-call(s32[9]{0:T(128)S(1)} %stack.92.place_ref, f32[3072,1536]{1,0:T(8,128)} %a_ref.7, bf16[512,1536]{1,0:T(8,128)(2,1)S(1)} %copy-done.9, bf16[512,1536]{1,0:T(8,128)(2,1)S(1)} %copy-done.11, f32[512,1536]{1,0:T(8,128)} %collective-permute-done.24.added_ref), custom_call_target="tpu_custom_call" | custom-call | flops 7247757312 | bytes 15728640 | tf_op jit(solution)/shard_map/pallas_call | solution.py:105
  205.0 8.2 %all-to-all-start.1 = ((f32[8,64,1536]{2,1,0:T(8,128)}), f32[8,64,1536]{2,1,0:T(8,128)}, u32[]{:S(2)}, u32[]{:S(2)}) async-start(f32[8,64,1536]{2,1,0:T(8,128)} %bitcast.84), calls=%async_computation.1 | async-start | bytes 6291456 | tf_op jit(solution)/shard_map/all_to_all | solution.py:190
  218.0 50.1 %collective-permute-done.11.refs_2_ = f32[128,1536]{1,0:T(8,128)S(1)} collective-permute-done((f32[128,1536]{1,0:T(8,128)S(1)}, f32[128,1536]{1,0:T(8,128)S(1)}, u32[]{:S(2)}, u32[]{:S(2)}) %collective-permute-start.11) | collective-permute-done | bytes 786464 | tf_op jit(solution)/shard_map/ppermute | solution.py:180
  270.8 11.1 %collective-permute-done.12.refs_3_ = f32[128,1536]{1,0:T(8,128)} collective-permute-done((f32[128,1536]{1,0:T(8,128)S(1)}, f32[128,1536]{1,0:T(8,128)}, u32[]{:S(2)}, u32[]{:S(2)}) %collective-permute-start.12) | collective-permute-done | bytes 786464 | tf_op jit(solution)/shard_map/ppermute | solution.py:181
  285.0 16.9 %collective-permute-done.15.refs_6_ = f32[128,1536]{1,0:T(8,128)} collective-permute-done((f32[128,1536]{1,0:T(8,128)S(1)}, f32[128,1536]{1,0:T(8,128)}, u32[]{:S(2)}, u32[]{:S(2)}) %collective-permute-start.15) | collective-permute-done | bytes 786464 | tf_op jit(solution)/shard_map/ppermute | solution.py:185
  310.4 3.6 convolution_bitcast_fusion.3
  317.8 3.4 convolution_bitcast_fusion.1
  323.0 9.2 %all_to_all.20 = f32[8,3,8,256]{3,2,1,0:T(8,128)S(1)} all-to-all(f32[8,3,8,256]{3,2,1,0:T(8,128)S(1)} %copy_bitcast_fusion), channel_id=1, replica_groups=mesh['xl'=2,'z'=4,'xh'=2,'y'=4,'core'=2] {'xl','z'}, dimensions={0} | all-to-all | bytes 393216 | tf_op jit(solution)/shard_map/all_to_all | solution.py:233
  332.3 27.9 %all_to_all.21 = f32[64,3,8,256]{3,2,1,0:T(8,128)S(1)} all-to-all(f32[64,3,8,256]{3,2,1,0:T(8,128)S(1)} %broadcast_in_dim.8), channel_id=1, replica_groups=mesh['xl'=2,'z'=4,'xh'=2,'y'=4,'core'=2] {'xl','z','xh','y'}, dimensions={0} | all-to-all | bytes 3145728 | tf_op jit(solution)/shard_map/all_to_all | solution.py:234
  (125 shorter events, 89.7 us)
Async XLA Ops:
  4.7 14.2 %collective-permute-start.1 = (f32[64,1536]{1,0:T(8,128)S(1)}, f32[64,1536]{1,0:T(8,128)S(1)}, u32[]{:S(2)}, u32[]{:S(2)}) collective-permute-start(f32[64,1536]{1,0:T(8,128)S(1)} %multiply_bitcast_fusion.refs_0_), channel_id=1, source_target_pairs={{0,16},{16,32},{32,48},{48,0},{1,17},{17,33},{33,49},{49,1},{2,18}... | collective-permute-start | bytes 1179656 | tf_op jit(solution)/shard_map/ppermute | solution.py:180
  13.1 11.1 %collective-permute-start.4 = (f32[64,1536]{1,0:T(8,128)S(1)}, f32[64,1536]{1,0:T(8,128)S(1)}, u32[]{:S(2)}, u32[]{:S(2)}) collective-permute-start(f32[64,1536]{1,0:T(8,128)S(1)} %collective-permute-done.refs_1_), channel_id=1, source_target_pairs={{0,48},{16,0},{32,16},{48,32},{1,49},{17,1},{33,17},{49,33},{2,50}... | collective-permute-start | bytes 1179656 | tf_op jit(solution)/shard_map/ppermute | solution.py:184
  17.3 15.4 %collective-permute-start.2 = (f32[64,1536]{1,0:T(8,128)S(1)}, f32[64,1536]{1,0:T(8,128)S(1)}, u32[]{:S(2)}, u32[]{:S(2)}) collective-permute-start(f32[64,1536]{1,0:T(8,128)S(1)} %multiply_bitcast_fusion.refs_0_), channel_id=1, source_target_pairs={{0,48},{16,0},{32,16},{48,32},{1,49},{17,1},{33,17},{49,33},{2,50}... | collective-permute-start | bytes 1179656 | tf_op jit(solution)/shard_map/ppermute | solution.py:181
  17.6 15.8 %collective-permute-start.3 = (f32[64,1536]{1,0:T(8,128)S(1)}, f32[64,1536]{1,0:T(8,128)S(1)}, u32[]{:S(2)}, u32[]{:S(2)}) collective-permute-start(f32[64,1536]{1,0:T(8,128)S(1)} %collective-permute-done.refs_1_), channel_id=1, source_target_pairs={{0,16},{16,32},{32,48},{48,0},{1,17},{17,33},{33,49},{49,1},{2,18}... | collective-permute-start | bytes 1179656 | tf_op jit(solution)/shard_map/ppermute | solution.py:183
  18.9 16.9 %collective-permute-start.5 = (f32[64,1536]{1,0:T(8,128)S(1)}, f32[64,1536]{1,0:T(8,128)S(1)}, u32[]{:S(2)}, u32[]{:S(2)}) collective-permute-start(f32[64,1536]{1,0:T(8,128)S(1)} %collective-permute-done.1.refs_2_), channel_id=1, source_target_pairs={{0,16},{16,32},{32,48},{48,0},{1,17},{17,33},{33,49},{49,1},{2,18}... | collective-permute-start | bytes 1179656 | tf_op jit(solution)/shard_map/ppermute | solution.py:185
  24.2 16.9 %collective-permute-start.6 = (f32[64,1536]{1,0:T(8,128)S(1)}, f32[64,1536]{1,0:T(8,128)S(1)}, u32[]{:S(2)}, u32[]{:S(2)}) collective-permute-start(f32[64,1536]{1,0:T(8,128)S(1)} %collective-permute-done.4.refs_5_), channel_id=1, source_target_pairs={{0,48},{16,0},{32,16},{48,32},{1,49},{17,1},{33,17},{49,33},{2,50}... | collective-permute-start | bytes 1179656 | tf_op jit(solution)/shard_map/ppermute | solution.py:186
  57.6 57.4 %collective-permute-start.7 = (f32[512,1536]{1,0:T(8,128)}, f32[512,1536]{1,0:T(8,128)}, u32[]{:S(2)}, u32[]{:S(2)}) collective-permute-start(f32[512,1536]{1,0:T(8,128)} %get-tuple-element.35), channel_id=1, source_target_pairs={{0,1},{1,0},{2,3},{3,2},{4,5},{5,4},{6,7},{7,6},{8,9},{9,8},{10,11... | collective-permute-start | bytes 9437192 | tf_op jit(solution)/shard_map/ppermute | solution.py:219
  61.2 14.3 %collective-permute-start.18 = (f32[64,1536]{1,0:T(8,128)S(1)}, f32[64,1536]{1,0:T(8,128)S(1)}, u32[]{:S(2)}, u32[]{:S(2)}) collective-permute-start(f32[64,1536]{1,0:T(8,128)S(1)} %multiply_bitcast_fusion.1.refs_0_), channel_id=1, source_target_pairs={{0,16},{16,32},{32,48},{48,0},{1,17},{17,33},{33,49},{49,1},{2,18}... | collective-permute-start | bytes 1179656 | tf_op jit(solution)/shard_map/ppermute | solution.py:180
  70.7 11.0 %collective-permute-start.21 = (f32[64,1536]{1,0:T(8,128)S(1)}, f32[64,1536]{1,0:T(8,128)S(1)}, u32[]{:S(2)}, u32[]{:S(2)}) collective-permute-start(f32[64,1536]{1,0:T(8,128)S(1)} %collective-permute-done.17.refs_1_), channel_id=1, source_target_pairs={{0,48},{16,0},{32,16},{48,32},{1,49},{17,1},{33,17},{49,33},{2,50}... | collective-permute-start | bytes 1179656 | tf_op jit(solution)/shard_map/ppermute | solution.py:184
  74.1 16.0 %collective-permute-start.19 = (f32[64,1536]{1,0:T(8,128)S(1)}, f32[64,1536]{1,0:T(8,128)S(1)}, u32[]{:S(2)}, u32[]{:S(2)}) collective-permute-start(f32[64,1536]{1,0:T(8,128)S(1)} %multiply_bitcast_fusion.1.refs_0_), channel_id=1, source_target_pairs={{0,48},{16,0},{32,16},{48,32},{1,49},{17,1},{33,17},{49,33},{2,50}... | collective-permute-start | bytes 1179656 | tf_op jit(solution)/shard_map/ppermute | solution.py:181
  74.1 16.0 %collective-permute-start.20 = (f32[64,1536]{1,0:T(8,128)S(1)}, f32[64,1536]{1,0:T(8,128)S(1)}, u32[]{:S(2)}, u32[]{:S(2)}) collective-permute-start(f32[64,1536]{1,0:T(8,128)S(1)} %collective-permute-done.17.refs_1_), channel_id=1, source_target_pairs={{0,16},{16,32},{32,48},{48,0},{1,17},{17,33},{33,49},{49,1},{2,18}... | collective-permute-start | bytes 1179656 | tf_op jit(solution)/shard_map/ppermute | solution.py:183
  75.6 17.7 %collective-permute-start.22 = (f32[64,1536]{1,0:T(8,128)S(1)}, f32[64,1536]{1,0:T(8,128)S(1)}, u32[]{:S(2)}, u32[]{:S(2)}) collective-permute-start(f32[64,1536]{1,0:T(8,128)S(1)} %collective-permute-done.18.refs_2_), channel_id=1, source_target_pairs={{0,16},{16,32},{32,48},{48,0},{1,17},{17,33},{33,49},{49,1},{2,18}... | collective-permute-start | bytes 1179656 | tf_op jit(solution)/shard_map/ppermute | solution.py:185
  81.7 16.9 %collective-permute-start.23 = (f32[64,1536]{1,0:T(8,128)S(1)}, f32[64,1536]{1,0:T(8,128)S(1)}, u32[]{:S(2)}, u32[]{:S(2)}) collective-permute-start(f32[64,1536]{1,0:T(8,128)S(1)} %collective-permute-done.21.refs_5_), channel_id=1, source_target_pairs={{0,48},{16,0},{32,16},{48,32},{1,49},{17,1},{33,17},{49,33},{2,50}... | collective-permute-start | bytes 1179656 | tf_op jit(solution)/shard_map/ppermute | solution.py:186
  113.3 77.7 %collective-permute-start.24 = (f32[512,1536]{1,0:T(8,128)}, f32[512,1536]{1,0:T(8,128)}, u32[]{:S(2)}, u32[]{:S(2)}) collective-permute-start(f32[512,1536]{1,0:T(8,128)} %get-tuple-element.43), channel_id=1, source_target_pairs={{0,1},{1,0},{2,3},{3,2},{4,5},{5,4},{6,7},{7,6},{8,9},{9,8},{10,11... | collective-permute-start | bytes 9437192 | tf_op jit(solution)/shard_map/ppermute | solution.py:224
  129.2 75.8 %all-to-all-start = ((f32[8,64,1536]{2,1,0:T(8,128)}), f32[8,64,1536]{2,1,0:T(8,128)}, u32[]{:S(2)}, u32[]{:S(2)}) async-start(f32[8,64,1536]{2,1,0:T(8,128)} %bitcast.85), calls=%async_computation | async-start | bytes 6291456 | tf_op jit(solution)/shard_map/all_to_all | solution.py:190
  136.8 77.9 %collective-permute-start.10 = (f32[128,1536]{1,0:T(8,128)S(1)}, f32[128,1536]{1,0:T(8,128)}, u32[]{:S(2)}, u32[]{:S(2)}) collective-permute-start(f32[128,1536]{1,0:T(8,128)S(1)} %collective-permute-done.9.refs_0_), channel_id=1, source_target_pairs={{0,8},{8,0},{1,9},{9,1},{2,10},{10,2},{3,11},{11,3},{4,12},{12,4},... | collective-permute-start | bytes 2359304 | tf_op jit(solution)/shard_map/ppermute | solution.py:182
  205.0 110.7 %all-to-all-start.1 = ((f32[8,64,1536]{2,1,0:T(8,128)}), f32[8,64,1536]{2,1,0:T(8,128)}, u32[]{:S(2)}, u32[]{:S(2)}) async-start(f32[8,64,1536]{2,1,0:T(8,128)} %bitcast.84), calls=%async_computation.1 | async-start | bytes 6291456 | tf_op jit(solution)/shard_map/all_to_all | solution.py:190
  213.2 54.9 %collective-permute-start.11 = (f32[128,1536]{1,0:T(8,128)S(1)}, f32[128,1536]{1,0:T(8,128)S(1)}, u32[]{:S(2)}, u32[]{:S(2)}) collective-permute-start(f32[128,1536]{1,0:T(8,128)S(1)} %collective-permute-done.9.refs_0_), channel_id=1, source_target_pairs={{0,2},{2,4},{4,6},{6,0},{1,3},{3,5},{5,7},{7,1},{8,10},{10,12},{12... | collective-permute-start | bytes 2359304 | tf_op jit(solution)/shard_map/ppermute | solution.py:180
  214.7 53.4 %collective-permute-start.14 = (f32[128,1536]{1,0:T(8,128)}, f32[128,1536]{1,0:T(8,128)S(1)}, u32[]{:S(2)}, u32[]{:S(2)}) collective-permute-start(f32[128,1536]{1,0:T(8,128)} %collective-permute-done.10.refs_1_), channel_id=1, source_target_pairs={{0,6},{2,0},{4,2},{6,4},{1,7},{3,1},{5,3},{7,5},{8,14},{10,8},{12,... | collective-permute-start | bytes 2359304 | tf_op jit(solution)/shard_map/ppermute | solution.py:184
  216.5 65.4 %collective-permute-start.12 = (f32[128,1536]{1,0:T(8,128)S(1)}, f32[128,1536]{1,0:T(8,128)}, u32[]{:S(2)}, u32[]{:S(2)}) collective-permute-start(f32[128,1536]{1,0:T(8,128)S(1)} %collective-permute-done.9.refs_0_), channel_id=1, source_target_pairs={{0,6},{2,0},{4,2},{6,4},{1,7},{3,1},{5,3},{7,5},{8,14},{10,8},{12,... | collective-permute-start | bytes 2359304 | tf_op jit(solution)/shard_map/ppermute | solution.py:181
  217.9 67.1 %collective-permute-start.13 = (f32[128,1536]{1,0:T(8,128)}, f32[128,1536]{1,0:T(8,128)}, u32[]{:S(2)}, u32[]{:S(2)}) collective-permute-start(f32[128,1536]{1,0:T(8,128)} %collective-permute-done.10.refs_1_), channel_id=1, source_target_pairs={{0,2},{2,4},{4,6},{6,0},{1,3},{3,5},{5,7},{7,1},{8,10},{10,12},{12... | collective-permute-start | bytes 2359304 | tf_op jit(solution)/shard_map/ppermute | solution.py:183
  268.1 33.8 %collective-permute-start.15 = (f32[128,1536]{1,0:T(8,128)S(1)}, f32[128,1536]{1,0:T(8,128)}, u32[]{:S(2)}, u32[]{:S(2)}) collective-permute-start(f32[128,1536]{1,0:T(8,128)S(1)} %collective-permute-done.11.refs_2_), channel_id=1, source_target_pairs={{0,2},{2,4},{4,6},{6,0},{1,3},{3,5},{5,7},{7,1},{8,10},{10,12},{12... | collective-permute-start | bytes 2359304 | tf_op jit(solution)/shard_map/ppermute | solution.py:185
  268.1 33.8 %collective-permute-start.16 = (f32[128,1536]{1,0:T(8,128)S(1)}, f32[128,1536]{1,0:T(8,128)}, u32[]{:S(2)}, u32[]{:S(2)}) collective-permute-start(f32[128,1536]{1,0:T(8,128)S(1)} %collective-permute-done.14.refs_5_), channel_id=1, source_target_pairs={{0,6},{2,0},{4,2},{6,4},{1,7},{3,1},{5,3},{7,5},{8,14},{10,8},{12,... | collective-permute-start | bytes 2359304 | tf_op jit(solution)/shard_map/ppermute | solution.py:186
  360.4 12.8 %collective-permute-start.26 = (f32[3,512,256]{2,1,0:T(8,128)S(1)}, f32[3,512,256]{2,1,0:T(8,128)}, u32[]{:S(2)}, u32[]{:S(2)}) collective-permute-start(f32[3,512,256]{2,1,0:T(8,128)S(1)} %bitcast.87), channel_id=1, source_target_pairs={{0,1},{1,0},{2,3},{3,2},{4,5},{5,4},{6,7},{7,6},{8,9},{9,8},{10,11... | collective-permute-start | bytes 4718600 | tf_op jit(solution)/shard_map/ppermute | solution.py:237
  (30 other events, 271.1 us)
